TPU v7x, 256 devices: a whole 4x4x8 slice. The times are simulated.
256 devices in a mesh: sec: 32 (over z, y), blk: 8 (over x, core).
Axes of the slice: x: 4, y: 4, z: 8, core: 2. Of those that a mesh axis runs over, the one named last changes fastest.
Arguments:
- state_now: float32 [128, 65536], P(None, ('sec', 'blk')), may hold values from -5 to 5
- source: float32 [128, 65536], P(None, ('sec', 'blk')), may hold values from -6 to 6
- fan_gain: float32 [65536], P(('sec', 'blk')), may hold values from 0.5 to 12
- section_block: bfloat16 [65536, 2048], P(('sec', 'blk')), may hold values from -1 to 7
- block_inverse: bfloat16 [65536, 2048], P(('sec', 'blk')), may hold values from -1 to 1
- back_panel: bfloat16 [65536, 128], P(('sec', 'blk')), may hold values from -6 to 6
- ahead_panel: bfloat16 [65536, 128], P(('sec', 'blk')), may hold values from -0.0625 to 0.0625
- interface: int32 [32, 128], P('sec'), may hold values from 0 to 2047, as said below
Outputs:
- new_state: float32 [128, 65536], P(None, ('sec', 'blk'))
Inputs may be any that keep to these rules, and one draw needn't show every extreme that they name: `interface`: entries of one section are distinct; entry p lies in [p * 16, (p + 1) * 16).
All inputs are finite; a program needn't handle non-finite values.
Results may differ from a plain program's by a relative error of at most 0.0063.
Values may be sent and summed in bfloat16 or wider, within the bound.
A program may use at most 64 MiB of HBM per device.

v0:
```python
import jax
import jax.numpy as jnp
from jax import lax
from jax.sharding import PartitionSpec as P

KRYLOV = 3


epsilon = 1e-06


def extended(x, sides, width):
    for axis, dim in sides:
        size, length = (lax.axis_size(axis), x.shape[dim])
        up = [(i, (i + 1) % size) for i in range(size - 1)]
        down = [(j, i) for i, j in up]
        last = lax.slice_in_dim(x, length - width, length, axis=dim)
        first = lax.slice_in_dim(x, 0, width, axis=dim)
        before = lax.ppermute(last, axis, up)
        after = lax.ppermute(first, axis, down)
        x = jnp.concatenate([before, x, after], axis=dim)
    return x


def entering(value, axis, join, neutral):
    count, mine = (lax.axis_size(axis), lax.axis_index(axis))
    pieces = jax.tree.map(lambda part: lax.all_gather(part, axis), value)
    so_far = jax.tree.map(
        lambda part, zero: jnp.full_like(part, 0) + jnp.asarray(zero, part.dtype), value, neutral
    )

    def step(position, so_far):
        longer = join(so_far, jax.tree.map(lambda part: part[position], pieces))
        return jax.tree.map(lambda new, old: jnp.where(position < mine, new, old), longer, so_far)

    return lax.fori_loop(0, count - 1, step, so_far)


def least_squares(hessen, beta):
    cases = hessen.shape[0]
    depth = hessen.shape[2]
    rhs = jnp.zeros((cases, depth + 1), jnp.float32).at[:, 0].set(beta)
    upper = hessen
    for column in range(depth):
        upper_row = upper[:, column, :]
        lower_row = upper[:, column + 1, :]
        radius = jnp.sqrt(upper_row[:, column] ** 2 + lower_row[:, column] ** 2)
        cosine = upper_row[:, column] / radius
        sine_term = lower_row[:, column] / radius
        upper = upper.at[:, column, :].set(
            cosine[:, None] * upper_row + sine_term[:, None] * lower_row
        )
        upper = upper.at[:, column + 1, :].set(
            -sine_term[:, None] * upper_row + cosine[:, None] * lower_row
        )
        first_rhs = rhs[:, column]
        second_rhs = rhs[:, column + 1]
        rhs = rhs.at[:, column].set(cosine * first_rhs + sine_term * second_rhs)
        rhs = rhs.at[:, column + 1].set(-sine_term * first_rhs + cosine * second_rhs)
    weights = jnp.zeros((cases, depth), jnp.float32)
    for column in reversed(range(depth)):
        remain = rhs[:, column] - jnp.sum(
            upper[:, column, column + 1 :] * weights[:, column + 1 :], axis=1
        )
        weights = weights.at[:, column].set(remain / upper[:, column, column])
    return weights


def local(
    state_now, source, fan_gain, section_block, block_inverse, back_panel, ahead_panel, interface
):
    highest = lax.Precision.HIGHEST
    cases, node_rows = state_now.shape
    panel_width = back_panel.shape[1]
    indices = interface[0]
    first_row = lax.axis_index("blk") * node_rows
    selector = (indices[None, :] == first_row + jnp.arange(node_rows)[:, None]).astype(jnp.float32)
    contract = (((1,), (1,)), ((), ()))
    gain_panel = jnp.dot(
        block_inverse,
        lax.all_gather(back_panel, "blk", axis=0, tiled=True),
        preferred_element_type=jnp.float32,
    )
    panel_maps = -lax.psum(jnp.dot(selector.T, gain_panel, precision=highest), "blk")

    def section_terms(dense_part, behind_vals, piece):
        width = piece.shape[1]
        dense_part = lax.dot_general(
            piece, section_block, contract, preferred_element_type=jnp.float32
        )
        picker = (indices[None, :] == jnp.arange(width)[:, None]).astype(jnp.bfloat16)
        behind_vals = jnp.dot(piece, picker, preferred_element_type=jnp.float32)
        return (dense_part, behind_vals)

    def fold_section(carry, piece):
        return section_terms(carry[0], carry[1], piece)

    def operator(vector):
        rounded = vector.astype(jnp.bfloat16)
        empty_dense = jnp.zeros((cases, node_rows), jnp.float32)
        empty_panel = jnp.zeros((cases, panel_width), jnp.float32)
        start_carry = (empty_dense, empty_panel)
        folded = fold_section(start_carry, lax.all_gather(rounded, "blk", axis=1, tiled=True))
        dense_part, behind_vals = folded
        upward = lax.psum(jnp.dot(rounded, ahead_panel, preferred_element_type=jnp.float32), "blk")
        framed = extended(jnp.stack([behind_vals, upward])[None], (("sec", 0),), 1)
        behind = framed[0, 0].astype(jnp.bfloat16)
        ahead_term = framed[2, 1]
        lower_term = lax.dot_general(
            behind, back_panel, contract, preferred_element_type=jnp.float32
        )
        upper_term = jnp.dot(ahead_term, selector.T, precision=highest)
        return dense_part + lower_term + upper_term

    def compose(earlier, later):
        first_map, first_value = earlier
        second_map, second_value = later
        joined_map = jnp.dot(second_map, first_map, precision=highest)
        joined_value = jnp.dot(first_value, second_map.T, precision=highest) + second_value
        return (joined_map, joined_value)

    def lengths(vector):
        return jnp.sqrt(lax.psum(jnp.sum(vector * vector, axis=1), ("sec", "blk")) + epsilon)

    bent = jnp.tanh(state_now)
    residual = source - operator(state_now) - fan_gain[None, :] * bent
    jac_diag = fan_gain[None, :] * (1.0 - bent * bent)
    beta = lengths(residual)
    basis = [residual / beta[:, None]]
    directions = []
    hessen = jnp.zeros((cases, KRYLOV + 1, KRYLOV), jnp.float32)
    for column in range(KRYLOV):
        precondition_rounded = basis[column].astype(jnp.bfloat16)
        precondition_folded = lax.dot_general(
            lax.all_gather(precondition_rounded, "blk", axis=1, tiled=True),
            block_inverse,
            contract,
            preferred_element_type=jnp.float32,
        )
        values = lax.psum(jnp.dot(precondition_folded, selector, precision=highest), "blk")
        identity = (
            jnp.eye(panel_width, dtype=jnp.float32),
            jnp.zeros((cases, panel_width), jnp.float32),
        )
        _, before = entering((panel_maps, values), "sec", compose, identity)
        direction = precondition_folded - lax.dot_general(
            before, gain_panel, contract, precision=highest
        )
        product = operator(direction) + jac_diag * direction
        stacked = jnp.stack(basis)
        projections = lax.psum(jnp.sum(product[None] * stacked, axis=2), ("sec", "blk"))
        product = product - jnp.sum(projections[:, :, None] * stacked, axis=0)
        length = lengths(product)
        hessen = hessen.at[:, : column + 1, column].set(projections.T)
        hessen = hessen.at[:, column + 1, column].set(length)
        basis.append(product / length[:, None])
        directions.append(direction)
    weights = least_squares(hessen, beta)
    update = jnp.zeros_like(state_now)
    for column in range(KRYLOV):
        update = update + weights[:, column : column + 1] * directions[column]
    return state_now + update


def solution(mesh):
    in_specs = (
        P(None, ("sec", "blk")),
        P(None, ("sec", "blk")),
        P(("sec", "blk")),
        P(("sec", "blk"), None),
        P(("sec", "blk"), None),
        P(("sec", "blk"), None),
        P(("sec", "blk"), None),
        P("sec", None),
    )
    out_specs = P(None, ("sec", "blk"))
    return jax.shard_map(local, mesh=mesh, in_specs=in_specs, out_specs=out_specs, check_vma=False)
```

profile of v0, /device:TPU:1, one launch (start us, length us, event | category | flops | bytes accessed | tf_op | source)
XLA Modules:
  0.0 1640.1 jit_solution(12427240941463223437)
XLA Ops:
  40.7 34.6 %all-reduce.11.cloned.1.call-done = f32[1,128,128]{1,2,0:T(8,128)} async-done(((f32[1,128,128]{1,2,0:T(8,128)}), f32[1,128,128]{1,2,0:T(8,128)}) %all-reduce.11.cloned.1.call-update) | async-done | bytes 65552 | tf_op jit(solution)/shard_map/psum | solution.py:105
  86.3 83.2 %psum.106 = f32[128]{0:T(128)S(1)} all-reduce(f32[128]{0:T(128)S(1)} %get-tuple-element.720), channel_id=1, replica_groups=mesh['sec'=32,'blk'=8] {'sec','blk'}, use_global_device_ids=true, to_apply=%region_4.0 | all-reduce | flops 128 | bytes 1024 | tf_op jit(solution)/shard_map/psum | solution.py:123
  185.0 57.8 %all-reduce.23.cloned.1.call-done = (f32[128,128]{1,0:T(8,128)}, f32[1,128,128]{2,1,0:T(8,128)}) async-done(((f32[128,128]{1,0:T(8,128)}, f32[1,128,128]{2,1,0:T(8,128)}), (f32[128,128]{1,0:T(8,128)}, f32[1,128,128]{2,1,0:T(8,128)})) %all-reduce.23.cloned.1.call-update) | async-done | bytes 131088 | tf_op jit(solution)/shard_map/psum | solution.py:84
  244.9 75.7 %all-gather.12.cloned.1.call-done = f32[4096,128]{1,0:T(8,128)} async-done(((f32[128,128]{1,0:T(8,128)}), f32[4096,128]{1,0:T(8,128)}) %all-gather.12.cloned.1.call-update) | async-done | bytes 2097168 | tf_op jit(solution)/shard_map/all_gather | solution.py:27
  320.6 77.6 %all-gather.6.cloned.1.call-done = f32[32,128,128]{2,1,0:T(8,128)} async-done(((f32[1,128,128]{2,1,0:T(8,128)}), f32[32,128,128]{2,1,0:T(8,128)}) %all-gather.6.cloned.1.call-update) | async-done | bytes 2097168 | tf_op jit(solution)/shard_map/all_gather | solution.py:27
  398.3 63.2 %while.64 = (s32[]{:T(128)}, f32[128,128]{0,1:T(8,128)S(1)}, s32[]{:T(128)}, f32[32,128,128]{2,1,0:T(8,128)}, f32[32,128,128]{2,1,0:T(8,128)}, /*index=5*/s32[]{:T(128)}, s32[]{:T(128)}) while((s32[]{:T(128)}, f32[128,128]{0,1:T(8,128)S(1)}, s32[]{:T(128)}, f32[32,128,128]{2,1,0:T(8,128)}, f32[32,128,128]{2,1,0:T(8,128)}, ...), condition=%wide.region_8.9_spmd.clone, body=%wide.region_7.8_spmd.clone.sunk | while | flops 25231364 | bytes 723043 | solution.py:36
  461.8 17.8 %all_gather.59 = bf16[128,2048]{1,0:T(8,128)(2,1)S(1)} all-gather(bf16[128,256]{1,0:T(8,128)(2,1)S(1)} %get-tuple-element.722), channel_id=1, replica_groups=mesh['sec'=32,'blk'=8] {'blk'}, dimensions={1}, use_global_device_ids=true | all-gather | bytes 589824 | tf_op jit(solution)/shard_map/all_gather | solution.py:103
  480.8 57.6 %all-reduce.13.cloned.1.call-done = f32[1,128,128]{2,1,0:T(8,128)} async-done(((f32[1,128,128]{2,1,0:T(8,128)}), f32[1,128,128]{2,1,0:T(8,128)}) %all-reduce.13.cloned.1.call-update) | async-done | bytes 65552 | tf_op jit(solution)/shard_map/psum | solution.py:105
  549.1 83.2 %psum.110 = f32[1,128]{1,0:T(1,128)S(1)} all-reduce(f32[1,128]{1,0:T(1,128)S(1)} %bitcast.287), channel_id=1, replica_groups=mesh['sec'=32,'blk'=8] {'sec','blk'}, use_global_device_ids=true, to_apply=%region_11.12 | all-reduce | flops 128 | bytes 1024 | tf_op jit(solution)/shard_map/psum | solution.py:151
  632.5 72.3 %psum.111 = f32[128]{0:T(128)S(1)} all-reduce(f32[128]{0:T(128)S(1)} %get-tuple-element.687), channel_id=1, replica_groups=mesh['sec'=32,'blk'=8] {'sec','blk'}, use_global_device_ids=true, to_apply=%region_13.14 | all-reduce | flops 128 | bytes 1024 | tf_op jit(solution)/shard_map/psum | solution.py:123
  720.1 58.5 %all-reduce.15.cloned.1.call-done = f32[1,128,128]{2,1,0:T(8,128)} async-done(((f32[1,128,128]{2,1,0:T(8,128)}), f32[1,128,128]{2,1,0:T(8,128)}) %all-reduce.15.cloned.1.call-update) | async-done | bytes 65552 | tf_op jit(solution)/shard_map/psum | solution.py:140
  778.7 77.7 %all-gather.8.cloned.1.call-done = f32[32,128,128]{2,1,0:T(8,128)} async-done(((f32[1,128,128]{2,1,0:T(8,128)}), f32[32,128,128]{2,1,0:T(8,128)}) %all-gather.8.cloned.1.call-update) | async-done | bytes 2097168 | tf_op jit(solution)/shard_map/all_gather | solution.py:27
  856.4 63.2 %while.65 = (s32[]{:T(128)}, f32[128,128]{0,1:T(8,128)S(1)}, s32[]{:T(128)}, f32[32,128,128]{2,1,0:T(8,128)}, f32[32,128,128]{2,1,0:T(8,128)}, /*index=5*/s32[]{:T(128)}, s32[]{:T(128)}) while((s32[]{:T(128)}, f32[128,128]{0,1:T(8,128)S(1)}, s32[]{:T(128)}, f32[32,128,128]{2,1,0:T(8,128)}, f32[32,128,128]{2,1,0:T(8,128)}, ...), condition=%wide.region_16.17_spmd.clone, body=%wide.region_15.16_spmd.clone.sunk | while | flops 25231364 | bytes 723043 | solution.py:36
  920.6 17.8 %all_gather.63 = bf16[128,2048]{1,0:T(8,128)(2,1)S(1)} all-gather(bf16[128,256]{1,0:T(8,128)(2,1)S(1)} %get-tuple-element.724), channel_id=1, replica_groups=mesh['sec'=32,'blk'=8] {'blk'}, dimensions={1}, use_global_device_ids=true | all-gather | bytes 589824 | tf_op jit(solution)/shard_map/all_gather | solution.py:103
  939.7 57.4 %all-reduce.17.cloned.1.call-done = f32[1,128,128]{2,1,0:T(8,128)} async-done(((f32[1,128,128]{2,1,0:T(8,128)}), f32[1,128,128]{2,1,0:T(8,128)}) %all-reduce.17.cloned.1.call-update) | async-done | bytes 65552 | tf_op jit(solution)/shard_map/psum | solution.py:105
  1007.8 83.2 %psum.114 = f32[2,128]{1,0:T(2,128)S(1)} all-reduce(f32[2,128]{1,0:T(2,128)S(1)} %multiply_reduce_fusion.3), channel_id=1, replica_groups=mesh['sec'=32,'blk'=8] {'sec','blk'}, use_global_device_ids=true, to_apply=%region_19.20 | all-reduce | flops 256 | bytes 2048 | tf_op jit(solution)/shard_map/psum | solution.py:151
  1091.2 72.3 %psum.115 = f32[128]{0:T(128)S(1)} all-reduce(f32[128]{0:T(128)S(1)} %get-tuple-element.683), channel_id=1, replica_groups=mesh['sec'=32,'blk'=8] {'sec','blk'}, use_global_device_ids=true, to_apply=%region_22.23 | all-reduce | flops 128 | bytes 1024 | tf_op jit(solution)/shard_map/psum | solution.py:123
  1178.8 58.5 %all-reduce.19.cloned.1.call-done = f32[1,128,128]{2,1,0:T(8,128)} async-done(((f32[1,128,128]{2,1,0:T(8,128)}), f32[1,128,128]{2,1,0:T(8,128)}) %all-reduce.19.cloned.1.call-update) | async-done | bytes 65552 | tf_op jit(solution)/shard_map/psum | solution.py:140
  1243.8 71.1 %all-gather.10.cloned.1.call-done = f32[32,128,128]{2,1,0:T(8,128)} async-done(((f32[1,128,128]{2,1,0:T(8,128)}), f32[32,128,128]{2,1,0:T(8,128)}) %all-gather.10.cloned.1.call-update) | async-done | bytes 2097168 | tf_op jit(solution)/shard_map/all_gather | solution.py:27
  1314.9 63.2 %while.66 = (s32[]{:T(128)}, f32[128,128]{0,1:T(8,128)S(1)}, s32[]{:T(128)}, f32[32,128,128]{2,1,0:T(8,128)}, f32[32,128,128]{2,1,0:T(8,128)}, /*index=5*/s32[]{:T(128)}, s32[]{:T(128)}) while((s32[]{:T(128)}, f32[128,128]{0,1:T(8,128)S(1)}, s32[]{:T(128)}, f32[32,128,128]{2,1,0:T(8,128)}, f32[32,128,128]{2,1,0:T(8,128)}, ...), condition=%wide.region_26.27_spmd.clone, body=%wide.region_25.26_spmd.clone.sunk | while | flops 25231364 | bytes 723043 | solution.py:36
  1379.1 17.8 %all_gather.67 = bf16[128,2048]{1,0:T(8,128)(2,1)S(1)} all-gather(bf16[128,256]{1,0:T(8,128)(2,1)S(1)} %get-tuple-element.726), channel_id=1, replica_groups=mesh['sec'=32,'blk'=8] {'blk'}, dimensions={1}, use_global_device_ids=true | all-gather | bytes 589824 | tf_op jit(solution)/shard_map/all_gather | solution.py:103
  1398.0 57.6 %all-reduce.21.cloned.1.call-done = f32[1,128,128]{2,1,0:T(8,128)} async-done(((f32[1,128,128]{2,1,0:T(8,128)}), f32[1,128,128]{2,1,0:T(8,128)}) %all-reduce.21.cloned.1.call-update) | async-done | bytes 65552 | tf_op jit(solution)/shard_map/psum | solution.py:105
  1467.2 83.2 %psum.118 = f32[3,128]{1,0:T(4,128)S(1)} all-reduce(f32[3,128]{1,0:T(4,128)S(1)} %multiply_reduce_fusion.1), channel_id=1, replica_groups=mesh['sec'=32,'blk'=8] {'sec','blk'}, use_global_device_ids=true, to_apply=%region_29.30 | all-reduce | flops 384 | bytes 3072 | tf_op jit(solution)/shard_map/psum | solution.py:151
  1550.6 72.3 %psum.119 = f32[128]{0:T(128)S(1)} all-reduce(f32[128]{0:T(128)S(1)} %multiply_reduce_fusion.4), channel_id=1, replica_groups=mesh['sec'=32,'blk'=8] {'sec','blk'}, use_global_device_ids=true, to_apply=%region_32.33 | all-reduce | flops 128 | bytes 1024 | tf_op jit(solution)/shard_map/psum | solution.py:123
  (529 shorter events, 334.7 us)
Async XLA Ops:
  6.5 68.7 %all-reduce.11.cloned.1.call-start = ((), (), s32[]{:S(2)}) async-start(), calls=%async_computation | async-start | bytes 131072 | tf_op jit(solution)/shard_map/psum | solution.py:105
  9.3 233.5 %all-reduce.23.cloned.1.call-start = ((), (), s32[]{:S(2)}) async-start(), calls=%async_computation.10 | async-start | bytes 262144 | tf_op jit(solution)/shard_map/psum | solution.py:84
  26.6 59.3 %copy-start.2 = (f32[128,256]{1,0:T(8,128)S(1)}, f32[128,256]{1,0:T(8,128)}, u32[]{:S(2)}) copy-start(f32[128,256]{1,0:T(8,128)} %param.58) | copy-start | bytes 393220
  26.6 59.3 %copy-start.8 = (f32[128,256]{1,0:T(8,128)S(1)}, f32[128,256]{1,0:T(8,128)}, u32[]{:S(2)}) copy-start(f32[128,256]{1,0:T(8,128)} %param.59) | copy-start | bytes 393220
  76.1 5.4 collective-permute-start
  80.2 5.7 collective-permute-start.1
  169.6 228.7 %copy-start.11 = (f32[128]{0:T(128)}, f32[128]{0:T(128)S(1)}, u32[]{:S(2)}) copy-start(f32[128]{0:T(128)S(1)} %psum.106) | copy-start | bytes 1540
  185.0 135.7 %all-gather.12.cloned.1.call-start = ((), (), s32[]{:S(2)}) async-start(), calls=%async_computation.9 | async-start | bytes 2162688 | tf_op jit(solution)/shard_map/all_gather | solution.py:27
  244.3 154.0 %all-gather.6.cloned.1.call-start = ((), (), s32[]{:S(2)}) async-start(), calls=%async_computation.1 | async-start | bytes 2162688 | tf_op jit(solution)/shard_map/all_gather | solution.py:27
  244.9 293.6 %all-reduce.13.cloned.1.call-start = ((), (), s32[]{:S(2)}) async-start(), calls=%async_computation.2 | async-start | bytes 131072 | tf_op jit(solution)/shard_map/psum | solution.py:105
  398.3 81.4 %copy-start.7 = (bf16[256,128]{1,0:T(8,128)(2,1)S(1)}, bf16[256,128]{1,0:T(8,128)(2,1)}, u32[]{:S(2)}) copy-start(bf16[256,128]{1,0:T(8,128)(2,1)} %param.64) | copy-start | bytes 196612
  480.4 298.2 %all-reduce.15.cloned.1.call-start = ((), (), s32[]{:S(2)}) async-start(), calls=%async_computation.3 | async-start | bytes 131072 | tf_op jit(solution)/shard_map/psum | solution.py:140
  539.3 4.9 collective-permute-start.2
  542.9 5.7 collective-permute-start.3
  720.0 136.3 %all-gather.8.cloned.1.call-start = ((), (), s32[]{:S(2)}) async-start(), calls=%async_computation.4 | async-start | bytes 2162688 | tf_op jit(solution)/shard_map/all_gather | solution.py:27
  778.6 218.5 %all-reduce.17.cloned.1.call-start = ((), (), s32[]{:S(2)}) async-start(), calls=%async_computation.5 | async-start | bytes 131072 | tf_op jit(solution)/shard_map/psum | solution.py:105
  939.1 298.2 %all-reduce.19.cloned.1.call-start = ((), (), s32[]{:S(2)}) async-start(), calls=%async_computation.6 | async-start | bytes 131072 | tf_op jit(solution)/shard_map/psum | solution.py:140
  998.0 4.9 collective-permute-start.4
  1001.6 5.7 collective-permute-start.5
  1178.8 136.2 %all-gather.10.cloned.1.call-start = ((), (), s32[]{:S(2)}) async-start(), calls=%async_computation.7 | async-start | bytes 2162688 | tf_op jit(solution)/shard_map/all_gather | solution.py:27
  1237.3 218.3 %all-reduce.21.cloned.1.call-start = ((), (), s32[]{:S(2)}) async-start(), calls=%async_computation.8 | async-start | bytes 131072 | tf_op jit(solution)/shard_map/psum | solution.py:105
  1456.6 175.3 %copy-start.5 = (f32[128,256]{1,0:T(8,128)S(1)}, f32[128,256]{1,0:T(8,128)}, u32[]{:S(2)}) copy-start(f32[128,256]{1,0:T(8,128)} %get-tuple-element.725) | copy-start | bytes 393220
  1456.6 5.0 collective-permute-start.6
  1460.3 5.7 collective-permute-start.7
  (7 other events, 206.9 us)
Sparse Core Ops, SparseCore 0:
  9.7 65.5 all-reduce.10
  185.1 57.6 all-reduce.22
  245.4 75.2 all-gather.11
  323.1 75.1 all-gather.5
  480.5 57.8 all-reduce.12
  720.2 58.4 all-reduce.14
  781.2 75.1 all-gather.7
  939.3 57.8 all-reduce.16
  1178.9 58.4 all-reduce.18
  1239.8 75.1 all-gather.9
  1397.8 57.8 all-reduce.20
where the time goes:
time: 1650 us; the launch traced here: 1640 us
  waiting for transfers between devices  702 us (43%)
  blocking collectives  674 us (41%)
  matrix products  116 us (7%)
  local copies, waits for them, and re-layouts  91.5 us (6%)
  other arithmetic  20.7 us (1%)
  starting transfers between devices  18.2 us (1%)
    all_gather x4, waiting for transfers between devices, entering(): pieces = jax.tree.map(lambda part: lax.all_gather(part, axis), value)  302 us
    psum x4, blocking collectives, lengths(): lax.psum(jnp.sum(vector * vector, axis=1), ('sec', 'blk')) + epsilon  300 us
    psum x3, blocking collectives, local(): lax.psum(jnp.sum(product[None] * stacked, axis=2), ('sec', 'blk'))  250 us
    psum x4, waiting for transfers between devices, operator(): lax.psum(jnp.dot(rounded, ahead_panel, preferred_element_type=jnp.float32...  207 us
    psum x2, waiting for transfers between devices, local(): lax.psum(jnp.dot(precondition_folded, selector, precision=highest), 'blk')  117 us
    dot_general x93, matrix products, compose(): jnp.dot(first_value, second_map.T, precision=highest) + second_value  97.7 us
    dynamic_slice x186, local copies, waits for them, and re-layouts, step(): longer = join(so_far, jax.tree.map(lambda part: part[position], pieces))  87 us
    all_gather x4, blocking collectives, operator(): lax.all_gather(rounded, 'blk', axis=1, tiled=True)  69.6 us
  transfers between devices with their start and end apart: 19, of which 15 were waited for; matrix products, arithmetic and copies ran while one was open for 1% of the time, Pallas kernels for 0%

commit v1 on v0

--- a/solution.py
+++ b/solution.py
@@ -1,7 +1,13 @@
+import functools
+
 import jax
 import jax.numpy as jnp
 from jax import lax
+from jax.experimental import pallas as pl
+from jax.experimental.pallas import tpu as pltpu
 from jax.sharding import PartitionSpec as P
+
+MESH = pl.DeviceIdType.MESH
 
 KRYLOV = 3
 
@@ -34,6 +40,83 @@
         return jax.tree.map(lambda new, old: jnp.where(position < mine, new, old), longer, so_far)
 
     return lax.fori_loop(0, count - 1, step, so_far)
+
+
+def _reduce_kernel(stages, x_ref, o_ref, *scratch):
+    count = len(stages)
+    slots = scratch[:count]
+    partial = scratch[count]
+    sends = scratch[count + 1 : 2 * count + 1]
+    recvs = scratch[2 * count + 1 :]
+    barrier = pltpu.get_barrier_semaphore()
+    peers = 0
+    for axis, n in stages:
+        mine = lax.axis_index(axis)
+        for k in range(1, n):
+            pl.semaphore_signal(
+                barrier, inc=1, device_id={axis: lax.rem(mine + k, n)}, device_id_type=MESH
+            )
+            peers += 1
+    pl.semaphore_wait(barrier, peers)
+    source = x_ref
+    for stage, (axis, n) in enumerate(stages):
+        mine = lax.axis_index(axis)
+        copies = []
+        for k in range(1, n):
+            copy = pltpu.make_async_remote_copy(
+                src_ref=source,
+                dst_ref=slots[stage].at[mine],
+                send_sem=sends[stage].at[k],
+                recv_sem=recvs[stage].at[mine],
+                device_id={axis: lax.rem(mine + k, n)},
+                device_id_type=MESH,
+            )
+            copy.start()
+            copies.append(copy)
+        slots[stage][mine] = source[...]
+        for k in range(1, n):
+            sender = lax.rem(mine + k, n)
+            pltpu.make_async_remote_copy(
+                src_ref=source,
+                dst_ref=slots[stage].at[sender],
+                send_sem=sends[stage].at[k],
+                recv_sem=recvs[stage].at[sender],
+                device_id={axis: sender},
+                device_id_type=MESH,
+            ).wait_recv()
+        for copy in copies:
+            copy.wait_send()
+        total = slots[stage][0]
+        for j in range(1, n):
+            total = total + slots[stage][j]
+        if stage == count - 1:
+            o_ref[...] = total
+        else:
+            partial[...] = total
+            source = partial
+
+
+def all_sum(x, axes, mesh_shape, collective):
+    stages = tuple((axis, mesh_shape[axis]) for axis in axes if mesh_shape[axis] > 1)
+    rows, cols = x.shape
+    scratch = [pltpu.VMEM((n, rows, cols), jnp.float32) for _, n in stages]
+    scratch.append(pltpu.VMEM((rows, cols), jnp.float32))
+    scratch += [pltpu.SemaphoreType.DMA((n,)) for _, n in stages]
+    scratch += [pltpu.SemaphoreType.DMA((n,)) for _, n in stages]
+    return pl.pallas_call(
+        functools.partial(_reduce_kernel, stages),
+        out_shape=jax.ShapeDtypeStruct((rows, cols), jnp.float32),
+        in_specs=[pl.BlockSpec(memory_space=pltpu.VMEM)],
+        out_specs=pl.BlockSpec(memory_space=pltpu.VMEM),
+        scratch_shapes=scratch,
+        compiler_params=pltpu.CompilerParams(collective_id=collective, has_side_effects=True),
+    )(x.astype(jnp.float32))
+
+
+def global_sum(rows_of_sums, mesh_shape):
+    count = rows_of_sums.shape[0]
+    padded = jnp.zeros((8, rows_of_sums.shape[1]), jnp.float32).at[:count].set(rows_of_sums)
+    return all_sum(padded, ("blk", "sec"), mesh_shape, 0)[:count]
 
 
 def least_squares(hessen, beta):
@@ -67,6 +150,7 @@
 
 
 def local(
+    mesh_shape,
     state_now, source, fan_gain, section_block, block_inverse, back_panel, ahead_panel, interface
 ):
     highest = lax.Precision.HIGHEST
@@ -81,7 +165,7 @@
         lax.all_gather(back_panel, "blk", axis=0, tiled=True),
         preferred_element_type=jnp.float32,
     )
-    panel_maps = -lax.psum(jnp.dot(selector.T, gain_panel, precision=highest), "blk")
+    panel_maps = -all_sum(jnp.dot(selector.T, gain_panel, precision=highest), ("blk",), mesh_shape, 1)
 
     def section_terms(dense_part, behind_vals, piece):
         width = piece.shape[1]
@@ -102,7 +186,9 @@
         start_carry = (empty_dense, empty_panel)
         folded = fold_section(start_carry, lax.all_gather(rounded, "blk", axis=1, tiled=True))
         dense_part, behind_vals = folded
-        upward = lax.psum(jnp.dot(rounded, ahead_panel, preferred_element_type=jnp.float32), "blk")
+        upward = all_sum(
+            jnp.dot(rounded, ahead_panel, preferred_element_type=jnp.float32), ("blk",), mesh_shape, 1
+        )
         framed = extended(jnp.stack([behind_vals, upward])[None], (("sec", 0),), 1)
         behind = framed[0, 0].astype(jnp.bfloat16)
         ahead_term = framed[2, 1]
@@ -120,7 +206,7 @@
         return (joined_map, joined_value)
 
     def lengths(vector):
-        return jnp.sqrt(lax.psum(jnp.sum(vector * vector, axis=1), ("sec", "blk")) + epsilon)
+        return jnp.sqrt(global_sum(jnp.sum(vector * vector, axis=1)[None], mesh_shape)[0] + epsilon)
 
     bent = jnp.tanh(state_now)
     residual = source - operator(state_now) - fan_gain[None, :] * bent
@@ -137,7 +223,9 @@
             contract,
             preferred_element_type=jnp.float32,
         )
-        values = lax.psum(jnp.dot(precondition_folded, selector, precision=highest), "blk")
+        values = all_sum(
+            jnp.dot(precondition_folded, selector, precision=highest), ("blk",), mesh_shape, 1
+        )
         identity = (
             jnp.eye(panel_width, dtype=jnp.float32),
             jnp.zeros((cases, panel_width), jnp.float32),
@@ -148,7 +236,7 @@
         )
         product = operator(direction) + jac_diag * direction
         stacked = jnp.stack(basis)
-        projections = lax.psum(jnp.sum(product[None] * stacked, axis=2), ("sec", "blk"))
+        projections = global_sum(jnp.sum(product[None] * stacked, axis=2), mesh_shape)
         product = product - jnp.sum(projections[:, :, None] * stacked, axis=0)
         length = lengths(product)
         hessen = hessen.at[:, : column + 1, column].set(projections.T)
@@ -174,4 +262,4 @@
         P("sec", None),
     )
     out_specs = P(None, ("sec", "blk"))
-    return jax.shard_map(local, mesh=mesh, in_specs=in_specs, out_specs=out_specs, check_vma=False)
+    return jax.shard_map(functools.partial(local, dict(mesh.shape)), mesh=mesh, in_specs=in_specs, out_specs=out_specs, check_vma=False)

time: 1650 us -> 858 us (0.52)
  blocking collectives: 674 us -> 127 us
  waiting for transfers between devices: 702 us -> 224 us
  Pallas kernels: 0 us -> 229 us
    psum x7 -> x0, blocking collectives: 550 us -> none  [the longest x4 300 us: lengths(): lax.psum(jnp.sum(vector * vector, axis=1), ('sec', 'blk')) + epsilon]
    psum x7 -> x0, waiting for transfers between devices: 382 us -> none  [the longest x4 207 us: operator(): lax.psum(jnp.dot(rounded, ahead_panel, preferred_element_type=jnp.float32...]
    pallas_call x0 -> x15, Pallas kernels: none -> 229 us  [all_sum(): pl.pallas_call(functools.partial(_reduce_kernel, stages), out_shape=jax.S...]
    all_gather x4, waiting for transfers between devices: 302 us -> 203 us  [entering(): pieces = jax.tree.map(lambda part: lax.all_gather(part, axis), value)]
  transfers between devices with their start and end apart: 19 -> 12, of which waited for: 15 -> 7; matrix products, arithmetic and copies ran while one was open for 1% -> 2% of each run, Pallas kernels for 0% -> 6%
where the time goes in v1:
time: 858 us; the launch traced here: 847 us
  Pallas kernels  229 us (27%)
  waiting for transfers between devices  224 us (26%)
  blocking collectives  127 us (15%)
  matrix products  115 us (13%)
  local copies, waits for them, and re-layouts  98 us (11%)
  other arithmetic  23 us (3%)
  between operations  13.9 us (2%)
  starting transfers between devices  13.4 us (2%)
    pallas_call x15, Pallas kernels, all_sum(): pl.pallas_call(functools.partial(_reduce_kernel, stages), out_shape=jax.S...  229 us
    all_gather x4, waiting for transfers between devices, entering(): pieces = jax.tree.map(lambda part: lax.all_gather(part, axis), value)  203 us
    dot_general x93, matrix products, compose(): jnp.dot(first_value, second_map.T, precision=highest) + second_value  97.8 us
    dynamic_slice x186, local copies, waits for them, and re-layouts, step(): longer = join(so_far, jax.tree.map(lambda part: part[position], pieces))  87 us
    all_gather x4, blocking collectives, operator(): lax.all_gather(rounded, 'blk', axis=1, tiled=True)  66.4 us
    all_gather x3, blocking collectives, local(): lax.all_gather(precondition_rounded, 'blk', axis=1, tiled=True)  44.2 us
    ppermute x4, waiting for transfers between devices, extended(): after = lax.ppermute(first, axis, down)  21.1 us
  transfers between devices with their start and end apart: 12, of which 7 were waited for; matrix products, arithmetic and copies ran while one was open for 2% of the time, Pallas kernels for 6%

profile of v1, /device:TPU:1, one launch (start us, length us, event | category | flops | bytes accessed | tf_op | source)
XLA Modules:
  0.0 847.5 jit_solution(6459418842264342692)
XLA Ops:
  6.6 16.5 %all_gather.54 = bf16[2048,128]{1,0:T(8,128)(2,1)S(1)} all-gather(bf16[256,128]{1,0:T(8,128)(2,1)} %param.77), channel_id=1, replica_groups=mesh['sec'=32,'blk'=8] {'blk'}, dimensions={0}, use_global_device_ids=true | all-gather | bytes 589824 | tf_op jit(solution)/shard_map/all_gather | solution.py:165
  49.5 12.8 %all_gather.52 = bf16[128,2048]{1,0:T(8,128)(2,1)S(1)} all-gather(bf16[128,256]{1,0:T(8,128)(2,1)S(1)} %convert_element_type.42), channel_id=1, replica_groups=mesh['sec'=32,'blk'=8] {'blk'}, dimensions={1}, use_global_device_ids=true | all-gather | bytes 589824 | tf_op jit(solution)/shard_map/all_gather | solution.py:187
  73.4 24.2 %shard_map.83 = f32[8,128]{1,0:T(8,128)} custom-call(f32[8,128]{1,0:T(8,128)} %scatter.50.x_ref), custom_call_target="tpu_custom_call" | custom-call | tf_op jit(solution)/shard_map/pallas_call | solution.py:106
  98.3 14.5 %all_gather.53 = bf16[128,2048]{1,0:T(8,128)(2,1)S(1)} all-gather(bf16[128,256]{1,0:T(8,128)(2,1)S(1)} %fusion.94), channel_id=1, replica_groups=mesh['sec'=32,'blk'=8] {'blk'}, dimensions={1}, use_global_device_ids=true | all-gather | bytes 589824 | tf_op jit(solution)/shard_map/all_gather | solution.py:221
  125.7 70.4 %all-gather.11.cloned.1.call-done = f32[4096,128]{1,0:T(8,128)} async-done(((f32[128,128]{1,0:T(8,128)}), f32[4096,128]{1,0:T(8,128)}) %all-gather.11.cloned.1.call-update) | async-done | bytes 2097168 | tf_op jit(solution)/shard_map/all_gather | solution.py:33
  196.1 63.2 %while.71 = (s32[]{:T(128)}, f32[128,128]{0,1:T(8,128)S(1)}, s32[]{:T(128)}, f32[32,128,128]{2,1,0:T(8,128)}, f32[32,128,128]{2,1,0:T(8,128)}, /*index=5*/s32[]{:T(128)}, s32[]{:T(128)}) while((s32[]{:T(128)}, f32[128,128]{0,1:T(8,128)S(1)}, s32[]{:T(128)}, f32[32,128,128]{2,1,0:T(8,128)}, f32[32,128,128]{2,1,0:T(8,128)}, ...), condition=%wide.region_4.5_spmd.clone, body=%wide.region_3.4_spmd.clone.sunk | while | flops 25231364 | bytes 723043 | solution.py:42
  259.6 17.8 %all_gather.59 = bf16[128,2048]{1,0:T(8,128)(2,1)S(1)} all-gather(bf16[128,256]{1,0:T(8,128)(2,1)S(1)} %get-tuple-element.792), channel_id=1, replica_groups=mesh['sec'=32,'blk'=8] {'blk'}, dimensions={1}, use_global_device_ids=true | all-gather | bytes 589824 | tf_op jit(solution)/shard_map/all_gather | solution.py:187
  278.6 11.6 %shard_map.86 = f32[128,128]{1,0:T(8,128)} custom-call(f32[128,128]{1,0:T(8,128)} %fusion.111.x_ref), custom_call_target="tpu_custom_call" | custom-call | tf_op jit(solution)/shard_map/pallas_call | solution.py:106
  301.6 20.4 %shard_map.87 = f32[8,128]{1,0:T(8,128)} custom-call(f32[8,128]{1,0:T(8,128)} %scatter.51.x_ref), custom_call_target="tpu_custom_call" | custom-call | tf_op jit(solution)/shard_map/pallas_call | solution.py:106
  323.4 17.4 %shard_map.88 = f32[8,128]{1,0:T(8,128)} custom-call(f32[8,128]{1,0:T(8,128)} %scatter.55.x_ref), custom_call_target="tpu_custom_call" | custom-call | tf_op jit(solution)/shard_map/pallas_call | solution.py:106
  341.6 14.8 %all_gather.60 = bf16[128,2048]{1,0:T(8,128)(2,1)S(1)} all-gather(bf16[128,256]{1,0:T(8,128)(2,1)S(1)} %get-tuple-element.764), channel_id=1, replica_groups=mesh['sec'=32,'blk'=8] {'blk'}, dimensions={1}, use_global_device_ids=true | all-gather | bytes 589824 | tf_op jit(solution)/shard_map/all_gather | solution.py:221
  369.2 69.8 %all-gather.13.cloned.1.call-done = f32[4096,128]{1,0:T(8,128)} async-done(((f32[128,128]{1,0:T(8,128)}), f32[4096,128]{1,0:T(8,128)}) %all-gather.13.cloned.1.call-update) | async-done | bytes 2097168 | tf_op jit(solution)/shard_map/all_gather | solution.py:33
  439.0 63.2 %while.72 = (s32[]{:T(128)}, f32[128,128]{0,1:T(8,128)S(1)}, s32[]{:T(128)}, f32[32,128,128]{2,1,0:T(8,128)}, f32[32,128,128]{2,1,0:T(8,128)}, /*index=5*/s32[]{:T(128)}, s32[]{:T(128)}) while((s32[]{:T(128)}, f32[128,128]{0,1:T(8,128)S(1)}, s32[]{:T(128)}, f32[32,128,128]{2,1,0:T(8,128)}, f32[32,128,128]{2,1,0:T(8,128)}, ...), condition=%wide.region_8.9_spmd.clone, body=%wide.region_7.8_spmd.clone.sunk | while | flops 25231364 | bytes 723043 | solution.py:42
  503.2 18.0 %all_gather.63 = bf16[128,2048]{1,0:T(8,128)(2,1)S(1)} all-gather(bf16[128,256]{1,0:T(8,128)(2,1)S(1)} %get-tuple-element.794), channel_id=1, replica_groups=mesh['sec'=32,'blk'=8] {'blk'}, dimensions={1}, use_global_device_ids=true | all-gather | bytes 589824 | tf_op jit(solution)/shard_map/all_gather | solution.py:187
  522.3 11.6 %shard_map.90 = f32[128,128]{1,0:T(8,128)} custom-call(f32[128,128]{1,0:T(8,128)} %fusion.114.x_ref), custom_call_target="tpu_custom_call" | custom-call | tf_op jit(solution)/shard_map/pallas_call | solution.py:106
  545.3 20.4 %shard_map.91 = f32[8,128]{1,0:T(8,128)} custom-call(f32[8,128]{1,0:T(8,128)} %scatter.59.x_ref), custom_call_target="tpu_custom_call" | custom-call | tf_op jit(solution)/shard_map/pallas_call | solution.py:106
  567.2 17.4 %shard_map.92 = f32[8,128]{1,0:T(8,128)} custom-call(f32[8,128]{1,0:T(8,128)} %scatter.61.x_ref), custom_call_target="tpu_custom_call" | custom-call | tf_op jit(solution)/shard_map/pallas_call | solution.py:106
  585.4 14.8 %all_gather.64 = bf16[128,2048]{1,0:T(8,128)(2,1)S(1)} all-gather(bf16[128,256]{1,0:T(8,128)(2,1)S(1)} %get-tuple-element.760), channel_id=1, replica_groups=mesh['sec'=32,'blk'=8] {'blk'}, dimensions={1}, use_global_device_ids=true | all-gather | bytes 589824 | tf_op jit(solution)/shard_map/all_gather | solution.py:221
  619.8 63.0 %all-gather.15.cloned.1.call-done = f32[4096,128]{1,0:T(8,128)} async-done(((f32[128,128]{1,0:T(8,128)}), f32[4096,128]{1,0:T(8,128)}) %all-gather.15.cloned.1.call-update) | async-done | bytes 2097168 | tf_op jit(solution)/shard_map/all_gather | solution.py:33
  682.7 63.2 %while.73 = (s32[]{:T(128)}, f32[128,128]{0,1:T(8,128)S(1)}, s32[]{:T(128)}, f32[32,128,128]{2,1,0:T(8,128)}, f32[32,128,128]{2,1,0:T(8,128)}, /*index=5*/s32[]{:T(128)}, s32[]{:T(128)}) while((s32[]{:T(128)}, f32[128,128]{0,1:T(8,128)S(1)}, s32[]{:T(128)}, f32[32,128,128]{2,1,0:T(8,128)}, f32[32,128,128]{2,1,0:T(8,128)}, ...), condition=%wide.region_14.15_spmd.clone, body=%wide.region_13.14_spmd.clone.sunk | while | flops 25231364 | bytes 723043 | solution.py:42
  747.0 17.8 %all_gather.67 = bf16[128,2048]{1,0:T(8,128)(2,1)S(1)} all-gather(bf16[128,256]{1,0:T(8,128)(2,1)S(1)} %get-tuple-element.796), channel_id=1, replica_groups=mesh['sec'=32,'blk'=8] {'blk'}, dimensions={1}, use_global_device_ids=true | all-gather | bytes 589824 | tf_op jit(solution)/shard_map/all_gather | solution.py:187
  765.9 11.6 %shard_map.94 = f32[128,128]{1,0:T(8,128)} custom-call(f32[128,128]{1,0:T(8,128)} %fusion.117.x_ref), custom_call_target="tpu_custom_call" | custom-call | tf_op jit(solution)/shard_map/pallas_call | solution.py:106
  789.7 20.4 %shard_map.95 = f32[8,128]{1,0:T(8,128)} custom-call(f32[8,128]{1,0:T(8,128)} %scatter.65.x_ref), custom_call_target="tpu_custom_call" | custom-call | tf_op jit(solution)/shard_map/pallas_call | solution.py:106
  811.6 17.4 %shard_map.96 = f32[8,128]{1,0:T(8,128)} custom-call(f32[8,128]{1,0:T(8,128)} %scatter.69.x_ref), custom_call_target="tpu_custom_call" | custom-call | tf_op jit(solution)/shard_map/pallas_call | solution.py:106
  (528 shorter events, 326.8 us)
Async XLA Ops:
  6.5 16.6 %copy-start = (bf16[256,2048]{1,0:T(8,128)(2,1)S(1)}, bf16[256,2048]{1,0:T(8,128)(2,1)}, u32[]{:S(2)}) copy-start(bf16[256,2048]{1,0:T(8,128)(2,1)} %param.76) | copy-start | bytes 3145732
  6.5 17.0 %copy-start.9 = (s32[1,128]{1,0:T(1,128)S(1)}, s32[1,128]{1,0:T(1,128)}, u32[]{:S(2)}) copy-start(s32[1,128]{1,0:T(1,128)} %param.79) | copy-start | bytes 1540
  6.5 30.9 %copy-start.2 = (f32[128,256]{1,0:T(8,128)S(1)}, f32[128,256]{1,0:T(8,128)}, u32[]{:S(2)}) copy-start(f32[128,256]{1,0:T(8,128)} %param.72) | copy-start | bytes 393220
  6.5 31.0 %copy-start.7 = (bf16[256,128]{1,0:T(8,128)(2,1)S(1)}, bf16[256,128]{1,0:T(8,128)(2,1)}, u32[]{:S(2)}) copy-start(bf16[256,128]{1,0:T(8,128)(2,1)} %param.78) | copy-start | bytes 196612
  6.5 119.2 %all-gather.9.cloned.1.call-start = ((), (), s32[]{:S(2)}) async-start(), calls=%async_computation | async-start | bytes 2162688 | tf_op jit(solution)/shard_map/all_gather | solution.py:33
  23.1 43.9 %copy-start.1 = (bf16[256,2048]{1,0:T(8,128)(2,1)S(1)}, bf16[256,2048]{1,0:T(8,128)(2,1)}, u32[]{:S(2)}) copy-start(bf16[256,2048]{1,0:T(8,128)(2,1)} %param.75) | copy-start | bytes 3145732
  24.6 43.0 %copy-start.3 = (bf16[256,128]{1,0:T(8,128)(2,1)S(1)}, bf16[256,128]{1,0:T(8,128)(2,1)}, u32[]{:S(2)}) copy-start(bf16[256,128]{1,0:T(8,128)(2,1)} %param.77) | copy-start | bytes 196612
  37.4 35.0 %copy-start.8 = (f32[128,256]{1,0:T(8,128)S(1)}, f32[128,256]{1,0:T(8,128)}, u32[]{:S(2)}) copy-start(f32[128,256]{1,0:T(8,128)} %param.73) | copy-start | bytes 393220
  37.4 35.0 %copy-start.10 = (f32[256]{0:T(256)S(1)}, f32[256]{0:T(256)}, u32[]{:S(2)}) copy-start(f32[256]{0:T(256)} %param.74) | copy-start | bytes 3076
  37.4 158.7 %all-gather.11.cloned.1.call-start = ((), (), s32[]{:S(2)}) async-start(), calls=%async_computation.1 | async-start | bytes 2162688 | tf_op jit(solution)/shard_map/all_gather | solution.py:33
  63.6 4.0 collective-permute-start
  65.7 6.6 collective-permute-start.1
  125.6 313.4 %all-gather.13.cloned.1.call-start = ((), (), s32[]{:S(2)}) async-start(), calls=%async_computation.2 | async-start | bytes 2162688 | tf_op jit(solution)/shard_map/all_gather | solution.py:33
  291.0 3.8 collective-permute-start.2
  293.5 7.0 collective-permute-start.3
  369.2 313.6 %all-gather.15.cloned.1.call-start = ((), (), s32[]{:S(2)}) async-start(), calls=%async_computation.3 | async-start | bytes 2162688 | tf_op jit(solution)/shard_map/all_gather | solution.py:33
  533.9 10.3 %copy-start.4 = (f32[128,256]{1,0:T(8,128)S(1)}, f32[128,256]{1,0:T(8,128)}, u32[]{:S(2)}) copy-start(f32[128,256]{1,0:T(8,128)} %get-tuple-element.795) | copy-start | bytes 393220
  534.8 3.7 collective-permute-start.4
  537.3 7.0 collective-permute-start.5
  777.5 10.5 %copy-start.6 = (f32[128,256]{1,0:T(8,128)S(1)}, f32[128,256]{1,0:T(8,128)}, u32[]{:S(2)}) copy-start(f32[128,256]{1,0:T(8,128)} %get-tuple-element.797) | copy-start | bytes 393220
  778.4 60.8 %copy-start.5 = (f32[128,256]{1,0:T(8,128)S(1)}, f32[128,256]{1,0:T(8,128)}, u32[]{:S(2)}) copy-start(f32[128,256]{1,0:T(8,128)} %get-tuple-element.795) | copy-start | bytes 393220
  778.4 3.9 collective-permute-start.6
  781.0 7.0 collective-permute-start.7
Sparse Core Ops, SparseCore 0:
  37.5 75.2 all-gather.8
  125.7 70.3 all-gather.10
  369.3 69.6 all-gather.12
  613.0 69.6 all-gather.14

commit v2 on v1

--- a/solution.py
+++ b/solution.py
@@ -119,6 +119,100 @@
     return all_sum(padded, ("blk", "sec"), mesh_shape, 0)[:count]
 
 
+def _doubling(n):
+    distances, d = [], 1
+    while d < n:
+        distances.append(d)
+        d *= 2
+    return tuple(distances)
+
+
+def _greet(n, distances):
+    barrier = pltpu.get_barrier_semaphore()
+    mine = lax.axis_index("sec")
+    for d in distances:
+        for peer in (lax.rem(mine + d, n), lax.rem(mine + n - d, n)):
+            pl.semaphore_signal(barrier, inc=1, device_id={"sec": peer}, device_id_type=MESH)
+    pl.semaphore_wait(barrier, 2 * len(distances))
+
+
+def _hop(n, d, source, slot, send_sem, recv_sem):
+    mine = lax.axis_index("sec")
+    copy = pltpu.make_async_remote_copy(
+        src_ref=source,
+        dst_ref=slot,
+        send_sem=send_sem,
+        recv_sem=recv_sem,
+        device_id={"sec": lax.rem(mine + d, n)},
+        device_id_type=MESH,
+    )
+    copy.start()
+    copy.wait_recv()
+    copy.wait_send()
+
+
+def _maps_kernel(n, distances, e_ref, t_ref, slots, sends, recvs):
+    mine = lax.axis_index("sec")
+    _greet(n, distances)
+    t_ref[0] = e_ref[...]
+    for k, d in enumerate(distances[:-1]):
+        _hop(n, d, t_ref.at[k], slots.at[k], sends.at[k], recvs.at[k])
+        joined = jnp.dot(
+            slots[k], t_ref[k], precision=lax.Precision.HIGHEST, preferred_element_type=jnp.float32
+        )
+        t_ref[k + 1] = jnp.where(mine >= d, joined, t_ref[k])
+
+
+def _sweep_kernel(n, distances, f_ref, t_ref, o_ref, carry, slots, sends, recvs):
+    mine = lax.axis_index("sec")
+    _greet(n, distances)
+    carry[0] = f_ref[...]
+    for k, d in enumerate(distances):
+        _hop(n, d, carry.at[k], slots.at[k], sends.at[k], recvs.at[k])
+        joined = carry[k] + jnp.dot(
+            slots[k], t_ref[k], precision=lax.Precision.HIGHEST, preferred_element_type=jnp.float32
+        )
+        carry[k + 1] = jnp.where(mine >= d, joined, carry[k])
+    last = len(distances)
+    _hop(n, 1, carry.at[last], slots.at[last], sends.at[last], recvs.at[last])
+    o_ref[...] = jnp.where(mine >= 1, slots[last], jnp.zeros_like(o_ref))
+
+
+def scan_maps(maps_t, n):
+    distances = _doubling(n)
+    rounds, width = len(distances), maps_t.shape[0]
+    return pl.pallas_call(
+        functools.partial(_maps_kernel, n, distances),
+        out_shape=jax.ShapeDtypeStruct((rounds, width, width), jnp.float32),
+        in_specs=[pl.BlockSpec(memory_space=pltpu.VMEM)],
+        out_specs=pl.BlockSpec(memory_space=pltpu.VMEM),
+        scratch_shapes=[
+            pltpu.VMEM((rounds, width, width), jnp.float32),
+            pltpu.SemaphoreType.DMA((rounds,)),
+            pltpu.SemaphoreType.DMA((rounds,)),
+        ],
+        compiler_params=pltpu.CompilerParams(collective_id=2, has_side_effects=True),
+    )(maps_t)
+
+
+def sweep(values, chain, n):
+    distances = _doubling(n)
+    rounds = len(distances)
+    return pl.pallas_call(
+        functools.partial(_sweep_kernel, n, distances),
+        out_shape=jax.ShapeDtypeStruct(values.shape, jnp.float32),
+        in_specs=[pl.BlockSpec(memory_space=pltpu.VMEM)] * 2,
+        out_specs=pl.BlockSpec(memory_space=pltpu.VMEM),
+        scratch_shapes=[
+            pltpu.VMEM((rounds + 1,) + values.shape, jnp.float32),
+            pltpu.VMEM((rounds + 1,) + values.shape, jnp.float32),
+            pltpu.SemaphoreType.DMA((rounds + 1,)),
+            pltpu.SemaphoreType.DMA((rounds + 1,)),
+        ],
+        compiler_params=pltpu.CompilerParams(collective_id=3, has_side_effects=True),
+    )(values, chain)
+
+
 def least_squares(hessen, beta):
     cases = hessen.shape[0]
     depth = hessen.shape[2]
@@ -167,6 +261,8 @@
     )
     panel_maps = -all_sum(jnp.dot(selector.T, gain_panel, precision=highest), ("blk",), mesh_shape, 1)
 
+    chain = scan_maps(panel_maps.T, mesh_shape["sec"])
+
     def section_terms(dense_part, behind_vals, piece):
         width = piece.shape[1]
         dense_part = lax.dot_general(
@@ -226,11 +322,7 @@
         values = all_sum(
             jnp.dot(precondition_folded, selector, precision=highest), ("blk",), mesh_shape, 1
         )
-        identity = (
-            jnp.eye(panel_width, dtype=jnp.float32),
-            jnp.zeros((cases, panel_width), jnp.float32),
-        )
-        _, before = entering((panel_maps, values), "sec", compose, identity)
+        before = sweep(values, chain, mesh_shape["sec"])
         direction = precondition_folded - lax.dot_general(
             before, gain_panel, contract, precision=highest
         )

time: 858 us -> 549 us (0.64)
  waiting for transfers between devices: 224 us -> 11.7 us
  Pallas kernels: 229 us -> 335 us
  matrix products: 115 us -> 22.1 us
  local copies, waits for them, and re-layouts: 98 us -> 18.3 us
  between operations: 13.9 us -> 0.74 us
    all_gather x4 -> x0, waiting for transfers between devices: 203 us -> none  [entering(): pieces = jax.tree.map(lambda part: lax.all_gather(part, axis), value)]
    pallas_call x0 -> x4, Pallas kernels: none -> 107 us  [the longest x3 82.7 us: sweep(): pl.pallas_call(functools.partial(_sweep_kernel, n, distances), out_shape=...]
    dot_general x93 -> x0, matrix products: 97.8 us -> none  [compose(): jnp.dot(first_value, second_map.T, precision=highest) + second_value]
    dynamic_slice x186 -> x0, local copies, waits for them, and re-layouts: 87 us -> none  [step(): longer = join(so_far, jax.tree.map(lambda part: part[position], pieces))]
    ppermute x4, waiting for transfers between devices: 21.1 us -> 11.7 us  [extended(): after = lax.ppermute(first, axis, down)]
  transfers between devices with their start and end apart: 12 -> 8, of which waited for: 7 -> 3; matrix products, arithmetic and copies ran while one was open for 2% -> 3% of each run, Pallas kernels for 6% -> 7%
where the time goes in v2:
time: 549 us; the launch traced here: 547 us
  Pallas kernels  335 us (61%)
  blocking collectives  125 us (23%)
  matrix products  22.1 us (4%)
  other arithmetic  20.2 us (4%)
  local copies, waits for them, and re-layouts  18.3 us (3%)
  starting transfers between devices  14.3 us (3%)
  waiting for transfers between devices  11.7 us (2%)
    pallas_call x15, Pallas kernels, all_sum(): pl.pallas_call(functools.partial(_reduce_kernel, stages), out_shape=jax.S...  227 us
    pallas_call x3, Pallas kernels, sweep(): pl.pallas_call(functools.partial(_sweep_kernel, n, distances), out_shape=...  82.7 us
    all_gather x4, blocking collectives, operator(): lax.all_gather(rounded, 'blk', axis=1, tiled=True)  69.3 us
    all_gather x3, blocking collectives, local(): lax.all_gather(precondition_rounded, 'blk', axis=1, tiled=True)  42.4 us
    pallas_call x1, Pallas kernels, scan_maps(): pl.pallas_call(functools.partial(_maps_kernel, n, distances), out_shape=j...  24.8 us
    all_gather x1, blocking collectives, local(): lax.all_gather(back_panel, 'blk', axis=0, tiled=True)  13 us
    ppermute x4, waiting for transfers between devices, extended(): after = lax.ppermute(first, axis, down)  11.7 us
  transfers between devices with their start and end apart: 8, of which 3 were waited for; matrix products, arithmetic and copies ran while one was open for 3% of the time, Pallas kernels for 7%

profile of v2, /device:TPU:1, one launch (start us, length us, event | category | flops | bytes accessed | tf_op | source)
XLA Modules:
  0.0 546.7 jit_solution(14695191867368245276)
XLA Ops:
  1.1 16.2 %all_gather.24 = bf16[128,2048]{1,0:T(8,128)(2,1)S(1)} all-gather(bf16[128,256]{1,0:T(8,128)(2,1)S(1)} %convert_element_type.42), channel_id=1, replica_groups=mesh['sec'=32,'blk'=8] {'blk'}, dimensions={1}, use_global_device_ids=true | all-gather | bytes 589824 | tf_op jit(solution)/shard_map/all_gather | solution.py:283
  39.4 13.0 %all_gather.26 = bf16[2048,128]{1,0:T(8,128)(2,1)S(1)} all-gather(bf16[256,128]{1,0:T(8,128)(2,1)S(1)} %copy-done.3), channel_id=1, replica_groups=mesh['sec'=32,'blk'=8] {'blk'}, dimensions={0}, use_global_device_ids=true | all-gather | bytes 589824 | tf_op jit(solution)/shard_map/all_gather | solution.py:259
  66.6 24.8 %shard_map.86.t_ref = f32[5,128,128]{2,1,0:T(8,128)} custom-call(f32[128,128]{1,0:T(8,128)} %negate_bitcast_fusion.e_ref), custom_call_target="tpu_custom_call" | custom-call | tf_op jit(solution)/shard_map/pallas_call | solution.py:184
  95.4 19.5 %shard_map.83 = f32[8,128]{1,0:T(8,128)} custom-call(f32[8,128]{1,0:T(8,128)} %scatter.50.x_ref), custom_call_target="tpu_custom_call" | custom-call | tf_op jit(solution)/shard_map/pallas_call | solution.py:106
  115.8 14.3 %all_gather.25 = bf16[128,2048]{1,0:T(8,128)(2,1)S(1)} all-gather(bf16[128,256]{1,0:T(8,128)(2,1)S(1)} %fusion.67), channel_id=1, replica_groups=mesh['sec'=32,'blk'=8] {'blk'}, dimensions={1}, use_global_device_ids=true | all-gather | bytes 589824 | tf_op jit(solution)/shard_map/all_gather | solution.py:317
  131.4 11.3 %shard_map.84.f_ref = f32[128,128]{1,0:T(8,128)} custom-call(f32[128,128]{1,0:T(8,128)} %fusion.18.x_ref), custom_call_target="tpu_custom_call" | custom-call | tf_op jit(solution)/shard_map/pallas_call | solution.py:106
  142.7 27.9 %shard_map.87 = f32[128,128]{1,0:T(8,128)} custom-call(f32[128,128]{1,0:T(8,128)} %shard_map.84.f_ref, f32[5,128,128]{2,1,0:T(8,128)} %shard_map.86.t_ref), custom_call_target="tpu_custom_call" | custom-call | tf_op jit(solution)/shard_map/pallas_call | solution.py:201
  171.8 17.4 %all_gather.27 = bf16[128,2048]{1,0:T(8,128)(2,1)S(1)} all-gather(bf16[128,256]{1,0:T(8,128)(2,1)S(1)} %get-tuple-element.408), channel_id=1, replica_groups=mesh['sec'=32,'blk'=8] {'blk'}, dimensions={1}, use_global_device_ids=true | all-gather | bytes 589824 | tf_op jit(solution)/shard_map/all_gather | solution.py:283
  190.0 11.3 %shard_map.88 = f32[128,128]{1,0:T(8,128)} custom-call(f32[128,128]{1,0:T(8,128)} %fusion.84.x_ref), custom_call_target="tpu_custom_call" | custom-call | tf_op jit(solution)/shard_map/pallas_call | solution.py:106
  212.7 21.6 %shard_map.89 = f32[8,128]{1,0:T(8,128)} custom-call(f32[8,128]{1,0:T(8,128)} %scatter.51.x_ref), custom_call_target="tpu_custom_call" | custom-call | tf_op jit(solution)/shard_map/pallas_call | solution.py:106
  236.3 18.1 %shard_map.90 = f32[8,128]{1,0:T(8,128)} custom-call(f32[8,128]{1,0:T(8,128)} %scatter.55.x_ref), custom_call_target="tpu_custom_call" | custom-call | tf_op jit(solution)/shard_map/pallas_call | solution.py:106
  255.7 14.1 %all_gather.28 = bf16[128,2048]{1,0:T(8,128)(2,1)S(1)} all-gather(bf16[128,256]{1,0:T(8,128)(2,1)S(1)} %get-tuple-element.380), channel_id=1, replica_groups=mesh['sec'=32,'blk'=8] {'blk'}, dimensions={1}, use_global_device_ids=true | all-gather | bytes 589824 | tf_op jit(solution)/shard_map/all_gather | solution.py:317
  271.2 11.3 %shard_map.91.f_ref = f32[128,128]{1,0:T(8,128)} custom-call(f32[128,128]{1,0:T(8,128)} %fusion.13.x_ref), custom_call_target="tpu_custom_call" | custom-call | tf_op jit(solution)/shard_map/pallas_call | solution.py:106
  282.5 27.4 %shard_map.92 = f32[128,128]{1,0:T(8,128)} custom-call(f32[128,128]{1,0:T(8,128)} %shard_map.91.f_ref, f32[5,128,128]{2,1,0:T(8,128)} %shard_map.86.t_ref), custom_call_target="tpu_custom_call" | custom-call | tf_op jit(solution)/shard_map/pallas_call | solution.py:201
  311.1 17.8 %all_gather.29 = bf16[128,2048]{1,0:T(8,128)(2,1)S(1)} all-gather(bf16[128,256]{1,0:T(8,128)(2,1)S(1)} %get-tuple-element.410), channel_id=1, replica_groups=mesh['sec'=32,'blk'=8] {'blk'}, dimensions={1}, use_global_device_ids=true | all-gather | bytes 589824 | tf_op jit(solution)/shard_map/all_gather | solution.py:283
  329.7 11.3 %shard_map.93 = f32[128,128]{1,0:T(8,128)} custom-call(f32[128,128]{1,0:T(8,128)} %fusion.87.x_ref), custom_call_target="tpu_custom_call" | custom-call | tf_op jit(solution)/shard_map/pallas_call | solution.py:106
  354.6 21.7 %shard_map.94 = f32[8,128]{1,0:T(8,128)} custom-call(f32[8,128]{1,0:T(8,128)} %scatter.59.x_ref), custom_call_target="tpu_custom_call" | custom-call | tf_op jit(solution)/shard_map/pallas_call | solution.py:106
  378.4 17.2 %shard_map.95 = f32[8,128]{1,0:T(8,128)} custom-call(f32[8,128]{1,0:T(8,128)} %scatter.61.x_ref), custom_call_target="tpu_custom_call" | custom-call | tf_op jit(solution)/shard_map/pallas_call | solution.py:106
  396.9 14.0 %all_gather.30 = bf16[128,2048]{1,0:T(8,128)(2,1)S(1)} all-gather(bf16[128,256]{1,0:T(8,128)(2,1)S(1)} %get-tuple-element.376), channel_id=1, replica_groups=mesh['sec'=32,'blk'=8] {'blk'}, dimensions={1}, use_global_device_ids=true | all-gather | bytes 589824 | tf_op jit(solution)/shard_map/all_gather | solution.py:317
  412.3 11.3 %shard_map.96.f_ref = f32[128,128]{1,0:T(8,128)} custom-call(f32[128,128]{1,0:T(8,128)} %fusion.10.x_ref), custom_call_target="tpu_custom_call" | custom-call | tf_op jit(solution)/shard_map/pallas_call | solution.py:106
  423.6 27.3 %shard_map.97 = f32[128,128]{1,0:T(8,128)} custom-call(f32[128,128]{1,0:T(8,128)} %shard_map.96.f_ref, f32[5,128,128]{2,1,0:T(8,128)} %shard_map.86.t_ref), custom_call_target="tpu_custom_call" | custom-call | tf_op jit(solution)/shard_map/pallas_call | solution.py:201
  452.7 17.8 %all_gather.31 = bf16[128,2048]{1,0:T(8,128)(2,1)S(1)} all-gather(bf16[128,256]{1,0:T(8,128)(2,1)S(1)} %get-tuple-element.412), channel_id=1, replica_groups=mesh['sec'=32,'blk'=8] {'blk'}, dimensions={1}, use_global_device_ids=true | all-gather | bytes 589824 | tf_op jit(solution)/shard_map/all_gather | solution.py:283
  495.9 21.9 %shard_map.99 = f32[8,128]{1,0:T(8,128)} custom-call(f32[8,128]{1,0:T(8,128)} %scatter.65.x_ref), custom_call_target="tpu_custom_call" | custom-call | tf_op jit(solution)/shard_map/pallas_call | solution.py:106
  522.7 17.1 %shard_map.100 = f32[8,128]{1,0:T(8,128)} custom-call(f32[8,128]{1,0:T(8,128)} %scatter.69.x_ref), custom_call_target="tpu_custom_call" | custom-call | tf_op jit(solution)/shard_map/pallas_call | solution.py:106
  (162 shorter events, 120.4 us)
Async XLA Ops:
  0.0 52.3 %copy-start = (bf16[256,2048]{1,0:T(8,128)(2,1)S(1)}, bf16[256,2048]{1,0:T(8,128)(2,1)}, u32[]{:S(2)}) copy-start(bf16[256,2048]{1,0:T(8,128)(2,1)} %param.70) | copy-start | bytes 3145732
  0.0 38.5 %copy-start.1 = (bf16[256,2048]{1,0:T(8,128)(2,1)S(1)}, bf16[256,2048]{1,0:T(8,128)(2,1)}, u32[]{:S(2)}) copy-start(bf16[256,2048]{1,0:T(8,128)(2,1)} %param.69) | copy-start | bytes 3145732
  30.8 0.8 copy-start.6
  31.7 61.8 %collective-permute-start = (bf16[1,2,128,128]{3,2,1,0:T(8,128)(2,1)S(1)}, bf16[1,2,128,128]{3,2,1,0:T(8,128)(2,1)S(1)}, u32[]{:S(2)}, u32[]{:S(2)}) collective-permute-start(bf16[1,2,128,128]{3,2,1,0:T(8,128)(2,1)S(1)} %get-tuple-element.373), channel_id=1, source_target_pairs={{0,8},{8,16},{16,24},{24,32},{32,40},{40,48},{48,56},{56,64},{64,7... | collective-permute-start | bytes 196616 | tf_op jit(solution)/shard_map/ppermute | solution.py:25
  33.9 59.8 %collective-permute-start.1 = (f32[1,2,128,128]{3,2,1,0:T(8,128)S(1)}, f32[1,2,128,128]{3,2,1,0:T(8,128)S(1)}, u32[]{:S(2)}, u32[]{:S(2)}) collective-permute-start(f32[1,2,128,128]{3,2,1,0:T(8,128)S(1)} %get-tuple-element.374), channel_id=1, source_target_pairs={{8,0},{16,8},{24,16},{32,24},{40,32},{48,40},{56,48},{64,56},{72,6... | collective-permute-start | bytes 393224 | tf_op jit(solution)/shard_map/ppermute | solution.py:26
  38.5 0.8 copy-start.3
  93.5 0.9 copy-start.2
  93.5 1.0 copy-start.10
  93.5 1.0 copy-start.12
  171.8 17.5 %copy-start.5 = (bf16[256,128]{1,0:T(8,128)(2,1)S(1)}, bf16[256,128]{1,0:T(8,128)(2,1)}, u32[]{:S(2)}) copy-start(bf16[256,128]{1,0:T(8,128)(2,1)} %param.72) | copy-start | bytes 196612
  201.3 0.8 copy-start.7
  202.2 3.5 collective-permute-start.2
  204.4 7.2 %collective-permute-start.3 = (f32[1,2,128,128]{3,2,1,0:T(8,128)S(1)}, f32[1,2,128,128]{3,2,1,0:T(8,128)S(1)}, u32[]{:S(2)}, u32[]{:S(2)}) collective-permute-start(f32[1,2,128,128]{3,2,1,0:T(8,128)S(1)} %get-tuple-element.372), channel_id=1, source_target_pairs={{8,0},{16,8},{24,16},{32,24},{40,32},{48,40},{56,48},{64,56},{72,6... | collective-permute-start | bytes 393224 | tf_op jit(solution)/shard_map/ppermute | solution.py:26
  341.0 0.8 copy-start.8
  342.5 5.8 %collective-permute-start.4 = (bf16[1,2,128,128]{3,2,1,0:T(8,128)(2,1)}, bf16[1,2,128,128]{3,2,1,0:T(8,128)(2,1)}, u32[]{:S(2)}, u32[]{:S(2)}) collective-permute-start(bf16[1,2,128,128]{3,2,1,0:T(8,128)(2,1)} %get-tuple-element.367), channel_id=1, source_target_pairs={{0,8},{8,16},{16,24},{24,32},{32,40},{40,48},{48,56},{56,64},{64,7... | collective-permute-start | bytes 196616 | tf_op jit(solution)/shard_map/ppermute | solution.py:25
  346.3 1.4 copy-start.17
  346.3 7.3 %collective-permute-start.5 = (f32[1,2,128,128]{3,2,1,0:T(8,128)}, f32[1,2,128,128]{3,2,1,0:T(8,128)S(1)}, u32[]{:S(2)}, u32[]{:S(2)}) collective-permute-start(f32[1,2,128,128]{3,2,1,0:T(8,128)} %get-tuple-element.368), channel_id=1, source_target_pairs={{8,0},{16,8},{24,16},{32,24},{40,32},{48,40},{56,48},{64,56},{72,6... | collective-permute-start | bytes 393224 | tf_op jit(solution)/shard_map/ppermute | solution.py:26
  349.4 4.2 copy-start.13
  482.6 0.8 copy-start.9
  484.1 7.8 %collective-permute-start.6 = (bf16[1,2,128,128]{3,2,1,0:T(8,128)(2,1)S(1)}, bf16[1,2,128,128]{3,2,1,0:T(8,128)(2,1)}, u32[]{:S(2)}, u32[]{:S(2)}) collective-permute-start(bf16[1,2,128,128]{3,2,1,0:T(8,128)(2,1)S(1)} %get-tuple-element.363), channel_id=1, source_target_pairs={{0,8},{8,16},{16,24},{24,32},{32,40},{40,48},{48,56},{56,64},{64,7... | collective-permute-start | bytes 196616 | tf_op jit(solution)/shard_map/ppermute | solution.py:25
  487.7 7.2 %collective-permute-start.7 = (f32[1,2,128,128]{3,2,1,0:T(8,128)}, f32[1,2,128,128]{3,2,1,0:T(8,128)S(1)}, u32[]{:S(2)}, u32[]{:S(2)}) collective-permute-start(f32[1,2,128,128]{3,2,1,0:T(8,128)} %get-tuple-element.364), channel_id=1, source_target_pairs={{8,0},{16,8},{24,16},{32,24},{40,32},{48,40},{56,48},{64,56},{72,6... | collective-permute-start | bytes 393224 | tf_op jit(solution)/shard_map/ppermute | solution.py:26
  491.9 3.0 copy-start.4
  493.0 1.8 copy-start.14
  520.5 1.4 slice-start
  (5 other events, 3.2 us)

commit v3 on v2

--- a/solution.py
+++ b/solution.py
@@ -213,6 +213,60 @@
     )(values, chain)
 
 
+def _gather_kernel(n, x_ref, o_ref, slots, sends, recvs):
+    mine = lax.axis_index("blk")
+    barrier = pltpu.get_barrier_semaphore()
+    for k in range(1, n):
+        pl.semaphore_signal(
+            barrier, inc=1, device_id={"blk": lax.rem(mine + k, n)}, device_id_type=MESH
+        )
+    pl.semaphore_wait(barrier, n - 1)
+    copies = []
+    for k in range(1, n):
+        copy = pltpu.make_async_remote_copy(
+            src_ref=x_ref,
+            dst_ref=slots.at[mine],
+            send_sem=sends.at[k],
+            recv_sem=recvs.at[mine],
+            device_id={"blk": lax.rem(mine + k, n)},
+            device_id_type=MESH,
+        )
+        copy.start()
+        copies.append(copy)
+    slots[mine] = x_ref[...]
+    for k in range(1, n):
+        sender = lax.rem(mine + k, n)
+        pltpu.make_async_remote_copy(
+            src_ref=x_ref,
+            dst_ref=slots.at[sender],
+            send_sem=sends.at[k],
+            recv_sem=recvs.at[sender],
+            device_id={"blk": sender},
+            device_id_type=MESH,
+        ).wait_recv()
+    for copy in copies:
+        copy.wait_send()
+    width = x_ref.shape[1]
+    for j in range(n):
+        o_ref[:, j * width : (j + 1) * width] = slots[j]
+
+
+def gather_blk(x, n):
+    rows, width = x.shape
+    return pl.pallas_call(
+        functools.partial(_gather_kernel, n),
+        out_shape=jax.ShapeDtypeStruct((rows, n * width), x.dtype),
+        in_specs=[pl.BlockSpec(memory_space=pltpu.VMEM)],
+        out_specs=pl.BlockSpec(memory_space=pltpu.VMEM),
+        scratch_shapes=[
+            pltpu.VMEM((n, rows, width), x.dtype),
+            pltpu.SemaphoreType.DMA((n,)),
+            pltpu.SemaphoreType.DMA((n,)),
+        ],
+        compiler_params=pltpu.CompilerParams(collective_id=4, has_side_effects=True),
+    )(x)
+
+
 def least_squares(hessen, beta):
     cases = hessen.shape[0]
     depth = hessen.shape[2]
@@ -280,7 +334,7 @@
         empty_dense = jnp.zeros((cases, node_rows), jnp.float32)
         empty_panel = jnp.zeros((cases, panel_width), jnp.float32)
         start_carry = (empty_dense, empty_panel)
-        folded = fold_section(start_carry, lax.all_gather(rounded, "blk", axis=1, tiled=True))
+        folded = fold_section(start_carry, gather_blk(rounded, mesh_shape["blk"]))
         dense_part, behind_vals = folded
         upward = all_sum(
             jnp.dot(rounded, ahead_panel, preferred_element_type=jnp.float32), ("blk",), mesh_shape, 1
@@ -314,7 +368,7 @@
     for column in range(KRYLOV):
         precondition_rounded = basis[column].astype(jnp.bfloat16)
         precondition_folded = lax.dot_general(
-            lax.all_gather(precondition_rounded, "blk", axis=1, tiled=True),
+            gather_blk(precondition_rounded, mesh_shape["blk"]),
             block_inverse,
             contract,
             preferred_element_type=jnp.float32,

time: 549 us -> 542 us (0.987)
  blocking collectives: 125 us -> 13 us
  Pallas kernels: 335 us -> 434 us
  matrix products: 22.1 us -> 28.6 us
    all_gather x7 -> x0, blocking collectives: 112 us -> none  [the longest x4 69.3 us: operator(): lax.all_gather(rounded, 'blk', axis=1, tiled=True)]
    pallas_call x0 -> x7, Pallas kernels: none -> 100 us  [gather_blk(): pl.pallas_call(functools.partial(_gather_kernel, n), out_shape=jax.ShapeD...]
  transfers between devices with their start and end apart: 8 -> 8, of which waited for: 3 -> 3; matrix products, arithmetic and copies ran while one was open for 3% -> 2% of each run, Pallas kernels for 7% -> 7%
where the time goes in v3:
time: 542 us; the launch traced here: 540 us
  Pallas kernels  434 us (80%)
  matrix products  28.6 us (5%)
  other arithmetic  20.5 us (4%)
  waiting for transfers between devices  16.4 us (3%)
  local copies, waits for them, and re-layouts  13.3 us (2%)
  starting transfers between devices  13.3 us (2%)
  blocking collectives  13 us (2%)
    pallas_call x15, Pallas kernels, all_sum(): pl.pallas_call(functools.partial(_reduce_kernel, stages), out_shape=jax.S...  227 us
    pallas_call x7, Pallas kernels, gather_blk(): pl.pallas_call(functools.partial(_gather_kernel, n), out_shape=jax.ShapeD...  100 us
    pallas_call x3, Pallas kernels, sweep(): pl.pallas_call(functools.partial(_sweep_kernel, n, distances), out_shape=...  82.7 us
    pallas_call x1, Pallas kernels, scan_maps(): pl.pallas_call(functools.partial(_maps_kernel, n, distances), out_shape=j...  24.8 us
    ppermute x4, waiting for transfers between devices, extended(): after = lax.ppermute(first, axis, down)  16.4 us
    all_gather x1, blocking collectives, local(): lax.all_gather(back_panel, 'blk', axis=0, tiled=True)  13 us
  transfers between devices with their start and end apart: 8, of which 3 were waited for; matrix products, arithmetic and copies ran while one was open for 2% of the time, Pallas kernels for 7%

profile of v3, /device:TPU:1, one launch (start us, length us, event | category | flops | bytes accessed | tf_op | source)
XLA Modules:
  0.0 540.1 jit_solution(11647091797790757869)
XLA Ops:
  1.7 14.6 %shard_map.82 = bf16[128,2048]{1,0:T(8,128)(2,1)} custom-call(bf16[128,256]{1,0:T(8,128)(2,1)} %convert_element_type.42.x_ref), custom_call_target="tpu_custom_call" | custom-call | tf_op jit(solution)/shard_map/pallas_call | solution.py:256
  39.0 13.0 %all_gather.3 = bf16[2048,128]{1,0:T(8,128)(2,1)S(1)} all-gather(bf16[256,128]{1,0:T(8,128)(2,1)S(1)} %copy-done.7), channel_id=1, replica_groups=mesh['sec'=32,'blk'=8] {'blk'}, dimensions={0}, use_global_device_ids=true | all-gather | bytes 589824 | tf_op jit(solution)/shard_map/all_gather | solution.py:313
  53.4 11.3 %shard_map.87 = f32[128,128]{1,0:T(8,128)} custom-call(f32[128,128]{1,0:T(8,128)} %fusion.16.x_ref), custom_call_target="tpu_custom_call" | custom-call | tf_op jit(solution)/shard_map/pallas_call | solution.py:106
  66.3 24.8 %shard_map.88.t_ref = f32[5,128,128]{2,1,0:T(8,128)} custom-call(f32[128,128]{1,0:T(8,128)} %negate_bitcast_fusion.e_ref), custom_call_target="tpu_custom_call" | custom-call | tf_op jit(solution)/shard_map/pallas_call | solution.py:184
  95.0 19.6 %shard_map.84 = f32[8,128]{1,0:T(8,128)} custom-call(f32[8,128]{1,0:T(8,128)} %scatter.50.x_ref), custom_call_target="tpu_custom_call" | custom-call | tf_op jit(solution)/shard_map/pallas_call | solution.py:106
  116.1 12.6 %shard_map.85 = bf16[128,2048]{1,0:T(8,128)(2,1)} custom-call(bf16[128,256]{1,0:T(8,128)(2,1)} %fusion.67.x_ref), custom_call_target="tpu_custom_call" | custom-call | tf_op jit(solution)/shard_map/pallas_call | solution.py:256
  131.1 11.2 %shard_map.86.f_ref = f32[128,128]{1,0:T(8,128)} custom-call(f32[128,128]{1,0:T(8,128)} %fusion.18.x_ref), custom_call_target="tpu_custom_call" | custom-call | tf_op jit(solution)/shard_map/pallas_call | solution.py:106
  142.4 27.9 %shard_map.89 = f32[128,128]{1,0:T(8,128)} custom-call(f32[128,128]{1,0:T(8,128)} %shard_map.86.f_ref, f32[5,128,128]{2,1,0:T(8,128)} %shard_map.88.t_ref), custom_call_target="tpu_custom_call" | custom-call | tf_op jit(solution)/shard_map/pallas_call | solution.py:201
  172.1 15.8 %shard_map.90 = bf16[128,2048]{1,0:T(8,128)(2,1)} custom-call(bf16[128,256]{1,0:T(8,128)(2,1)} %get-tuple-element.408.x_ref), custom_call_target="tpu_custom_call" | custom-call | tf_op jit(solution)/shard_map/pallas_call | solution.py:256
  188.7 11.2 %shard_map.91 = f32[128,128]{1,0:T(8,128)} custom-call(f32[128,128]{1,0:T(8,128)} %fusion.84.x_ref), custom_call_target="tpu_custom_call" | custom-call | tf_op jit(solution)/shard_map/pallas_call | solution.py:106
  212.7 21.1 %shard_map.92 = f32[8,128]{1,0:T(8,128)} custom-call(f32[8,128]{1,0:T(8,128)} %scatter.51.x_ref), custom_call_target="tpu_custom_call" | custom-call | tf_op jit(solution)/shard_map/pallas_call | solution.py:106
  235.4 17.7 %shard_map.93 = f32[8,128]{1,0:T(8,128)} custom-call(f32[8,128]{1,0:T(8,128)} %scatter.55.x_ref), custom_call_target="tpu_custom_call" | custom-call | tf_op jit(solution)/shard_map/pallas_call | solution.py:106
  254.5 12.3 %shard_map.94 = bf16[128,2048]{1,0:T(8,128)(2,1)} custom-call(bf16[128,256]{1,0:T(8,128)(2,1)} %get-tuple-element.380.x_ref), custom_call_target="tpu_custom_call" | custom-call | tf_op jit(solution)/shard_map/pallas_call | solution.py:256
  269.2 11.2 %shard_map.95.f_ref = f32[128,128]{1,0:T(8,128)} custom-call(f32[128,128]{1,0:T(8,128)} %fusion.13.x_ref), custom_call_target="tpu_custom_call" | custom-call | tf_op jit(solution)/shard_map/pallas_call | solution.py:106
  280.5 27.4 %shard_map.96 = f32[128,128]{1,0:T(8,128)} custom-call(f32[128,128]{1,0:T(8,128)} %shard_map.95.f_ref, f32[5,128,128]{2,1,0:T(8,128)} %shard_map.88.t_ref), custom_call_target="tpu_custom_call" | custom-call | tf_op jit(solution)/shard_map/pallas_call | solution.py:201
  309.7 16.3 %shard_map.97 = bf16[128,2048]{1,0:T(8,128)(2,1)} custom-call(bf16[128,256]{1,0:T(8,128)(2,1)} %get-tuple-element.410.x_ref), custom_call_target="tpu_custom_call" | custom-call | tf_op jit(solution)/shard_map/pallas_call | solution.py:256
  351.8 21.9 %shard_map.99 = f32[8,128]{1,0:T(8,128)} custom-call(f32[8,128]{1,0:T(8,128)} %scatter.59.x_ref), custom_call_target="tpu_custom_call" | custom-call | tf_op jit(solution)/shard_map/pallas_call | solution.py:106
  375.2 16.7 %shard_map.100 = f32[8,128]{1,0:T(8,128)} custom-call(f32[8,128]{1,0:T(8,128)} %scatter.61.x_ref), custom_call_target="tpu_custom_call" | custom-call | tf_op jit(solution)/shard_map/pallas_call | solution.py:106
  393.4 12.4 %shard_map.101 = bf16[128,2048]{1,0:T(8,128)(2,1)} custom-call(bf16[128,256]{1,0:T(8,128)(2,1)} %get-tuple-element.376.x_ref), custom_call_target="tpu_custom_call" | custom-call | tf_op jit(solution)/shard_map/pallas_call | solution.py:256
  408.3 11.2 %shard_map.102.f_ref = f32[128,128]{1,0:T(8,128)} custom-call(f32[128,128]{1,0:T(8,128)} %fusion.10.x_ref), custom_call_target="tpu_custom_call" | custom-call | tf_op jit(solution)/shard_map/pallas_call | solution.py:106
  419.5 27.3 %shard_map.103 = f32[128,128]{1,0:T(8,128)} custom-call(f32[128,128]{1,0:T(8,128)} %shard_map.102.f_ref, f32[5,128,128]{2,1,0:T(8,128)} %shard_map.88.t_ref), custom_call_target="tpu_custom_call" | custom-call | tf_op jit(solution)/shard_map/pallas_call | solution.py:201
  448.6 16.3 %shard_map.104 = bf16[128,2048]{1,0:T(8,128)(2,1)} custom-call(bf16[128,256]{1,0:T(8,128)(2,1)} %get-tuple-element.412.x_ref), custom_call_target="tpu_custom_call" | custom-call | tf_op jit(solution)/shard_map/pallas_call | solution.py:256
  488.8 22.9 %shard_map.106 = f32[8,128]{1,0:T(8,128)} custom-call(f32[8,128]{1,0:T(8,128)} %scatter.65.x_ref), custom_call_target="tpu_custom_call" | custom-call | tf_op jit(solution)/shard_map/pallas_call | solution.py:106
  516.4 16.8 %shard_map.107 = f32[8,128]{1,0:T(8,128)} custom-call(f32[8,128]{1,0:T(8,128)} %scatter.69.x_ref), custom_call_target="tpu_custom_call" | custom-call | tf_op jit(solution)/shard_map/pallas_call | solution.py:106
  (162 shorter events, 125.8 us)
Async XLA Ops:
  0.0 52.0 %copy-start = (bf16[256,2048]{1,0:T(8,128)(2,1)S(1)}, bf16[256,2048]{1,0:T(8,128)(2,1)}, u32[]{:S(2)}) copy-start(bf16[256,2048]{1,0:T(8,128)(2,1)} %param.70) | copy-start | bytes 3145732
  0.0 38.2 %copy-start.1 = (bf16[256,2048]{1,0:T(8,128)(2,1)S(1)}, bf16[256,2048]{1,0:T(8,128)(2,1)}, u32[]{:S(2)}) copy-start(bf16[256,2048]{1,0:T(8,128)(2,1)} %param.69) | copy-start | bytes 3145732
  29.8 1.5 copy-start.12
  29.8 8.4 %copy-start.3 = (bf16[128,2048]{1,0:T(8,128)(2,1)S(1)}, bf16[128,2048]{1,0:T(8,128)(2,1)}, u32[]{:S(2)}) copy-start(bf16[128,2048]{1,0:T(8,128)(2,1)} %shard_map.82) | copy-start | bytes 1572868
  31.3 61.8 %collective-permute-start = (bf16[1,2,128,128]{3,2,1,0:T(8,128)(2,1)S(1)}, bf16[1,2,128,128]{3,2,1,0:T(8,128)(2,1)S(1)}, u32[]{:S(2)}, u32[]{:S(2)}) collective-permute-start(bf16[1,2,128,128]{3,2,1,0:T(8,128)(2,1)S(1)} %get-tuple-element.373), channel_id=1, source_target_pairs={{0,8},{8,16},{16,24},{24,32},{32,40},{40,48},{48,56},{56,64},{64,7... | collective-permute-start | bytes 196616 | tf_op jit(solution)/shard_map/ppermute | solution.py:25
  33.5 59.8 %collective-permute-start.1 = (f32[1,2,128,128]{3,2,1,0:T(8,128)S(1)}, f32[1,2,128,128]{3,2,1,0:T(8,128)S(1)}, u32[]{:S(2)}, u32[]{:S(2)}) collective-permute-start(f32[1,2,128,128]{3,2,1,0:T(8,128)S(1)} %get-tuple-element.374), channel_id=1, source_target_pairs={{8,0},{16,8},{24,16},{32,24},{40,32},{48,40},{56,48},{64,56},{72,6... | collective-permute-start | bytes 393224 | tf_op jit(solution)/shard_map/ppermute | solution.py:26
  93.1 1.0 copy-start.18
  172.1 15.8 %copy-start.8 = (bf16[256,128]{1,0:T(8,128)(2,1)S(1)}, bf16[256,128]{1,0:T(8,128)(2,1)}, u32[]{:S(2)}) copy-start(bf16[256,128]{1,0:T(8,128)(2,1)} %param.72) | copy-start | bytes 196612
  172.1 15.8 %copy-start.10 = (bf16[128,256]{1,0:T(8,128)(2,1)S(1)}, bf16[128,256]{1,0:T(8,128)(2,1)}, u32[]{:S(2)}) copy-start(bf16[128,256]{1,0:T(8,128)(2,1)} %get-tuple-element.408.x_ref) | copy-start | bytes 196612
  199.9 1.5 copy-start.13
  199.9 3.4 copy-start.4
  201.4 3.9 collective-permute-start.2
  203.8 7.8 %collective-permute-start.3 = (f32[1,2,128,128]{3,2,1,0:T(8,128)S(1)}, f32[1,2,128,128]{3,2,1,0:T(8,128)S(1)}, u32[]{:S(2)}, u32[]{:S(2)}) collective-permute-start(f32[1,2,128,128]{3,2,1,0:T(8,128)S(1)} %get-tuple-element.372), channel_id=1, source_target_pairs={{8,0},{16,8},{24,16},{32,24},{40,32},{48,40},{56,48},{64,56},{72,6... | collective-permute-start | bytes 393224 | tf_op jit(solution)/shard_map/ppermute | solution.py:26
  309.7 16.3 %copy-start.11 = (bf16[128,256]{1,0:T(8,128)(2,1)S(1)}, bf16[128,256]{1,0:T(8,128)(2,1)}, u32[]{:S(2)}) copy-start(bf16[128,256]{1,0:T(8,128)(2,1)} %get-tuple-element.410.x_ref) | copy-start | bytes 196612
  338.0 1.5 copy-start.14
  338.0 3.6 copy-start.5
  339.5 3.9 collective-permute-start.4
  342.0 7.9 %collective-permute-start.5 = (f32[1,2,128,128]{3,2,1,0:T(8,128)S(1)}, f32[1,2,128,128]{3,2,1,0:T(8,128)}, u32[]{:S(2)}, u32[]{:S(2)}) collective-permute-start(f32[1,2,128,128]{3,2,1,0:T(8,128)S(1)} %get-tuple-element.368), channel_id=1, source_target_pairs={{8,0},{16,8},{24,16},{32,24},{40,32},{48,40},{56,48},{64,56},{72,6... | collective-permute-start | bytes 393224 | tf_op jit(solution)/shard_map/ppermute | solution.py:26
  448.6 16.3 %copy-start.9 = (bf16[128,256]{1,0:T(8,128)(2,1)S(1)}, bf16[128,256]{1,0:T(8,128)(2,1)}, u32[]{:S(2)}) copy-start(bf16[128,256]{1,0:T(8,128)(2,1)} %get-tuple-element.412.x_ref) | copy-start | bytes 196612
  476.9 1.5 copy-start.15
  476.9 3.4 copy-start.6
  478.4 5.3 collective-permute-start.6
  480.8 7.0 %collective-permute-start.7 = (f32[1,2,128,128]{3,2,1,0:T(8,128)S(1)}, f32[1,2,128,128]{3,2,1,0:T(8,128)S(1)}, u32[]{:S(2)}, u32[]{:S(2)}) collective-permute-start(f32[1,2,128,128]{3,2,1,0:T(8,128)S(1)} %get-tuple-element.364), channel_id=1, source_target_pairs={{8,0},{16,8},{24,16},{32,24},{40,32},{48,40},{56,48},{64,56},{72,6... | collective-permute-start | bytes 393224 | tf_op jit(solution)/shard_map/ppermute | solution.py:26
  514.2 1.3 slice-start
  (5 other events, 4.0 us)

commit v4 on v3

--- a/solution.py
+++ b/solution.py
@@ -267,6 +267,123 @@
     )(x)
 
 
+def _operator_kernel(n_sec, n_blk, x_ref, up_ref, be_ref, g_ref, b_ref, a_ref, *scratch):
+    gslots, bslots, aslots, gsend, grecv, bsend, brecv, asend, arecv = scratch
+    sec, blk = lax.axis_index("sec"), lax.axis_index("blk")
+    nxt, prv = lax.rem(sec + 1, n_sec), lax.rem(sec + n_sec - 1, n_sec)
+    piece = bslots.shape[1]
+    barrier = pltpu.get_barrier_semaphore()
+    for k in range(1, n_blk):
+        pl.semaphore_signal(
+            barrier, inc=1, device_id={"blk": lax.rem(blk + k, n_blk)}, device_id_type=MESH
+        )
+    for j in range(n_blk):
+        for other in (nxt, prv):
+            pl.semaphore_signal(
+                barrier, inc=1, device_id={"sec": other, "blk": j}, device_id_type=MESH
+            )
+    pl.semaphore_wait(barrier, 3 * n_blk - 1)
+    copies = []
+    for k in range(1, n_blk):
+        copies.append(
+            pltpu.make_async_remote_copy(
+                src_ref=x_ref,
+                dst_ref=gslots.at[blk],
+                send_sem=gsend.at[k],
+                recv_sem=grecv.at[blk],
+                device_id={"blk": lax.rem(blk + k, n_blk)},
+                device_id_type=MESH,
+            )
+        )
+    mine = pl.ds(pl.multiple_of(blk * piece, 8), piece)
+    for j in range(n_blk):
+        copies.append(
+            pltpu.make_async_remote_copy(
+                src_ref=be_ref.at[mine],
+                dst_ref=bslots.at[blk],
+                send_sem=bsend.at[j],
+                recv_sem=brecv.at[blk],
+                device_id={"sec": nxt, "blk": j},
+                device_id_type=MESH,
+            )
+        )
+        copies.append(
+            pltpu.make_async_remote_copy(
+                src_ref=up_ref.at[pl.ds(j * piece, piece)],
+                dst_ref=aslots.at[blk],
+                send_sem=asend.at[j],
+                recv_sem=arecv.at[blk],
+                device_id={"sec": prv, "blk": j},
+                device_id_type=MESH,
+            )
+        )
+    for copy in copies:
+        copy.start()
+    gslots[blk] = x_ref[...]
+    for k in range(1, n_blk):
+        sender = lax.rem(blk + k, n_blk)
+        pltpu.make_async_remote_copy(
+            src_ref=x_ref,
+            dst_ref=gslots.at[sender],
+            send_sem=gsend.at[k],
+            recv_sem=grecv.at[sender],
+            device_id={"blk": sender},
+            device_id_type=MESH,
+        ).wait_recv()
+    for j in range(n_blk):
+        pltpu.make_async_remote_copy(
+            src_ref=be_ref.at[mine],
+            dst_ref=bslots.at[j],
+            send_sem=bsend.at[j],
+            recv_sem=brecv.at[j],
+            device_id={"sec": prv, "blk": j},
+            device_id_type=MESH,
+        ).wait_recv()
+        pltpu.make_async_remote_copy(
+            src_ref=up_ref.at[pl.ds(j * piece, piece)],
+            dst_ref=aslots.at[j],
+            send_sem=asend.at[j],
+            recv_sem=arecv.at[j],
+            device_id={"sec": nxt, "blk": j},
+            device_id_type=MESH,
+        ).wait_recv()
+    for copy in copies:
+        copy.wait_send()
+    width = x_ref.shape[1]
+    for j in range(n_blk):
+        g_ref[:, j * width : (j + 1) * width] = gslots[j]
+        b_ref[j * piece : (j + 1) * piece, :] = jnp.where(
+            sec >= 1, bslots[j], jnp.zeros_like(bslots[j])
+        )
+    total = aslots[0]
+    for j in range(1, n_blk):
+        total = total + aslots[j]
+    a_ref[...] = jnp.where(sec <= n_sec - 2, total, jnp.zeros_like(total))
+
+
+def operator_exchange(x, up_t, be_t, n_sec, n_blk):
+    rows, width = x.shape
+    panel, cases = up_t.shape
+    piece = panel // n_blk
+    return pl.pallas_call(
+        functools.partial(_operator_kernel, n_sec, n_blk),
+        out_shape=(
+            jax.ShapeDtypeStruct((rows, n_blk * width), x.dtype),
+            jax.ShapeDtypeStruct((panel, cases), jnp.float32),
+            jax.ShapeDtypeStruct((piece, cases), jnp.float32),
+        ),
+        in_specs=[pl.BlockSpec(memory_space=pltpu.VMEM)] * 3,
+        out_specs=[pl.BlockSpec(memory_space=pltpu.VMEM)] * 3,
+        scratch_shapes=[
+            pltpu.VMEM((n_blk, rows, width), x.dtype),
+            pltpu.VMEM((n_blk, piece, cases), jnp.float32),
+            pltpu.VMEM((n_blk, piece, cases), jnp.float32),
+        ]
+        + [pltpu.SemaphoreType.DMA((n_blk,))] * 6,
+        compiler_params=pltpu.CompilerParams(collective_id=5, has_side_effects=True),
+    )(x, up_t, be_t)
+
+
 def least_squares(hessen, beta):
     cases = hessen.shape[0]
     depth = hessen.shape[2]
@@ -331,21 +448,31 @@
 
     def operator(vector):
         rounded = vector.astype(jnp.bfloat16)
-        empty_dense = jnp.zeros((cases, node_rows), jnp.float32)
-        empty_panel = jnp.zeros((cases, panel_width), jnp.float32)
-        start_carry = (empty_dense, empty_panel)
-        folded = fold_section(start_carry, gather_blk(rounded, mesh_shape["blk"]))
-        dense_part, behind_vals = folded
-        upward = all_sum(
-            jnp.dot(rounded, ahead_panel, preferred_element_type=jnp.float32), ("blk",), mesh_shape, 1
-        )
-        framed = extended(jnp.stack([behind_vals, upward])[None], (("sec", 0),), 1)
-        behind = framed[0, 0].astype(jnp.bfloat16)
-        ahead_term = framed[2, 1]
+        n_sec, n_blk = mesh_shape["sec"], mesh_shape["blk"]
+        piece = panel_width // n_blk
+        up_t = lax.dot_general(
+            ahead_panel, rounded, (((0,), (1,)), ((), ())), preferred_element_type=jnp.float32
+        )
+        be_t = lax.dot_general(
+            selector.astype(jnp.bfloat16),
+            rounded,
+            (((0,), (1,)), ((), ())),
+            preferred_element_type=jnp.float32,
+        )
+        gathered, behind_t, ahead_piece = operator_exchange(rounded, up_t, be_t, n_sec, n_blk)
+        dense_part = lax.dot_general(
+            gathered, section_block, contract, preferred_element_type=jnp.float32
+        )
         lower_term = lax.dot_general(
-            behind, back_panel, contract, preferred_element_type=jnp.float32
-        )
-        upper_term = jnp.dot(ahead_term, selector.T, precision=highest)
+            behind_t.astype(jnp.bfloat16),
+            back_panel,
+            (((0,), (1,)), ((), ())),
+            preferred_element_type=jnp.float32,
+        )
+        local_picks = lax.dynamic_slice_in_dim(selector, lax.axis_index("blk") * piece, piece, 1)
+        upper_term = lax.dot_general(
+            ahead_piece, local_picks, (((0,), (1,)), ((), ())), precision=highest
+        )
         return dense_part + lower_term + upper_term
 
     def compose(earlier, later):

time: 542 us -> 467 us (0.86)
  Pallas kernels: 434 us -> 388 us
  waiting for transfers between devices: 16.4 us -> 0 us
  starting transfers between devices: 13.3 us -> 0 us
    pallas_call x0 -> x4, Pallas kernels: none -> 81.9 us  [operator_exchange(): pl.pallas_call(functools.partial(_operator_kernel, n_sec, n_blk), out_sha...]
    pallas_call x7 -> x3, Pallas kernels: 100 us -> 37.4 us  [gather_blk(): pl.pallas_call(functools.partial(_gather_kernel, n), out_shape=jax.ShapeD...]
    pallas_call x15 -> x11, Pallas kernels: 227 us -> 169 us  [all_sum(): pl.pallas_call(functools.partial(_reduce_kernel, stages), out_shape=jax.S...]
    ppermute x8 -> x0, waiting for transfers between devices: 16.4 us -> none  [the longest x4 16.4 us: extended(): after = lax.ppermute(first, axis, down)]
    ppermute x8 -> x0, starting transfers between devices: 13.3 us -> none  [the longest x4 7.92 us: extended(): before = lax.ppermute(last, axis, up)]
    pallas_call x1, Pallas kernels: 24.8 us -> 18.1 us  [scan_maps(): pl.pallas_call(functools.partial(_maps_kernel, n, distances), out_shape=j...]
  transfers between devices with their start and end apart: 8 -> 0, of which waited for: 3 -> 0; matrix products, arithmetic and copies ran while one was open for 2% -> 0% of each run, Pallas kernels for 7% -> 0%
where the time goes in v4:
time: 467 us; the launch traced here: 465 us
  Pallas kernels  388 us (83%)
  matrix products  30.7 us (7%)
  other arithmetic  19.7 us (4%)
  blocking collectives  12.8 us (3%)
  local copies, waits for them, and re-layouts  12.7 us (3%)
    pallas_call x11, Pallas kernels, all_sum(): pl.pallas_call(functools.partial(_reduce_kernel, stages), out_shape=jax.S...  169 us
    pallas_call x3, Pallas kernels, sweep(): pl.pallas_call(functools.partial(_sweep_kernel, n, distances), out_shape=...  82.3 us
    pallas_call x4, Pallas kernels, operator_exchange(): pl.pallas_call(functools.partial(_operator_kernel, n_sec, n_blk), out_sha...  81.9 us
    pallas_call x3, Pallas kernels, gather_blk(): pl.pallas_call(functools.partial(_gather_kernel, n), out_shape=jax.ShapeD...  37.4 us
    pallas_call x1, Pallas kernels, scan_maps(): pl.pallas_call(functools.partial(_maps_kernel, n, distances), out_shape=j...  18.1 us
    all_gather x1, blocking collectives, local(): lax.all_gather(back_panel, 'blk', axis=0, tiled=True)  12.8 us

profile of v4, /device:TPU:1, one launch (start us, length us, event | category | flops | bytes accessed | tf_op | source)
XLA Modules:
  0.0 464.8 jit_solution(12583843362340056771)
XLA Ops:
  8.1 22.1 %shard_map.82 = (bf16[128,2048]{1,0:T(8,128)(2,1)}, f32[128,128]{1,0:T(8,128)}, f32[16,128]{1,0:T(8,128)}) custom-call(bf16[128,256]{1,0:T(8,128)(2,1)} %copy-done.5, f32[128,128]{1,0:T(8,128)} %fusion.92.up_ref, f32[128,128]{1,0:T(8,128)} %fusion.24.be_ref), custom_call_target="tpu_custom_call" | custom-call | tf_op jit(solution)/shard_map/pallas_call | solution.py:368
  34.5 17.2 %shard_map.83 = f32[8,128]{1,0:T(8,128)} custom-call(f32[8,128]{1,0:T(8,128)} %scatter.50.x_ref), custom_call_target="tpu_custom_call" | custom-call | tf_op jit(solution)/shard_map/pallas_call | solution.py:106
  53.1 12.4 %shard_map.84 = bf16[128,2048]{1,0:T(8,128)(2,1)} custom-call(bf16[128,256]{1,0:T(8,128)(2,1)} %fusion.84.x_ref), custom_call_target="tpu_custom_call" | custom-call | tf_op jit(solution)/shard_map/pallas_call | solution.py:256
  67.9 11.2 %shard_map.85.f_ref = f32[128,128]{1,0:T(8,128)} custom-call(f32[128,128]{1,0:T(8,128)} %fusion.15.x_ref), custom_call_target="tpu_custom_call" | custom-call | tf_op jit(solution)/shard_map/pallas_call | solution.py:106
  79.1 12.8 %all_gather.3 = bf16[2048,128]{1,0:T(8,128)(2,1)S(1)} all-gather(bf16[256,128]{1,0:T(8,128)(2,1)S(1)} %copy-done.3), channel_id=1, replica_groups=mesh['sec'=32,'blk'=8] {'blk'}, dimensions={0}, use_global_device_ids=true | all-gather | bytes 589824 | tf_op jit(solution)/shard_map/all_gather | solution.py:430
  93.4 11.3 %shard_map.86 = f32[128,128]{1,0:T(8,128)} custom-call(f32[128,128]{1,0:T(8,128)} %fusion.13.x_ref), custom_call_target="tpu_custom_call" | custom-call | tf_op jit(solution)/shard_map/pallas_call | solution.py:106
  106.2 18.1 %shard_map.87.t_ref = f32[5,128,128]{2,1,0:T(8,128)} custom-call(f32[128,128]{1,0:T(8,128)} %negate_bitcast_fusion.e_ref), custom_call_target="tpu_custom_call" | custom-call | tf_op jit(solution)/shard_map/pallas_call | solution.py:184
  124.3 27.5 %shard_map.88 = f32[128,128]{1,0:T(8,128)} custom-call(f32[128,128]{1,0:T(8,128)} %shard_map.85.f_ref, f32[5,128,128]{2,1,0:T(8,128)} %shard_map.87.t_ref), custom_call_target="tpu_custom_call" | custom-call | tf_op jit(solution)/shard_map/pallas_call | solution.py:201
  154.7 22.0 %shard_map.89 = (bf16[128,2048]{1,0:T(8,128)(2,1)}, f32[128,128]{1,0:T(8,128)}, f32[16,128]{1,0:T(8,128)}) custom-call(bf16[128,256]{1,0:T(8,128)(2,1)} %copy-done.7, f32[128,128]{1,0:T(8,128)} %convolution_bitcast_fusion.2.up_ref, f32[128,128]{1,0:T(8,128)} %fusion.22.be_ref), custom_call_target="tpu_custom_call" | custom-call | tf_op jit(solution)/shard_map/pallas_call | solution.py:368
  180.4 16.0 %shard_map.90 = f32[8,128]{1,0:T(8,128)} custom-call(f32[8,128]{1,0:T(8,128)} %scatter.51.x_ref), custom_call_target="tpu_custom_call" | custom-call | tf_op jit(solution)/shard_map/pallas_call | solution.py:106
  197.9 18.0 %shard_map.91 = f32[8,128]{1,0:T(8,128)} custom-call(f32[8,128]{1,0:T(8,128)} %scatter.55.x_ref), custom_call_target="tpu_custom_call" | custom-call | tf_op jit(solution)/shard_map/pallas_call | solution.py:106
  217.5 12.7 %shard_map.92 = bf16[128,2048]{1,0:T(8,128)(2,1)} custom-call(bf16[128,256]{1,0:T(8,128)(2,1)} %get-tuple-element.396.x_ref), custom_call_target="tpu_custom_call" | custom-call | tf_op jit(solution)/shard_map/pallas_call | solution.py:256
  232.7 11.2 %shard_map.93.f_ref = f32[128,128]{1,0:T(8,128)} custom-call(f32[128,128]{1,0:T(8,128)} %fusion.11.x_ref), custom_call_target="tpu_custom_call" | custom-call | tf_op jit(solution)/shard_map/pallas_call | solution.py:106
  244.0 27.6 %shard_map.94 = f32[128,128]{1,0:T(8,128)} custom-call(f32[128,128]{1,0:T(8,128)} %shard_map.93.f_ref, f32[5,128,128]{2,1,0:T(8,128)} %shard_map.87.t_ref), custom_call_target="tpu_custom_call" | custom-call | tf_op jit(solution)/shard_map/pallas_call | solution.py:201
  274.5 18.9 %shard_map.95 = (bf16[128,2048]{1,0:T(8,128)(2,1)}, f32[128,128]{1,0:T(8,128)}, f32[16,128]{1,0:T(8,128)}) custom-call(bf16[128,256]{1,0:T(8,128)(2,1)} %copy-done.8, f32[128,128]{1,0:T(8,128)} %convolution_bitcast_fusion.1.up_ref, f32[128,128]{1,0:T(8,128)} %fusion.20.be_ref), custom_call_target="tpu_custom_call" | custom-call | tf_op jit(solution)/shard_map/pallas_call | solution.py:368
  297.0 18.3 %shard_map.96 = f32[8,128]{1,0:T(8,128)} custom-call(f32[8,128]{1,0:T(8,128)} %scatter.59.x_ref), custom_call_target="tpu_custom_call" | custom-call | tf_op jit(solution)/shard_map/pallas_call | solution.py:106
  318.2 18.0 %shard_map.97 = f32[8,128]{1,0:T(8,128)} custom-call(f32[8,128]{1,0:T(8,128)} %scatter.61.x_ref), custom_call_target="tpu_custom_call" | custom-call | tf_op jit(solution)/shard_map/pallas_call | solution.py:106
  337.7 12.3 %shard_map.98 = bf16[128,2048]{1,0:T(8,128)(2,1)} custom-call(bf16[128,256]{1,0:T(8,128)(2,1)} %get-tuple-element.392.x_ref), custom_call_target="tpu_custom_call" | custom-call | tf_op jit(solution)/shard_map/pallas_call | solution.py:256
  352.4 11.2 %shard_map.99.f_ref = f32[128,128]{1,0:T(8,128)} custom-call(f32[128,128]{1,0:T(8,128)} %fusion.9.x_ref), custom_call_target="tpu_custom_call" | custom-call | tf_op jit(solution)/shard_map/pallas_call | solution.py:106
  363.6 27.2 %shard_map.100 = f32[128,128]{1,0:T(8,128)} custom-call(f32[128,128]{1,0:T(8,128)} %shard_map.99.f_ref, f32[5,128,128]{2,1,0:T(8,128)} %shard_map.87.t_ref), custom_call_target="tpu_custom_call" | custom-call | tf_op jit(solution)/shard_map/pallas_call | solution.py:201
  393.7 19.0 %shard_map.101 = (bf16[128,2048]{1,0:T(8,128)(2,1)}, f32[128,128]{1,0:T(8,128)}, f32[16,128]{1,0:T(8,128)}) custom-call(bf16[128,256]{1,0:T(8,128)(2,1)} %copy-done.6, f32[128,128]{1,0:T(8,128)} %convolution_bitcast_fusion.up_ref, f32[128,128]{1,0:T(8,128)} %fusion.18.be_ref), custom_call_target="tpu_custom_call" | custom-call | tf_op jit(solution)/shard_map/pallas_call | solution.py:368
  416.2 18.8 %shard_map.102 = f32[8,128]{1,0:T(8,128)} custom-call(f32[8,128]{1,0:T(8,128)} %scatter.65.x_ref), custom_call_target="tpu_custom_call" | custom-call | tf_op jit(solution)/shard_map/pallas_call | solution.py:106
  440.4 17.5 %shard_map.103 = f32[8,128]{1,0:T(8,128)} custom-call(f32[8,128]{1,0:T(8,128)} %scatter.69.x_ref), custom_call_target="tpu_custom_call" | custom-call | tf_op jit(solution)/shard_map/pallas_call | solution.py:106
  458.8 3.2 broadcast_select_fusion
  (130 shorter events, 59.9 us)
Async XLA Ops:
  0.0 31.6 %copy-start = (bf16[256,2048]{1,0:T(8,128)(2,1)S(1)}, bf16[256,2048]{1,0:T(8,128)(2,1)}, u32[]{:S(2)}) copy-start(bf16[256,2048]{1,0:T(8,128)(2,1)} %param.69) | copy-start | bytes 3145732
  4.7 0.7 copy-start.11
  6.3 0.9 copy-start.5
  6.3 0.9 copy-start.4
  8.1 22.1 %copy-start.3 = (bf16[256,128]{1,0:T(8,128)(2,1)S(1)}, bf16[256,128]{1,0:T(8,128)(2,1)}, u32[]{:S(2)}) copy-start(bf16[256,128]{1,0:T(8,128)(2,1)} %param.71) | copy-start | bytes 196612
  30.2 1.1 copy-start.13
  30.2 1.4 copy-start.9
  31.3 0.9 copy-start.2
  31.3 0.9 copy-start.12
  32.2 33.3 %copy-start.1 = (bf16[256,2048]{1,0:T(8,128)(2,1)S(1)}, bf16[256,2048]{1,0:T(8,128)(2,1)}, u32[]{:S(2)}) copy-start(bf16[256,2048]{1,0:T(8,128)(2,1)} %param.70) | copy-start | bytes 3145732
  153.0 0.9 copy-start.7
  176.7 1.0 copy-start.14
  272.7 0.9 copy-start.8
  293.4 1.0 copy-start.15
  391.9 0.9 copy-start.6
  412.7 1.1 copy-start.10
  438.9 0.7 slice-start

commit v5 on v4

--- a/solution.py
+++ b/solution.py
@@ -158,7 +158,7 @@
     for k, d in enumerate(distances[:-1]):
         _hop(n, d, t_ref.at[k], slots.at[k], sends.at[k], recvs.at[k])
         joined = jnp.dot(
-            slots[k], t_ref[k], precision=lax.Precision.HIGHEST, preferred_element_type=jnp.float32
+            t_ref[k], slots[k], precision=lax.Precision.HIGHEST, preferred_element_type=jnp.float32
         )
         t_ref[k + 1] = jnp.where(mine >= d, joined, t_ref[k])
 
@@ -384,6 +384,109 @@
     )(x, up_t, be_t)
 
 
+def _precondition_kernel(n_sec, n_blk, distances, x_ref, inv_ref, pick_ref, u_ref, w_ref, o_ref, *scratch):
+    gslots, fslots, carry, slots, gsend, grecv, fsend, frecv, ssend, srecv = scratch
+    sec, blk = lax.axis_index("sec"), lax.axis_index("blk")
+    barrier = pltpu.get_barrier_semaphore()
+    for k in range(1, n_blk):
+        pl.semaphore_signal(
+            barrier, inc=1, device_id={"blk": lax.rem(blk + k, n_blk)}, device_id_type=MESH
+        )
+    for d in distances:
+        for peer in (lax.rem(sec + d, n_sec), lax.rem(sec + n_sec - d, n_sec)):
+            pl.semaphore_signal(barrier, inc=1, device_id={"sec": peer}, device_id_type=MESH)
+    pl.semaphore_wait(barrier, n_blk - 1 + 2 * len(distances))
+
+    def blk_copy(source, slot_ref, send, recv, k, target):
+        return pltpu.make_async_remote_copy(
+            src_ref=source,
+            dst_ref=slot_ref.at[target[1]],
+            send_sem=send.at[k],
+            recv_sem=recv.at[target[1]],
+            device_id={"blk": target[0]},
+            device_id_type=MESH,
+        )
+
+    outgoing = [
+        blk_copy(x_ref, gslots, gsend, grecv, k, (lax.rem(blk + k, n_blk), blk))
+        for k in range(1, n_blk)
+    ]
+    for copy in outgoing:
+        copy.start()
+    gslots[blk] = x_ref[...]
+    for k in range(1, n_blk):
+        sender = lax.rem(blk + k, n_blk)
+        blk_copy(x_ref, gslots, gsend, grecv, k, (sender, sender)).wait_recv()
+    for copy in outgoing:
+        copy.wait_send()
+    width = x_ref.shape[1]
+    contract = (((1,), (1,)), ((), ()))
+    folded = lax.dot_general(
+        gslots[0], inv_ref[:, 0:width], contract, preferred_element_type=jnp.float32
+    )
+    for j in range(1, n_blk):
+        folded = folded + lax.dot_general(
+            gslots[j],
+            inv_ref[:, j * width : (j + 1) * width],
+            contract,
+            preferred_element_type=jnp.float32,
+        )
+    w_ref[...] = folded
+    fslots[blk] = lax.dot_general(
+        pick_ref[...], folded, contract, precision=lax.Precision.HIGHEST,
+        preferred_element_type=jnp.float32,
+    )
+    outgoing = [
+        blk_copy(fslots.at[blk], fslots, fsend, frecv, k, (lax.rem(blk + k, n_blk), blk))
+        for k in range(1, n_blk)
+    ]
+    for copy in outgoing:
+        copy.start()
+    for k in range(1, n_blk):
+        sender = lax.rem(blk + k, n_blk)
+        blk_copy(fslots.at[blk], fslots, fsend, frecv, k, (sender, sender)).wait_recv()
+    for copy in outgoing:
+        copy.wait_send()
+    piece = fslots.shape[1]
+    for j in range(n_blk):
+        carry[0, j * piece : (j + 1) * piece, :] = fslots[j]
+    for k, d in enumerate(distances):
+        _hop(n_sec, d, carry.at[k], slots.at[k], ssend.at[k], srecv.at[k])
+        joined = carry[k] + jnp.dot(
+            u_ref[k], slots[k], precision=lax.Precision.HIGHEST, preferred_element_type=jnp.float32
+        )
+        carry[k + 1] = jnp.where(sec >= d, joined, carry[k])
+    last = len(distances)
+    _hop(n_sec, 1, carry.at[last], slots.at[last], ssend.at[last], srecv.at[last])
+    o_ref[...] = jnp.where(sec >= 1, slots[last], jnp.zeros_like(o_ref))
+
+
+def precondition_sweep(x, inverse, picks, chain, n_sec, n_blk):
+    cases, width = x.shape
+    piece, _ = picks.shape
+    panel = piece * n_blk
+    distances = _doubling(n_sec)
+    rounds = len(distances)
+    return pl.pallas_call(
+        functools.partial(_precondition_kernel, n_sec, n_blk, distances),
+        out_shape=(
+            jax.ShapeDtypeStruct((cases, width), jnp.float32),
+            jax.ShapeDtypeStruct((panel, cases), jnp.float32),
+        ),
+        in_specs=[pl.BlockSpec(memory_space=pltpu.VMEM)] * 4,
+        out_specs=[pl.BlockSpec(memory_space=pltpu.VMEM)] * 2,
+        scratch_shapes=[
+            pltpu.VMEM((n_blk, cases, width), x.dtype),
+            pltpu.VMEM((n_blk, piece, cases), jnp.float32),
+            pltpu.VMEM((rounds + 1, panel, cases), jnp.float32),
+            pltpu.VMEM((rounds + 1, panel, cases), jnp.float32),
+        ]
+        + [pltpu.SemaphoreType.DMA((n_blk,))] * 4
+        + [pltpu.SemaphoreType.DMA((rounds + 1,))] * 2,
+        compiler_params=pltpu.CompilerParams(collective_id=6, has_side_effects=True),
+    )(x, inverse, picks, chain)
+
+
 def least_squares(hessen, beta):
     cases = hessen.shape[0]
     depth = hessen.shape[2]
@@ -432,7 +535,9 @@
     )
     panel_maps = -all_sum(jnp.dot(selector.T, gain_panel, precision=highest), ("blk",), mesh_shape, 1)
 
-    chain = scan_maps(panel_maps.T, mesh_shape["sec"])
+    chain = scan_maps(panel_maps, mesh_shape["sec"])
+    own_piece = panel_width // mesh_shape["blk"]
+    own_picks = lax.dynamic_slice_in_dim(selector, lax.axis_index("blk") * own_piece, own_piece, 1).T
 
     def section_terms(dense_part, behind_vals, piece):
         width = piece.shape[1]
@@ -494,18 +599,11 @@
     hessen = jnp.zeros((cases, KRYLOV + 1, KRYLOV), jnp.float32)
     for column in range(KRYLOV):
         precondition_rounded = basis[column].astype(jnp.bfloat16)
-        precondition_folded = lax.dot_general(
-            gather_blk(precondition_rounded, mesh_shape["blk"]),
-            block_inverse,
-            contract,
-            preferred_element_type=jnp.float32,
-        )
-        values = all_sum(
-            jnp.dot(precondition_folded, selector, precision=highest), ("blk",), mesh_shape, 1
-        )
-        before = sweep(values, chain, mesh_shape["sec"])
+        precondition_folded, before_t = precondition_sweep(
+            precondition_rounded, block_inverse, own_picks, chain, mesh_shape["sec"], mesh_shape["blk"]
+        )
         direction = precondition_folded - lax.dot_general(
-            before, gain_panel, contract, precision=highest
+            before_t, gain_panel, (((0,), (1,)), ((), ())), precision=highest
         )
         product = operator(direction) + jac_diag * direction
         stacked = jnp.stack(basis)

time: 467 us -> 429 us (0.919)
  Pallas kernels: 388 us -> 357 us
  matrix products: 30.7 us -> 22.6 us
    pallas_call x11 -> x8, Pallas kernels: 169 us -> 133 us  [all_sum(): pl.pallas_call(functools.partial(_reduce_kernel, stages), out_shape=jax.S...]
    dot_general x9 -> x3, matrix products: 10.7 us -> 3.94 us  [local(): lax.dot_general(before_t, gain_panel, (((0,), (1,)), ((), ())), precision...]
    pallas_call x6 -> x3, Pallas kernels: 120 us -> 122 us  [precondition_sweep(): pl.pallas_call(functools.partial(_precondition_kernel, n_sec, n_blk, dist...]
where the time goes in v5:
time: 429 us; the launch traced here: 427 us
  Pallas kernels  357 us (83%)
  matrix products  22.6 us (5%)
  other arithmetic  20 us (5%)
  blocking collectives  14 us (3%)
  local copies, waits for them, and re-layouts  13.2 us (3%)
    pallas_call x8, Pallas kernels, all_sum(): pl.pallas_call(functools.partial(_reduce_kernel, stages), out_shape=jax.S...  133 us
    pallas_call x3, Pallas kernels, precondition_sweep(): pl.pallas_call(functools.partial(_precondition_kernel, n_sec, n_blk, dist...  122 us
    pallas_call x4, Pallas kernels, operator_exchange(): pl.pallas_call(functools.partial(_operator_kernel, n_sec, n_blk), out_sha...  83.4 us
    pallas_call x1, Pallas kernels, scan_maps(): pl.pallas_call(functools.partial(_maps_kernel, n, distances), out_shape=j...  18.1 us
    all_gather x1, blocking collectives, local(): lax.all_gather(back_panel, 'blk', axis=0, tiled=True)  14 us

profile of v5, /device:TPU:1, one launch (start us, length us, event | category | flops | bytes accessed | tf_op | source)
XLA Modules:
  0.0 427.0 jit_solution(714777180155698547)
XLA Ops:
  2.7 22.0 %shard_map.82 = (bf16[128,2048]{1,0:T(8,128)(2,1)}, f32[128,128]{1,0:T(8,128)}, f32[16,128]{1,0:T(8,128)}) custom-call(bf16[128,256]{1,0:T(8,128)(2,1)} %copy-done.5, f32[128,128]{1,0:T(8,128)} %fusion.72.up_ref, f32[128,128]{1,0:T(8,128)} %fusion.20.be_ref), custom_call_target="tpu_custom_call" | custom-call | tf_op jit(solution)/shard_map/pallas_call | solution.py:368
  27.4 1.7 multiply_reduce_fusion.8
  29.7 17.1 %shard_map.83 = f32[8,128]{1,0:T(8,128)} custom-call(f32[8,128]{1,0:T(8,128)} %scatter.50.x_ref), custom_call_target="tpu_custom_call" | custom-call | tf_op jit(solution)/shard_map/pallas_call | solution.py:106
  48.9 14.0 %all_gather.3 = bf16[2048,128]{1,0:T(8,128)(2,1)S(1)} all-gather(bf16[256,128]{1,0:T(8,128)(2,1)S(1)} %copy-done.3), channel_id=1, replica_groups=mesh['sec'=32,'blk'=8] {'blk'}, dimensions={0}, use_global_device_ids=true | all-gather | bytes 589824 | tf_op jit(solution)/shard_map/all_gather | solution.py:533
  64.2 11.3 %shard_map.84 = f32[128,128]{1,0:T(8,128)} custom-call(f32[128,128]{1,0:T(8,128)} %fusion.9.x_ref), custom_call_target="tpu_custom_call" | custom-call | tf_op jit(solution)/shard_map/pallas_call | solution.py:106
  77.0 18.1 %shard_map.85.u_ref = f32[5,128,128]{2,1,0:T(8,128)} custom-call(f32[128,128]{1,0:T(8,128)} %neg.25.e_ref), custom_call_target="tpu_custom_call" | custom-call | tf_op jit(solution)/shard_map/pallas_call | solution.py:184
  95.0 42.6 %shard_map.86 = (f32[128,256]{1,0:T(8,128)}, f32[128,128]{1,0:T(8,128)}) custom-call(bf16[128,256]{1,0:T(8,128)(2,1)} %fusion.64.x_ref, bf16[256,2048]{1,0:T(8,128)(2,1)} %inv_ref.5, f32[16,256]{1,0:T(8,128)} %dynamic-slice_bitcast_fusion.pick_ref, f32[5,128,128]{2,1,0:T(8,128)} %shard_map.85.u_ref), custom_call_target="tpu_custom_call" | custom-call | tf_op jit(solution)/shard_map/pallas_call | solution.py:470
  140.6 17.9 %shard_map.87 = (bf16[128,2048]{1,0:T(8,128)(2,1)}, f32[128,128]{1,0:T(8,128)}, f32[16,128]{1,0:T(8,128)}) custom-call(bf16[128,256]{1,0:T(8,128)(2,1)} %copy-done.7, f32[128,128]{1,0:T(8,128)} %convolution_bitcast_fusion.2.up_ref, f32[128,128]{1,0:T(8,128)} %fusion.18.be_ref), custom_call_target="tpu_custom_call" | custom-call | tf_op jit(solution)/shard_map/pallas_call | solution.py:368
  159.8 1.5 fusion.5
  162.1 19.0 %shard_map.88 = f32[8,128]{1,0:T(8,128)} custom-call(f32[8,128]{1,0:T(8,128)} %scatter.51.x_ref), custom_call_target="tpu_custom_call" | custom-call | tf_op jit(solution)/shard_map/pallas_call | solution.py:106
  182.6 15.9 %shard_map.89 = f32[8,128]{1,0:T(8,128)} custom-call(f32[8,128]{1,0:T(8,128)} %scatter.55.x_ref), custom_call_target="tpu_custom_call" | custom-call | tf_op jit(solution)/shard_map/pallas_call | solution.py:106
  200.0 40.8 %shard_map.90 = (f32[128,256]{1,0:T(8,128)}, f32[128,128]{1,0:T(8,128)}) custom-call(bf16[128,256]{1,0:T(8,128)(2,1)} %get-tuple-element.408.x_ref, bf16[256,2048]{1,0:T(8,128)(2,1)} %inv_ref.5, f32[16,256]{1,0:T(8,128)} %dynamic-slice_bitcast_fusion.pick_ref, f32[5,128,128]{2,1,0:T(8,128)} %shard_map.85.u_ref), custom_call_target="tpu_custom_call" | custom-call | tf_op jit(solution)/shard_map/pallas_call | solution.py:470
  243.7 21.8 %shard_map.91 = (bf16[128,2048]{1,0:T(8,128)(2,1)}, f32[128,128]{1,0:T(8,128)}, f32[16,128]{1,0:T(8,128)}) custom-call(bf16[128,256]{1,0:T(8,128)(2,1)} %copy-done.8, f32[128,128]{1,0:T(8,128)} %convolution_bitcast_fusion.1.up_ref, f32[128,128]{1,0:T(8,128)} %fusion.16.be_ref), custom_call_target="tpu_custom_call" | custom-call | tf_op jit(solution)/shard_map/pallas_call | solution.py:368
  266.9 1.5 fusion.3
  269.1 16.8 %shard_map.92 = f32[8,128]{1,0:T(8,128)} custom-call(f32[8,128]{1,0:T(8,128)} %scatter.59.x_ref), custom_call_target="tpu_custom_call" | custom-call | tf_op jit(solution)/shard_map/pallas_call | solution.py:106
  287.4 17.8 %shard_map.93 = f32[8,128]{1,0:T(8,128)} custom-call(f32[8,128]{1,0:T(8,128)} %scatter.61.x_ref), custom_call_target="tpu_custom_call" | custom-call | tf_op jit(solution)/shard_map/pallas_call | solution.py:106
  306.7 39.1 %shard_map.94 = (f32[128,256]{1,0:T(8,128)}, f32[128,128]{1,0:T(8,128)}) custom-call(bf16[128,256]{1,0:T(8,128)(2,1)} %get-tuple-element.404.x_ref, bf16[256,2048]{1,0:T(8,128)(2,1)} %inv_ref.5, f32[16,256]{1,0:T(8,128)} %dynamic-slice_bitcast_fusion.pick_ref, f32[5,128,128]{2,1,0:T(8,128)} %shard_map.85.u_ref), custom_call_target="tpu_custom_call" | custom-call | tf_op jit(solution)/shard_map/pallas_call | solution.py:470
  348.9 21.7 %shard_map.95 = (bf16[128,2048]{1,0:T(8,128)(2,1)}, f32[128,128]{1,0:T(8,128)}, f32[16,128]{1,0:T(8,128)}) custom-call(bf16[128,256]{1,0:T(8,128)(2,1)} %copy-done.6, f32[128,128]{1,0:T(8,128)} %convolution_bitcast_fusion.up_ref, f32[128,128]{1,0:T(8,128)} %fusion.14.be_ref), custom_call_target="tpu_custom_call" | custom-call | tf_op jit(solution)/shard_map/pallas_call | solution.py:368
  371.9 1.5 fusion.1
  374.2 16.3 %shard_map.96 = f32[8,128]{1,0:T(8,128)} custom-call(f32[8,128]{1,0:T(8,128)} %scatter.65.x_ref), custom_call_target="tpu_custom_call" | custom-call | tf_op jit(solution)/shard_map/pallas_call | solution.py:106
  392.0 18.4 %shard_map.97 = f32[8,128]{1,0:T(8,128)} custom-call(f32[8,128]{1,0:T(8,128)} %scatter.69.x_ref), custom_call_target="tpu_custom_call" | custom-call | tf_op jit(solution)/shard_map/pallas_call | solution.py:106
  414.6 2.0 bitcast_select_fusion
  420.9 3.3 broadcast_select_fusion
  424.3 1.9 fusion.46
  (122 shorter events, 42.4 us)
Async XLA Ops:
  0.0 26.7 %copy-start = (bf16[256,2048]{1,0:T(8,128)(2,1)S(1)}, bf16[256,2048]{1,0:T(8,128)(2,1)}, u32[]{:S(2)}) copy-start(bf16[256,2048]{1,0:T(8,128)(2,1)} %param.69) | copy-start | bytes 3145732
  0.0 1.0 copy-start.11
  1.0 0.9 copy-start.5
  1.0 0.9 copy-start.4
  24.9 0.7 copy-start.14
  25.6 0.8 copy-start.3
  25.6 0.9 copy-start.10
  26.4 0.9 copy-start.2
  26.5 1.0 copy-start.9
  26.6 0.8 copy-start.12
  27.4 35.5 %copy-start.1 = (bf16[256,2048]{1,0:T(8,128)(2,1)S(1)}, bf16[256,2048]{1,0:T(8,128)(2,1)}, u32[]{:S(2)}) copy-start(bf16[256,2048]{1,0:T(8,128)(2,1)} %inv_ref.5) | copy-start | bytes 3145732
  138.9 0.8 copy-start.7
  158.5 1.0 copy-start.16
  242.0 0.8 copy-start.8
  265.5 1.0 copy-start.17
  347.2 0.8 copy-start.6
  370.6 1.0 copy-start.15
  390.5 0.7 slice-start
  413.8 0.8 copy-start.13

commit v6 on v5

--- a/solution.py
+++ b/solution.py
@@ -151,66 +151,79 @@
     copy.wait_send()
 
 
-def _maps_kernel(n, distances, e_ref, t_ref, slots, sends, recvs):
-    mine = lax.axis_index("sec")
-    _greet(n, distances)
-    t_ref[0] = e_ref[...]
-    for k, d in enumerate(distances[:-1]):
-        _hop(n, d, t_ref.at[k], slots.at[k], sends.at[k], recvs.at[k])
-        joined = jnp.dot(
-            t_ref[k], slots[k], precision=lax.Precision.HIGHEST, preferred_element_type=jnp.float32
-        )
-        t_ref[k + 1] = jnp.where(mine >= d, joined, t_ref[k])
-
-
-def _sweep_kernel(n, distances, f_ref, t_ref, o_ref, carry, slots, sends, recvs):
-    mine = lax.axis_index("sec")
-    _greet(n, distances)
-    carry[0] = f_ref[...]
-    for k, d in enumerate(distances):
-        _hop(n, d, carry.at[k], slots.at[k], sends.at[k], recvs.at[k])
-        joined = carry[k] + jnp.dot(
-            slots[k], t_ref[k], precision=lax.Precision.HIGHEST, preferred_element_type=jnp.float32
-        )
-        carry[k + 1] = jnp.where(mine >= d, joined, carry[k])
-    last = len(distances)
-    _hop(n, 1, carry.at[last], slots.at[last], sends.at[last], recvs.at[last])
-    o_ref[...] = jnp.where(mine >= 1, slots[last], jnp.zeros_like(o_ref))
-
-
-def scan_maps(maps_t, n):
-    distances = _doubling(n)
-    rounds, width = len(distances), maps_t.shape[0]
+RADIX = 4
+
+
+def _plan(n):
+    rounds, d = [], 1
+    while d < n:
+        rounds.append((d, tuple(j for j in range(1, RADIX) if j * d < n)))
+        d *= RADIX
+    return tuple(rounds)
+
+
+def _plan_peers(rounds):
+    return tuple(sorted({j * d for d, js in rounds for j in js} | {1}))
+
+
+def _send_all(n, sec, sources, slots, sends, recvs, flat, d, js):
+    copies = []
+    for i, j in enumerate(js):
+        copy = pltpu.make_async_remote_copy(
+            src_ref=sources,
+            dst_ref=slots.at[flat + i],
+            send_sem=sends.at[flat + i],
+            recv_sem=recvs.at[flat + i],
+            device_id={"sec": lax.rem(sec + j * d, n)},
+            device_id_type=MESH,
+        )
+        copy.start()
+        copies.append(copy)
+    for copy in copies:
+        copy.wait_recv()
+    for copy in copies:
+        copy.wait_send()
+
+
+def _maps_kernel(n, rounds, e_ref, a_ref, current, slots, sends, recvs):
+    sec = lax.axis_index("sec")
+    _greet(n, _plan_peers(rounds))
+    current[...] = e_ref[...]
+    flat = 0
+    for k, (d, js) in enumerate(rounds):
+        onward = k < len(rounds) - 1
+        if onward or len(js) > 1:
+            _send_all(n, sec, current, slots, sends, recvs, flat, d, js)
+        joined = current[...]
+        for i, j in enumerate(js):
+            a_ref[flat + i] = joined
+            if onward or i < len(js) - 1:
+                joined = jnp.dot(
+                    joined, slots[flat + i], precision=lax.Precision.HIGHEST,
+                    preferred_element_type=jnp.float32,
+                )
+        if onward:
+            current[...] = joined
+        flat += len(js)
+
+
+def scan_maps(maps, n):
+    rounds = _plan(n)
+    total = sum(len(js) for _, js in rounds)
+    width = maps.shape[0]
     return pl.pallas_call(
-        functools.partial(_maps_kernel, n, distances),
-        out_shape=jax.ShapeDtypeStruct((rounds, width, width), jnp.float32),
+        functools.partial(_maps_kernel, n, rounds),
+        out_shape=jax.ShapeDtypeStruct((total, width, width), jnp.float32),
         in_specs=[pl.BlockSpec(memory_space=pltpu.VMEM)],
         out_specs=pl.BlockSpec(memory_space=pltpu.VMEM),
         scratch_shapes=[
-            pltpu.VMEM((rounds, width, width), jnp.float32),
-            pltpu.SemaphoreType.DMA((rounds,)),
-            pltpu.SemaphoreType.DMA((rounds,)),
+            pltpu.VMEM((width, width), jnp.float32),
+            pltpu.VMEM((total, width, width), jnp.float32),
+            pltpu.SemaphoreType.DMA((total,)),
+            pltpu.SemaphoreType.DMA((total,)),
         ],
         compiler_params=pltpu.CompilerParams(collective_id=2, has_side_effects=True),
-    )(maps_t)
-
-
-def sweep(values, chain, n):
-    distances = _doubling(n)
-    rounds = len(distances)
-    return pl.pallas_call(
-        functools.partial(_sweep_kernel, n, distances),
-        out_shape=jax.ShapeDtypeStruct(values.shape, jnp.float32),
-        in_specs=[pl.BlockSpec(memory_space=pltpu.VMEM)] * 2,
-        out_specs=pl.BlockSpec(memory_space=pltpu.VMEM),
-        scratch_shapes=[
-            pltpu.VMEM((rounds + 1,) + values.shape, jnp.float32),
-            pltpu.VMEM((rounds + 1,) + values.shape, jnp.float32),
-            pltpu.SemaphoreType.DMA((rounds + 1,)),
-            pltpu.SemaphoreType.DMA((rounds + 1,)),
-        ],
-        compiler_params=pltpu.CompilerParams(collective_id=3, has_side_effects=True),
-    )(values, chain)
+    )(maps)
 
 
 def _gather_kernel(n, x_ref, o_ref, slots, sends, recvs):
@@ -384,7 +397,7 @@
     )(x, up_t, be_t)
 
 
-def _precondition_kernel(n_sec, n_blk, distances, x_ref, inv_ref, pick_ref, u_ref, w_ref, o_ref, *scratch):
+def _precondition_kernel(n_sec, n_blk, rounds, x_ref, inv_ref, pick_ref, u_ref, w_ref, o_ref, *scratch):
     gslots, fslots, carry, slots, gsend, grecv, fsend, frecv, ssend, srecv = scratch
     sec, blk = lax.axis_index("sec"), lax.axis_index("blk")
     barrier = pltpu.get_barrier_semaphore()
@@ -392,6 +405,7 @@
         pl.semaphore_signal(
             barrier, inc=1, device_id={"blk": lax.rem(blk + k, n_blk)}, device_id_type=MESH
         )
+    distances = _plan_peers(rounds)
     for d in distances:
         for peer in (lax.rem(sec + d, n_sec), lax.rem(sec + n_sec - d, n_sec)):
             pl.semaphore_signal(barrier, inc=1, device_id={"sec": peer}, device_id_type=MESH)
@@ -450,25 +464,32 @@
     piece = fslots.shape[1]
     for j in range(n_blk):
         carry[0, j * piece : (j + 1) * piece, :] = fslots[j]
-    for k, d in enumerate(distances):
-        _hop(n_sec, d, carry.at[k], slots.at[k], ssend.at[k], srecv.at[k])
-        joined = carry[k] + jnp.dot(
-            u_ref[k], slots[k], precision=lax.Precision.HIGHEST, preferred_element_type=jnp.float32
-        )
-        carry[k + 1] = jnp.where(sec >= d, joined, carry[k])
-    last = len(distances)
-    _hop(n_sec, 1, carry.at[last], slots.at[last], ssend.at[last], srecv.at[last])
-    o_ref[...] = jnp.where(sec >= 1, slots[last], jnp.zeros_like(o_ref))
+    flat = 0
+    for k, (d, js) in enumerate(rounds):
+        _send_all(n_sec, sec, carry.at[k], slots, ssend, srecv, flat, d, js)
+        joined = carry[k]
+        for i, j in enumerate(js):
+            term = jnp.dot(
+                u_ref[flat + i], slots[flat + i], precision=lax.Precision.HIGHEST,
+                preferred_element_type=jnp.float32,
+            )
+            joined = joined + jnp.where(sec >= j * d, term, jnp.zeros_like(term))
+        carry[k + 1] = joined
+        flat += len(js)
+    last = len(rounds)
+    _hop(n_sec, 1, carry.at[last], slots.at[flat], ssend.at[flat], srecv.at[flat])
+    o_ref[...] = jnp.where(sec >= 1, slots[flat], jnp.zeros_like(o_ref))
 
 
 def precondition_sweep(x, inverse, picks, chain, n_sec, n_blk):
     cases, width = x.shape
     piece, _ = picks.shape
     panel = piece * n_blk
-    distances = _doubling(n_sec)
-    rounds = len(distances)
+    plan = _plan(n_sec)
+    rounds = len(plan)
+    total = sum(len(js) for _, js in plan) + 1
     return pl.pallas_call(
-        functools.partial(_precondition_kernel, n_sec, n_blk, distances),
+        functools.partial(_precondition_kernel, n_sec, n_blk, plan),
         out_shape=(
             jax.ShapeDtypeStruct((cases, width), jnp.float32),
             jax.ShapeDtypeStruct((panel, cases), jnp.float32),
@@ -479,10 +500,10 @@
             pltpu.VMEM((n_blk, cases, width), x.dtype),
             pltpu.VMEM((n_blk, piece, cases), jnp.float32),
             pltpu.VMEM((rounds + 1, panel, cases), jnp.float32),
-            pltpu.VMEM((rounds + 1, panel, cases), jnp.float32),
+            pltpu.VMEM((total, panel, cases), jnp.float32),
         ]
         + [pltpu.SemaphoreType.DMA((n_blk,))] * 4
-        + [pltpu.SemaphoreType.DMA((rounds + 1,))] * 2,
+        + [pltpu.SemaphoreType.DMA((total,))] * 2,
         compiler_params=pltpu.CompilerParams(collective_id=6, has_side_effects=True),
     )(x, inverse, picks, chain)
 

time: 429 us -> 431 us (level)
    pallas_call x4, Pallas kernels: 140 us -> 150 us  [the longest x3 132 us: precondition_sweep(): pl.pallas_call(functools.partial(_precondition_kernel, n_sec, n_blk, plan...]
    pallas_call x4, Pallas kernels: 83.4 us -> 74.2 us  [operator_exchange(): pl.pallas_call(functools.partial(_operator_kernel, n_sec, n_blk), out_sha...]
where the time goes in v6:
time: 431 us; the launch traced here: 429 us
  Pallas kernels  359 us (83%)
  matrix products  22.4 us (5%)
  other arithmetic  20 us (5%)
  blocking collectives  14 us (3%)
  local copies, waits for them, and re-layouts  13.2 us (3%)
    pallas_call x8, Pallas kernels, all_sum(): pl.pallas_call(functools.partial(_reduce_kernel, stages), out_shape=jax.S...  135 us
    pallas_call x3, Pallas kernels, precondition_sweep(): pl.pallas_call(functools.partial(_precondition_kernel, n_sec, n_blk, plan...  132 us
    pallas_call x4, Pallas kernels, operator_exchange(): pl.pallas_call(functools.partial(_operator_kernel, n_sec, n_blk), out_sha...  74.2 us
    pallas_call x1, Pallas kernels, scan_maps(): pl.pallas_call(functools.partial(_maps_kernel, n, rounds), out_shape=jax....  17.9 us
    all_gather x1, blocking collectives, local(): lax.all_gather(back_panel, 'blk', axis=0, tiled=True)  14 us

profile of v6, /device:TPU:1, one launch (start us, length us, event | category | flops | bytes accessed | tf_op | source)
XLA Modules:
  0.0 428.9 jit_solution(14200153613711208532)
XLA Ops:
  2.7 22.0 %shard_map.82 = (bf16[128,2048]{1,0:T(8,128)(2,1)}, f32[128,128]{1,0:T(8,128)}, f32[16,128]{1,0:T(8,128)}) custom-call(bf16[128,256]{1,0:T(8,128)(2,1)} %copy-done.5, f32[128,128]{1,0:T(8,128)} %fusion.72.up_ref, f32[128,128]{1,0:T(8,128)} %fusion.20.be_ref), custom_call_target="tpu_custom_call" | custom-call | tf_op jit(solution)/shard_map/pallas_call | solution.py:381
  27.4 1.7 multiply_reduce_fusion.8
  29.7 17.1 %shard_map.83 = f32[8,128]{1,0:T(8,128)} custom-call(f32[8,128]{1,0:T(8,128)} %scatter.50.x_ref), custom_call_target="tpu_custom_call" | custom-call | tf_op jit(solution)/shard_map/pallas_call | solution.py:106
  48.9 14.0 %all_gather.3 = bf16[2048,128]{1,0:T(8,128)(2,1)S(1)} all-gather(bf16[256,128]{1,0:T(8,128)(2,1)S(1)} %copy-done.3), channel_id=1, replica_groups=mesh['sec'=32,'blk'=8] {'blk'}, dimensions={0}, use_global_device_ids=true | all-gather | bytes 589824 | tf_op jit(solution)/shard_map/all_gather | solution.py:554
  64.2 11.3 %shard_map.84 = f32[128,128]{1,0:T(8,128)} custom-call(f32[128,128]{1,0:T(8,128)} %fusion.9.x_ref), custom_call_target="tpu_custom_call" | custom-call | tf_op jit(solution)/shard_map/pallas_call | solution.py:106
  77.0 17.9 %shard_map.85.u_ref = f32[7,128,128]{2,1,0:T(8,128)} custom-call(f32[128,128]{1,0:T(8,128)} %neg.25.e_ref), custom_call_target="tpu_custom_call" | custom-call | tf_op jit(solution)/shard_map/pallas_call | solution.py:214
  94.8 46.2 %shard_map.86 = (f32[128,256]{1,0:T(8,128)}, f32[128,128]{1,0:T(8,128)}) custom-call(bf16[128,256]{1,0:T(8,128)(2,1)} %fusion.64.x_ref, bf16[256,2048]{1,0:T(8,128)(2,1)} %inv_ref.5, f32[16,256]{1,0:T(8,128)} %dynamic-slice_bitcast_fusion.pick_ref, f32[7,128,128]{2,1,0:T(8,128)} %shard_map.85.u_ref), custom_call_target="tpu_custom_call" | custom-call | tf_op jit(solution)/shard_map/pallas_call | solution.py:491
  144.0 16.7 %shard_map.87 = (bf16[128,2048]{1,0:T(8,128)(2,1)}, f32[128,128]{1,0:T(8,128)}, f32[16,128]{1,0:T(8,128)}) custom-call(bf16[128,256]{1,0:T(8,128)(2,1)} %copy-done.7, f32[128,128]{1,0:T(8,128)} %convolution_bitcast_fusion.2.up_ref, f32[128,128]{1,0:T(8,128)} %fusion.18.be_ref), custom_call_target="tpu_custom_call" | custom-call | tf_op jit(solution)/shard_map/pallas_call | solution.py:381
  162.1 1.5 fusion.5
  164.4 18.1 %shard_map.88 = f32[8,128]{1,0:T(8,128)} custom-call(f32[8,128]{1,0:T(8,128)} %scatter.51.x_ref), custom_call_target="tpu_custom_call" | custom-call | tf_op jit(solution)/shard_map/pallas_call | solution.py:106
  184.0 17.5 %shard_map.89 = f32[8,128]{1,0:T(8,128)} custom-call(f32[8,128]{1,0:T(8,128)} %scatter.55.x_ref), custom_call_target="tpu_custom_call" | custom-call | tf_op jit(solution)/shard_map/pallas_call | solution.py:106
  202.9 43.7 %shard_map.90 = (f32[128,256]{1,0:T(8,128)}, f32[128,128]{1,0:T(8,128)}) custom-call(bf16[128,256]{1,0:T(8,128)(2,1)} %get-tuple-element.408.x_ref, bf16[256,2048]{1,0:T(8,128)(2,1)} %inv_ref.5, f32[16,256]{1,0:T(8,128)} %dynamic-slice_bitcast_fusion.pick_ref, f32[7,128,128]{2,1,0:T(8,128)} %shard_map.85.u_ref), custom_call_target="tpu_custom_call" | custom-call | tf_op jit(solution)/shard_map/pallas_call | solution.py:491
  249.5 16.2 %shard_map.91 = (bf16[128,2048]{1,0:T(8,128)(2,1)}, f32[128,128]{1,0:T(8,128)}, f32[16,128]{1,0:T(8,128)}) custom-call(bf16[128,256]{1,0:T(8,128)(2,1)} %copy-done.8, f32[128,128]{1,0:T(8,128)} %convolution_bitcast_fusion.1.up_ref, f32[128,128]{1,0:T(8,128)} %fusion.16.be_ref), custom_call_target="tpu_custom_call" | custom-call | tf_op jit(solution)/shard_map/pallas_call | solution.py:381
  267.0 1.5 fusion.3
  269.3 20.0 %shard_map.92 = f32[8,128]{1,0:T(8,128)} custom-call(f32[8,128]{1,0:T(8,128)} %scatter.59.x_ref), custom_call_target="tpu_custom_call" | custom-call | tf_op jit(solution)/shard_map/pallas_call | solution.py:106
  290.8 16.2 %shard_map.93 = f32[8,128]{1,0:T(8,128)} custom-call(f32[8,128]{1,0:T(8,128)} %scatter.61.x_ref), custom_call_target="tpu_custom_call" | custom-call | tf_op jit(solution)/shard_map/pallas_call | solution.py:106
  308.5 42.1 %shard_map.94 = (f32[128,256]{1,0:T(8,128)}, f32[128,128]{1,0:T(8,128)}) custom-call(bf16[128,256]{1,0:T(8,128)(2,1)} %get-tuple-element.404.x_ref, bf16[256,2048]{1,0:T(8,128)(2,1)} %inv_ref.5, f32[16,256]{1,0:T(8,128)} %dynamic-slice_bitcast_fusion.pick_ref, f32[7,128,128]{2,1,0:T(8,128)} %shard_map.85.u_ref), custom_call_target="tpu_custom_call" | custom-call | tf_op jit(solution)/shard_map/pallas_call | solution.py:491
  353.5 19.1 %shard_map.95 = (bf16[128,2048]{1,0:T(8,128)(2,1)}, f32[128,128]{1,0:T(8,128)}, f32[16,128]{1,0:T(8,128)}) custom-call(bf16[128,256]{1,0:T(8,128)(2,1)} %copy-done.6, f32[128,128]{1,0:T(8,128)} %convolution_bitcast_fusion.up_ref, f32[128,128]{1,0:T(8,128)} %fusion.14.be_ref), custom_call_target="tpu_custom_call" | custom-call | tf_op jit(solution)/shard_map/pallas_call | solution.py:381
  374.0 1.5 fusion.1
  376.3 17.4 %shard_map.96 = f32[8,128]{1,0:T(8,128)} custom-call(f32[8,128]{1,0:T(8,128)} %scatter.65.x_ref), custom_call_target="tpu_custom_call" | custom-call | tf_op jit(solution)/shard_map/pallas_call | solution.py:106
  395.2 17.1 %shard_map.97 = f32[8,128]{1,0:T(8,128)} custom-call(f32[8,128]{1,0:T(8,128)} %scatter.69.x_ref), custom_call_target="tpu_custom_call" | custom-call | tf_op jit(solution)/shard_map/pallas_call | solution.py:106
  416.5 2.0 bitcast_select_fusion
  422.8 3.3 broadcast_select_fusion
  426.2 1.9 fusion.46
  (122 shorter events, 42.2 us)
Async XLA Ops:
  0.0 26.7 %copy-start = (bf16[256,2048]{1,0:T(8,128)(2,1)S(1)}, bf16[256,2048]{1,0:T(8,128)(2,1)}, u32[]{:S(2)}) copy-start(bf16[256,2048]{1,0:T(8,128)(2,1)} %param.69) | copy-start | bytes 3145732
  0.0 1.0 copy-start.11
  1.0 0.9 copy-start.5
  1.0 0.9 copy-start.4
  24.9 0.7 copy-start.14
  25.6 0.8 copy-start.3
  25.6 0.9 copy-start.10
  26.4 0.9 copy-start.2
  26.5 1.0 copy-start.9
  26.6 0.8 copy-start.12
  27.4 35.5 %copy-start.1 = (bf16[256,2048]{1,0:T(8,128)(2,1)S(1)}, bf16[256,2048]{1,0:T(8,128)(2,1)}, u32[]{:S(2)}) copy-start(bf16[256,2048]{1,0:T(8,128)(2,1)} %inv_ref.5) | copy-start | bytes 3145732
  142.3 0.8 copy-start.7
  160.7 1.0 copy-start.16
  247.8 0.8 copy-start.8
  265.7 1.0 copy-start.17
  351.8 0.8 copy-start.6
  372.6 1.0 copy-start.15
  393.7 0.7 slice-start
  415.7 0.8 copy-start.13

commit v7 on v6

--- a/solution.py
+++ b/solution.py
@@ -185,12 +185,79 @@
         copy.wait_send()
 
 
-def _maps_kernel(n, rounds, e_ref, a_ref, current, slots, sends, recvs):
+def _spread(n_sec, n_blk, offsets, piece_ref, slots, sends, recvs):
+    sec, blk = lax.axis_index("sec"), lax.axis_index("blk")
+
+    def copy(o, j, index):
+        return pltpu.make_async_remote_copy(
+            src_ref=piece_ref,
+            dst_ref=slots.at[index],
+            send_sem=sends.at[(o - 1) * n_blk + j],
+            recv_sem=recvs.at[index],
+            device_id={"sec": lax.rem(sec + o, n_sec), "blk": j},
+            device_id_type=MESH,
+        )
+
+    outgoing = [
+        copy(o, j, (o - 1) * n_blk + blk) for o in range(1, offsets + 1) for j in range(n_blk)
+    ]
+    for c in outgoing:
+        c.start()
+    for o in range(1, offsets + 1):
+        for j in range(n_blk):
+            copy(o, j, (o - 1) * n_blk + j).wait_recv()
+    for c in outgoing:
+        c.wait_send()
+
+
+def _assemble(n_blk, offsets, slots, mats):
+    piece = slots.shape[1]
+    for o in range(offsets):
+        for j in range(n_blk):
+            mats[o, j * piece : (j + 1) * piece, :] = slots[o * n_blk + j]
+
+
+def _greet_all(n_sec, n_blk, offsets, rounds, blk_peers):
+    barrier = pltpu.get_barrier_semaphore()
+    sec, blk = lax.axis_index("sec"), lax.axis_index("blk")
+    count = 0
+    if blk_peers:
+        for k in range(1, n_blk):
+            pl.semaphore_signal(
+                barrier, inc=1, device_id={"blk": lax.rem(blk + k, n_blk)}, device_id_type=MESH
+            )
+            count += 1
+    for o in range(1, offsets + 1):
+        for j in range(n_blk):
+            for peer in (lax.rem(sec + o, n_sec), lax.rem(sec + n_sec - o, n_sec)):
+                pl.semaphore_signal(
+                    barrier, inc=1, device_id={"sec": peer, "blk": j}, device_id_type=MESH
+                )
+                count += 1
+    for d in sorted({j * d for d, js in rounds[1:] for j in js}):
+        for peer in (lax.rem(sec + d, n_sec), lax.rem(sec + n_sec - d, n_sec)):
+            pl.semaphore_signal(barrier, inc=1, device_id={"sec": peer}, device_id_type=MESH)
+            count += 1
+    pl.semaphore_wait(barrier, count)
+
+
+def _maps_kernel(n, n_blk, rounds, e_ref, a_ref, eslots, emat, current, slots, esend, erecv, sends, recvs):
     sec = lax.axis_index("sec")
-    _greet(n, _plan_peers(rounds))
-    current[...] = e_ref[...]
-    flat = 0
-    for k, (d, js) in enumerate(rounds):
+    first = rounds[0][1]
+    offsets = len(first) + 1
+    _greet_all(n, n_blk, offsets, rounds, False)
+    _spread(n, n_blk, offsets, e_ref, eslots, esend, erecv)
+    _assemble(n_blk, offsets, eslots, emat)
+    joined = emat[0]
+    for i, j in enumerate(first):
+        a_ref[i] = joined
+        joined = jnp.dot(
+            joined, emat[j], precision=lax.Precision.HIGHEST, preferred_element_type=jnp.float32
+        )
+    current[...] = joined
+    flat = len(first)
+    for k in range(1, len(rounds)):
+        d, js = rounds[k]
         onward = k < len(rounds) - 1
         if onward or len(js) > 1:
             _send_all(n, sec, current, slots, sends, recvs, flat, d, js)
@@ -207,23 +274,28 @@
         flat += len(js)
 
 
-def scan_maps(maps, n):
+def scan_maps(e_piece, n, n_blk):
     rounds = _plan(n)
     total = sum(len(js) for _, js in rounds)
-    width = maps.shape[0]
+    offsets = len(rounds[0][1]) + 1
+    piece, width = e_piece.shape
     return pl.pallas_call(
-        functools.partial(_maps_kernel, n, rounds),
+        functools.partial(_maps_kernel, n, n_blk, rounds),
         out_shape=jax.ShapeDtypeStruct((total, width, width), jnp.float32),
         in_specs=[pl.BlockSpec(memory_space=pltpu.VMEM)],
         out_specs=pl.BlockSpec(memory_space=pltpu.VMEM),
         scratch_shapes=[
+            pltpu.VMEM((offsets * n_blk, piece, width), jnp.float32),
+            pltpu.VMEM((offsets, width, width), jnp.float32),
             pltpu.VMEM((width, width), jnp.float32),
             pltpu.VMEM((total, width, width), jnp.float32),
+            pltpu.SemaphoreType.DMA((offsets * n_blk,)),
+            pltpu.SemaphoreType.DMA((offsets * n_blk,)),
             pltpu.SemaphoreType.DMA((total,)),
             pltpu.SemaphoreType.DMA((total,)),
         ],
         compiler_params=pltpu.CompilerParams(collective_id=2, has_side_effects=True),
-    )(maps)
+    )(e_piece)
 
 
 def _gather_kernel(n, x_ref, o_ref, slots, sends, recvs):
@@ -398,39 +470,29 @@
 
 
 def _precondition_kernel(n_sec, n_blk, rounds, x_ref, inv_ref, pick_ref, u_ref, w_ref, o_ref, *scratch):
-    gslots, fslots, carry, slots, gsend, grecv, fsend, frecv, ssend, srecv = scratch
+    gslots, fpiece, fslots, fmat, carry, slots, gsend, grecv, fsend, frecv, ssend, srecv = scratch
     sec, blk = lax.axis_index("sec"), lax.axis_index("blk")
-    barrier = pltpu.get_barrier_semaphore()
-    for k in range(1, n_blk):
-        pl.semaphore_signal(
-            barrier, inc=1, device_id={"blk": lax.rem(blk + k, n_blk)}, device_id_type=MESH
-        )
-    distances = _plan_peers(rounds)
-    for d in distances:
-        for peer in (lax.rem(sec + d, n_sec), lax.rem(sec + n_sec - d, n_sec)):
-            pl.semaphore_signal(barrier, inc=1, device_id={"sec": peer}, device_id_type=MESH)
-    pl.semaphore_wait(barrier, n_blk - 1 + 2 * len(distances))
-
-    def blk_copy(source, slot_ref, send, recv, k, target):
+    first = rounds[0][1]
+    offsets = len(first) + 1
+    _greet_all(n_sec, n_blk, offsets, rounds, True)
+
+    def blk_copy(k, target, slot):
         return pltpu.make_async_remote_copy(
-            src_ref=source,
-            dst_ref=slot_ref.at[target[1]],
-            send_sem=send.at[k],
-            recv_sem=recv.at[target[1]],
-            device_id={"blk": target[0]},
+            src_ref=x_ref,
+            dst_ref=gslots.at[slot],
+            send_sem=gsend.at[k],
+            recv_sem=grecv.at[slot],
+            device_id={"blk": target},
             device_id_type=MESH,
         )
 
-    outgoing = [
-        blk_copy(x_ref, gslots, gsend, grecv, k, (lax.rem(blk + k, n_blk), blk))
-        for k in range(1, n_blk)
-    ]
+    outgoing = [blk_copy(k, lax.rem(blk + k, n_blk), blk) for k in range(1, n_blk)]
     for copy in outgoing:
         copy.start()
     gslots[blk] = x_ref[...]
     for k in range(1, n_blk):
         sender = lax.rem(blk + k, n_blk)
-        blk_copy(x_ref, gslots, gsend, grecv, k, (sender, sender)).wait_recv()
+        blk_copy(k, sender, sender).wait_recv()
     for copy in outgoing:
         copy.wait_send()
     width = x_ref.shape[1]
@@ -446,26 +508,22 @@
             preferred_element_type=jnp.float32,
         )
     w_ref[...] = folded
-    fslots[blk] = lax.dot_general(
+    fpiece[...] = lax.dot_general(
         pick_ref[...], folded, contract, precision=lax.Precision.HIGHEST,
         preferred_element_type=jnp.float32,
     )
-    outgoing = [
-        blk_copy(fslots.at[blk], fslots, fsend, frecv, k, (lax.rem(blk + k, n_blk), blk))
-        for k in range(1, n_blk)
-    ]
-    for copy in outgoing:
-        copy.start()
-    for k in range(1, n_blk):
-        sender = lax.rem(blk + k, n_blk)
-        blk_copy(fslots.at[blk], fslots, fsend, frecv, k, (sender, sender)).wait_recv()
-    for copy in outgoing:
-        copy.wait_send()
-    piece = fslots.shape[1]
-    for j in range(n_blk):
-        carry[0, j * piece : (j + 1) * piece, :] = fslots[j]
-    flat = 0
-    for k, (d, js) in enumerate(rounds):
+    _spread(n_sec, n_blk, offsets, fpiece, fslots, fsend, frecv)
+    _assemble(n_blk, offsets, fslots, fmat)
+    joined = jnp.where(sec >= 1, fmat[0], jnp.zeros_like(fmat[0]))
+    for i, j in enumerate(first):
+        term = jnp.dot(
+            u_ref[i], fmat[j], precision=lax.Precision.HIGHEST, preferred_element_type=jnp.float32
+        )
+        joined = joined + jnp.where(sec >= j + 1, term, jnp.zeros_like(term))
+    carry[1] = joined
+    flat = len(first)
+    for k in range(1, len(rounds)):
+        d, js = rounds[k]
         _send_all(n_sec, sec, carry.at[k], slots, ssend, srecv, flat, d, js)
         joined = carry[k]
         for i, j in enumerate(js):
@@ -476,9 +534,7 @@
             joined = joined + jnp.where(sec >= j * d, term, jnp.zeros_like(term))
         carry[k + 1] = joined
         flat += len(js)
-    last = len(rounds)
-    _hop(n_sec, 1, carry.at[last], slots.at[flat], ssend.at[flat], srecv.at[flat])
-    o_ref[...] = jnp.where(sec >= 1, slots[flat], jnp.zeros_like(o_ref))
+    o_ref[...] = carry[len(rounds)]
 
 
 def precondition_sweep(x, inverse, picks, chain, n_sec, n_blk):
@@ -487,7 +543,8 @@
     panel = piece * n_blk
     plan = _plan(n_sec)
     rounds = len(plan)
-    total = sum(len(js) for _, js in plan) + 1
+    total = sum(len(js) for _, js in plan)
+    offsets = len(plan[0][1]) + 1
     return pl.pallas_call(
         functools.partial(_precondition_kernel, n_sec, n_blk, plan),
         out_shape=(
@@ -498,12 +555,18 @@
         out_specs=[pl.BlockSpec(memory_space=pltpu.VMEM)] * 2,
         scratch_shapes=[
             pltpu.VMEM((n_blk, cases, width), x.dtype),
-            pltpu.VMEM((n_blk, piece, cases), jnp.float32),
+            pltpu.VMEM((piece, cases), jnp.float32),
+            pltpu.VMEM((offsets * n_blk, piece, cases), jnp.float32),
+            pltpu.VMEM((offsets, panel, cases), jnp.float32),
             pltpu.VMEM((rounds + 1, panel, cases), jnp.float32),
             pltpu.VMEM((total, panel, cases), jnp.float32),
-        ]
-        + [pltpu.SemaphoreType.DMA((n_blk,))] * 4
-        + [pltpu.SemaphoreType.DMA((total,))] * 2,
+            pltpu.SemaphoreType.DMA((n_blk,)),
+            pltpu.SemaphoreType.DMA((n_blk,)),
+            pltpu.SemaphoreType.DMA((offsets * n_blk,)),
+            pltpu.SemaphoreType.DMA((offsets * n_blk,)),
+            pltpu.SemaphoreType.DMA((total,)),
+            pltpu.SemaphoreType.DMA((total,)),
+        ],
         compiler_params=pltpu.CompilerParams(collective_id=6, has_side_effects=True),
     )(x, inverse, picks, chain)
 
@@ -554,11 +617,11 @@
         lax.all_gather(back_panel, "blk", axis=0, tiled=True),
         preferred_element_type=jnp.float32,
     )
-    panel_maps = -all_sum(jnp.dot(selector.T, gain_panel, precision=highest), ("blk",), mesh_shape, 1)
-
-    chain = scan_maps(panel_maps, mesh_shape["sec"])
+
     own_piece = panel_width // mesh_shape["blk"]
     own_picks = lax.dynamic_slice_in_dim(selector, lax.axis_index("blk") * own_piece, own_piece, 1).T
+    own_maps = -jnp.dot(own_picks, gain_panel, precision=highest)
+    chain = scan_maps(own_maps, mesh_shape["sec"], mesh_shape["blk"])
 
     def section_terms(dense_part, behind_vals, piece):
         width = piece.shape[1]

time: 431 us -> 413 us (0.958)
  Pallas kernels: 359 us -> 343 us
    pallas_call x3, Pallas kernels: 132 us -> 116 us  [precondition_sweep(): pl.pallas_call(functools.partial(_precondition_kernel, n_sec, n_blk, plan...]
    pallas_call x8 -> x7, Pallas kernels: 135 us -> 123 us  [all_sum(): pl.pallas_call(functools.partial(_reduce_kernel, stages), out_shape=jax.S...]
    pallas_call x4, Pallas kernels: 74.2 us -> 83.1 us  [operator_exchange(): pl.pallas_call(functools.partial(_operator_kernel, n_sec, n_blk), out_sha...]
where the time goes in v7:
time: 413 us; the launch traced here: 411 us
  Pallas kernels  343 us (83%)
  matrix products  22.3 us (5%)
  other arithmetic  18.6 us (5%)
  blocking collectives  14 us (3%)
  local copies, waits for them, and re-layouts  13.2 us (3%)
    pallas_call x7, Pallas kernels, all_sum(): pl.pallas_call(functools.partial(_reduce_kernel, stages), out_shape=jax.S...  123 us
    pallas_call x3, Pallas kernels, precondition_sweep(): pl.pallas_call(functools.partial(_precondition_kernel, n_sec, n_blk, plan...  116 us
    pallas_call x4, Pallas kernels, operator_exchange(): pl.pallas_call(functools.partial(_operator_kernel, n_sec, n_blk), out_sha...  83.1 us
    pallas_call x1, Pallas kernels, scan_maps(): pl.pallas_call(functools.partial(_maps_kernel, n, n_blk, rounds), out_sha...  20.6 us
    all_gather x1, blocking collectives, local(): lax.all_gather(back_panel, 'blk', axis=0, tiled=True)  14 us

profile of v7, /device:TPU:1, one launch (start us, length us, event | category | flops | bytes accessed | tf_op | source)
XLA Modules:
  0.0 411.3 jit_solution(8261165157672987551)
XLA Ops:
  2.7 22.0 %shard_map.82 = (bf16[128,2048]{1,0:T(8,128)(2,1)}, f32[128,128]{1,0:T(8,128)}, f32[16,128]{1,0:T(8,128)}) custom-call(bf16[128,256]{1,0:T(8,128)(2,1)} %copy-done.5, f32[128,128]{1,0:T(8,128)} %fusion.56.up_ref, f32[128,128]{1,0:T(8,128)} %fusion.12.be_ref), custom_call_target="tpu_custom_call" | custom-call | tf_op jit(solution)/shard_map/pallas_call | solution.py:453
  27.4 1.7 multiply_reduce_fusion.8
  29.7 17.1 %shard_map.83 = f32[8,128]{1,0:T(8,128)} custom-call(f32[8,128]{1,0:T(8,128)} %scatter.50.x_ref), custom_call_target="tpu_custom_call" | custom-call | tf_op jit(solution)/shard_map/pallas_call | solution.py:106
  48.3 14.0 %all_gather.3 = bf16[2048,128]{1,0:T(8,128)(2,1)S(1)} all-gather(bf16[256,128]{1,0:T(8,128)(2,1)S(1)} %copy-done.3), channel_id=1, replica_groups=mesh['sec'=32,'blk'=8] {'blk'}, dimensions={0}, use_global_device_ids=true | all-gather | bytes 589824 | tf_op jit(solution)/shard_map/all_gather | solution.py:617
  63.5 20.6 %shard_map.84.u_ref = f32[7,128,128]{2,1,0:T(8,128)} custom-call(f32[16,128]{1,0:T(8,128)} %convolution_negate_fusion.e_ref), custom_call_target="tpu_custom_call" | custom-call | tf_op jit(solution)/shard_map/pallas_call | solution.py:282
  84.8 43.4 %shard_map.85 = (f32[128,256]{1,0:T(8,128)}, f32[128,128]{1,0:T(8,128)}) custom-call(bf16[128,256]{1,0:T(8,128)(2,1)} %fusion.48.x_ref, bf16[256,2048]{1,0:T(8,128)(2,1)} %inv_ref.5, f32[16,256]{1,0:T(8,128)} %dynamic-slice_bitcast_fusion.pick_ref, f32[7,128,128]{2,1,0:T(8,128)} %shard_map.84.u_ref), custom_call_target="tpu_custom_call" | custom-call | tf_op jit(solution)/shard_map/pallas_call | solution.py:548
  131.2 18.4 %shard_map.86 = (bf16[128,2048]{1,0:T(8,128)(2,1)}, f32[128,128]{1,0:T(8,128)}, f32[16,128]{1,0:T(8,128)}) custom-call(bf16[128,256]{1,0:T(8,128)(2,1)} %copy-done.7, f32[128,128]{1,0:T(8,128)} %convolution_bitcast_fusion.2.up_ref, f32[128,128]{1,0:T(8,128)} %fusion.11.be_ref), custom_call_target="tpu_custom_call" | custom-call | tf_op jit(solution)/shard_map/pallas_call | solution.py:453
  150.9 1.5 fusion.5
  153.3 18.0 %shard_map.87 = f32[8,128]{1,0:T(8,128)} custom-call(f32[8,128]{1,0:T(8,128)} %scatter.51.x_ref), custom_call_target="tpu_custom_call" | custom-call | tf_op jit(solution)/shard_map/pallas_call | solution.py:106
  172.7 17.4 %shard_map.88 = f32[8,128]{1,0:T(8,128)} custom-call(f32[8,128]{1,0:T(8,128)} %scatter.55.x_ref), custom_call_target="tpu_custom_call" | custom-call | tf_op jit(solution)/shard_map/pallas_call | solution.py:106
  191.6 35.9 %shard_map.89 = (f32[128,256]{1,0:T(8,128)}, f32[128,128]{1,0:T(8,128)}) custom-call(bf16[128,256]{1,0:T(8,128)(2,1)} %get-tuple-element.408.x_ref, bf16[256,2048]{1,0:T(8,128)(2,1)} %inv_ref.5, f32[16,256]{1,0:T(8,128)} %dynamic-slice_bitcast_fusion.pick_ref, f32[7,128,128]{2,1,0:T(8,128)} %shard_map.84.u_ref), custom_call_target="tpu_custom_call" | custom-call | tf_op jit(solution)/shard_map/pallas_call | solution.py:548
  230.4 20.9 %shard_map.90 = (bf16[128,2048]{1,0:T(8,128)(2,1)}, f32[128,128]{1,0:T(8,128)}, f32[16,128]{1,0:T(8,128)}) custom-call(bf16[128,256]{1,0:T(8,128)(2,1)} %copy-done.8, f32[128,128]{1,0:T(8,128)} %convolution_bitcast_fusion.1.up_ref, f32[128,128]{1,0:T(8,128)} %fusion.10.be_ref), custom_call_target="tpu_custom_call" | custom-call | tf_op jit(solution)/shard_map/pallas_call | solution.py:453
  252.7 1.5 fusion.3
  254.9 18.6 %shard_map.91 = f32[8,128]{1,0:T(8,128)} custom-call(f32[8,128]{1,0:T(8,128)} %scatter.59.x_ref), custom_call_target="tpu_custom_call" | custom-call | tf_op jit(solution)/shard_map/pallas_call | solution.py:106
  275.1 17.1 %shard_map.92 = f32[8,128]{1,0:T(8,128)} custom-call(f32[8,128]{1,0:T(8,128)} %scatter.61.x_ref), custom_call_target="tpu_custom_call" | custom-call | tf_op jit(solution)/shard_map/pallas_call | solution.py:106
  293.6 36.3 %shard_map.93 = (f32[128,256]{1,0:T(8,128)}, f32[128,128]{1,0:T(8,128)}) custom-call(bf16[128,256]{1,0:T(8,128)(2,1)} %get-tuple-element.404.x_ref, bf16[256,2048]{1,0:T(8,128)(2,1)} %inv_ref.5, f32[16,256]{1,0:T(8,128)} %dynamic-slice_bitcast_fusion.pick_ref, f32[7,128,128]{2,1,0:T(8,128)} %shard_map.84.u_ref), custom_call_target="tpu_custom_call" | custom-call | tf_op jit(solution)/shard_map/pallas_call | solution.py:548
  332.8 21.8 %shard_map.94 = (bf16[128,2048]{1,0:T(8,128)(2,1)}, f32[128,128]{1,0:T(8,128)}, f32[16,128]{1,0:T(8,128)}) custom-call(bf16[128,256]{1,0:T(8,128)(2,1)} %copy-done.6, f32[128,128]{1,0:T(8,128)} %convolution_bitcast_fusion.up_ref, f32[128,128]{1,0:T(8,128)} %fusion.9.be_ref), custom_call_target="tpu_custom_call" | custom-call | tf_op jit(solution)/shard_map/pallas_call | solution.py:453
  355.9 1.5 fusion.1
  358.2 17.5 %shard_map.95 = f32[8,128]{1,0:T(8,128)} custom-call(f32[8,128]{1,0:T(8,128)} %scatter.65.x_ref), custom_call_target="tpu_custom_call" | custom-call | tf_op jit(solution)/shard_map/pallas_call | solution.py:106
  377.2 17.5 %shard_map.96 = f32[8,128]{1,0:T(8,128)} custom-call(f32[8,128]{1,0:T(8,128)} %scatter.69.x_ref), custom_call_target="tpu_custom_call" | custom-call | tf_op jit(solution)/shard_map/pallas_call | solution.py:106
  398.9 2.0 bitcast_select_fusion
  400.9 1.4 scatter.66
  405.2 3.3 broadcast_select_fusion
  408.6 1.9 fusion.25
  (120 shorter events, 39.2 us)
Async XLA Ops:
  0.0 26.7 %copy-start = (bf16[256,2048]{1,0:T(8,128)(2,1)S(1)}, bf16[256,2048]{1,0:T(8,128)(2,1)}, u32[]{:S(2)}) copy-start(bf16[256,2048]{1,0:T(8,128)(2,1)} %param.69) | copy-start | bytes 3145732
  0.0 1.0 copy-start.13
  1.0 0.9 copy-start.5
  1.0 0.9 copy-start.4
  24.9 0.7 copy-start.14
  25.6 0.8 copy-start.3
  25.6 0.9 copy-start.10
  26.4 0.9 copy-start.2
  26.5 1.0 copy-start.9
  26.6 0.8 copy-start.11
  27.4 34.9 %copy-start.1 = (bf16[256,2048]{1,0:T(8,128)(2,1)S(1)}, bf16[256,2048]{1,0:T(8,128)(2,1)}, u32[]{:S(2)}) copy-start(bf16[256,2048]{1,0:T(8,128)(2,1)} %inv_ref.5) | copy-start | bytes 3145732
  129.5 0.8 copy-start.7
  149.6 1.0 copy-start.16
  228.7 0.8 copy-start.8
  251.3 1.0 copy-start.17
  331.1 0.8 copy-start.6
  354.6 1.0 copy-start.15
  375.7 0.7 slice-start
  398.1 0.8 copy-start.12

commit v8 on v7

--- a/solution.py
+++ b/solution.py
@@ -571,6 +571,126 @@
     )(x, inverse, picks, chain)
 
 
+def _exchange_sum(stages, source, slots, partial, sends, recvs, out):
+    count = len(stages)
+    for stage, (axis, n) in enumerate(stages):
+        mine = lax.axis_index(axis)
+        copies = []
+        for k in range(1, n):
+            copy = pltpu.make_async_remote_copy(
+                src_ref=source,
+                dst_ref=slots[stage].at[mine],
+                send_sem=sends[stage].at[k],
+                recv_sem=recvs[stage].at[mine],
+                device_id={axis: lax.rem(mine + k, n)},
+                device_id_type=MESH,
+            )
+            copy.start()
+            copies.append(copy)
+        slots[stage][mine] = source[...]
+        for k in range(1, n):
+            sender = lax.rem(mine + k, n)
+            pltpu.make_async_remote_copy(
+                src_ref=source,
+                dst_ref=slots[stage].at[sender],
+                send_sem=sends[stage].at[k],
+                recv_sem=recvs[stage].at[sender],
+                device_id={axis: sender},
+                device_id_type=MESH,
+            ).wait_recv()
+        for copy in copies:
+            copy.wait_send()
+        total = slots[stage][0]
+        for j in range(1, n):
+            total = total + slots[stage][j]
+        if stage == count - 1:
+            out[...] = total
+        else:
+            partial[...] = total
+            source = partial
+
+
+def _project_kernel(stages, depth, basis_ref, image_ref, h_ref, next_ref, *scratch):
+    count = len(stages)
+    first, second = scratch[: 3 * count + 1], scratch[3 * count + 1 : 6 * count + 2]
+    rows, work = scratch[6 * count + 2 :]
+    barrier = pltpu.get_barrier_semaphore()
+    peers = 0
+    for axis, n in stages:
+        mine = lax.axis_index(axis)
+        for k in range(1, n):
+            pl.semaphore_signal(
+                barrier, inc=1, device_id={axis: lax.rem(mine + k, n)}, device_id_type=MESH
+            )
+            peers += 1
+    pl.semaphore_wait(barrier, peers)
+    highest = lax.Precision.HIGHEST
+    contract = (((1,), (1,)), ((), ()))
+    image = image_ref[...]
+    ones = jnp.ones((8, image.shape[1]), jnp.float32)
+    eye = (
+        lax.broadcasted_iota(jnp.int32, (image.shape[0],) * 2, 0)
+        == lax.broadcasted_iota(jnp.int32, (image.shape[0],) * 2, 1)
+    ).astype(jnp.float32)
+    rows[...] = jnp.zeros_like(rows)
+    for i in range(depth):
+        summed = lax.dot_general(
+            ones, image * basis_ref[i], contract, precision=highest,
+            preferred_element_type=jnp.float32,
+        )
+        rows[i : i + 1, :] = summed[0:1, :]
+
+    def run(buffers, source, out):
+        slots = buffers[:count]
+        partial = buffers[count]
+        sends = buffers[count + 1 : 2 * count + 1]
+        recvs = buffers[2 * count + 1 :]
+        _exchange_sum(stages, source, slots, partial, sends, recvs, out)
+
+    run(first, rows, h_ref)
+    columns = lax.dot_general(
+        eye, h_ref[...], contract, precision=highest, preferred_element_type=jnp.float32
+    )
+    for i in range(depth):
+        image = image - columns[:, i : i + 1] * basis_ref[i]
+    work[...] = lax.dot_general(
+        ones, image * image, contract, precision=highest, preferred_element_type=jnp.float32
+    )
+    run(second, work, rows)
+    length = jnp.sqrt(rows[...] + epsilon)
+    h_ref[depth : depth + 1, :] = length[0:1, :]
+    scale = lax.dot_general(
+        eye, length, contract, precision=highest, preferred_element_type=jnp.float32
+    )
+    next_ref[...] = image / scale[:, 0:1]
+
+
+def project(stacked, image, mesh_shape):
+    depth, cases, width = stacked.shape
+    stages = tuple((axis, mesh_shape[axis]) for axis in ("blk", "sec") if mesh_shape[axis] > 1)
+
+    def buffers():
+        out = [pltpu.VMEM((n, 8, cases), jnp.float32) for _, n in stages]
+        out.append(pltpu.VMEM((8, cases), jnp.float32))
+        out += [pltpu.SemaphoreType.DMA((n,)) for _, n in stages]
+        out += [pltpu.SemaphoreType.DMA((n,)) for _, n in stages]
+        return out
+
+    return pl.pallas_call(
+        functools.partial(_project_kernel, stages, depth),
+        out_shape=(
+            jax.ShapeDtypeStruct((8, cases), jnp.float32),
+            jax.ShapeDtypeStruct((cases, width), jnp.float32),
+        ),
+        in_specs=[pl.BlockSpec(memory_space=pltpu.VMEM)] * 2,
+        out_specs=[pl.BlockSpec(memory_space=pltpu.VMEM)] * 2,
+        scratch_shapes=buffers()
+        + buffers()
+        + [pltpu.VMEM((8, cases), jnp.float32), pltpu.VMEM((8, cases), jnp.float32)],
+        compiler_params=pltpu.CompilerParams(collective_id=6 + depth, has_side_effects=True),
+    )(stacked, image)
+
+
 def least_squares(hessen, beta):
     cases = hessen.shape[0]
     depth = hessen.shape[2]
@@ -691,12 +811,9 @@
         )
         product = operator(direction) + jac_diag * direction
         stacked = jnp.stack(basis)
-        projections = global_sum(jnp.sum(product[None] * stacked, axis=2), mesh_shape)
-        product = product - jnp.sum(projections[:, :, None] * stacked, axis=0)
-        length = lengths(product)
-        hessen = hessen.at[:, : column + 1, column].set(projections.T)
-        hessen = hessen.at[:, column + 1, column].set(length)
-        basis.append(product / length[:, None])
+        sums, following = project(stacked, product, mesh_shape)
+        hessen = hessen.at[:, : column + 2, column].set(sums[: column + 2].T)
+        basis.append(following)
         directions.append(direction)
     weights = least_squares(hessen, beta)
     update = jnp.zeros_like(state_now)

time: 413 us -> 391 us (0.947)
  Pallas kernels: 343 us -> 329 us
  local copies, waits for them, and re-layouts: 13.2 us -> 6.07 us
    pallas_call x7 -> x1, Pallas kernels: 123 us -> 17.2 us  [all_sum(): pl.pallas_call(functools.partial(_reduce_kernel, stages), out_shape=jax.S...]
    pallas_call x0 -> x3, Pallas kernels: none -> 93.6 us  [project(): pl.pallas_call(functools.partial(_project_kernel, stages, depth), out_sha...]
    pallas_call x4, Pallas kernels: 83.1 us -> 78.8 us  [operator_exchange(): pl.pallas_call(functools.partial(_operator_kernel, n_sec, n_blk), out_sha...]
where the time goes in v8:
time: 391 us; the launch traced here: 389 us
  Pallas kernels  329 us (84%)
  matrix products  24.3 us (6%)
  other arithmetic  15.9 us (4%)
  blocking collectives  14 us (4%)
  local copies, waits for them, and re-layouts  6.07 us (2%)
    pallas_call x3, Pallas kernels, precondition_sweep(): pl.pallas_call(functools.partial(_precondition_kernel, n_sec, n_blk, plan...  118 us
    pallas_call x3, Pallas kernels, project(): pl.pallas_call(functools.partial(_project_kernel, stages, depth), out_sha...  93.6 us
    pallas_call x4, Pallas kernels, operator_exchange(): pl.pallas_call(functools.partial(_operator_kernel, n_sec, n_blk), out_sha...  78.8 us
    pallas_call x1, Pallas kernels, scan_maps(): pl.pallas_call(functools.partial(_maps_kernel, n, n_blk, rounds), out_sha...  20.7 us
    pallas_call x1, Pallas kernels, all_sum(): pl.pallas_call(functools.partial(_reduce_kernel, stages), out_shape=jax.S...  17.2 us
    all_gather x1, blocking collectives, local(): lax.all_gather(back_panel, 'blk', axis=0, tiled=True)  14 us
    dot_general x4, matrix products, operator(): lax.dot_general(gathered, section_block, contract, preferred_element_type...  8.35 us

profile of v8, /device:TPU:1, one launch (start us, length us, event | category | flops | bytes accessed | tf_op | source)
XLA Modules:
  0.0 389.5 jit_solution(10530737698401232674)
XLA Ops:
  2.7 22.1 %shard_map.82 = (bf16[128,2048]{1,0:T(8,128)(2,1)}, f32[128,128]{1,0:T(8,128)}, f32[16,128]{1,0:T(8,128)}) custom-call(bf16[128,256]{1,0:T(8,128)(2,1)} %copy-done.7, f32[128,128]{1,0:T(8,128)} %fusion.47.up_ref, f32[128,128]{1,0:T(8,128)} %fusion.12.be_ref), custom_call_target="tpu_custom_call" | custom-call | tf_op jit(solution)/shard_map/pallas_call | solution.py:453
  27.5 1.7 multiply_reduce_fusion
  29.8 17.2 %shard_map.83 = f32[8,128]{1,0:T(8,128)} custom-call(f32[8,128]{1,0:T(8,128)} %scatter.20.x_ref), custom_call_target="tpu_custom_call" | custom-call | tf_op jit(solution)/shard_map/pallas_call | solution.py:106
  48.4 14.0 %all_gather.3 = bf16[2048,128]{1,0:T(8,128)(2,1)S(1)} all-gather(bf16[256,128]{1,0:T(8,128)(2,1)S(1)} %copy-done.4), channel_id=1, replica_groups=mesh['sec'=32,'blk'=8] {'blk'}, dimensions={0}, use_global_device_ids=true | all-gather | bytes 589824 | tf_op jit(solution)/shard_map/all_gather | solution.py:737
  63.6 20.7 %shard_map.84.u_ref = f32[7,128,128]{2,1,0:T(8,128)} custom-call(f32[16,128]{1,0:T(8,128)} %convolution_negate_fusion.e_ref), custom_call_target="tpu_custom_call" | custom-call | tf_op jit(solution)/shard_map/pallas_call | solution.py:282
  84.9 43.5 %shard_map.85 = (f32[128,256]{1,0:T(8,128)}, f32[128,128]{1,0:T(8,128)}) custom-call(bf16[128,256]{1,0:T(8,128)(2,1)} %get-tuple-element.301.x_ref, bf16[256,2048]{1,0:T(8,128)(2,1)} %inv_ref.5, f32[16,256]{1,0:T(8,128)} %dynamic-slice_bitcast_fusion.pick_ref, f32[7,128,128]{2,1,0:T(8,128)} %shard_map.84.u_ref), custom_call_target="tpu_custom_call" | custom-call | tf_op jit(solution)/shard_map/pallas_call | solution.py:548
  128.4 1.3 fusion.44
  131.3 18.7 %shard_map.86 = (bf16[128,2048]{1,0:T(8,128)(2,1)}, f32[128,128]{1,0:T(8,128)}, f32[16,128]{1,0:T(8,128)}) custom-call(bf16[128,256]{1,0:T(8,128)(2,1)} %copy-done.9, f32[128,128]{1,0:T(8,128)} %convolution_bitcast_fusion.2.up_ref, f32[128,128]{1,0:T(8,128)} %fusion.11.be_ref), custom_call_target="tpu_custom_call" | custom-call | tf_op jit(solution)/shard_map/pallas_call | solution.py:453
  151.3 2.2 fusion.5.image_ref
  153.5 31.4 %shard_map.87 = (f32[8,128]{1,0:T(8,128)}, f32[128,256]{1,0:T(8,128)}) custom-call(f32[1,128,256]{2,1,0:T(8,128)} %get-tuple-element.302.basis_ref, f32[128,256]{1,0:T(8,128)} %fusion.5.image_ref), custom_call_target="tpu_custom_call" | custom-call | tf_op jit(solution)/shard_map/pallas_call | solution.py:679
  184.9 1.5 convert_element_type.49.x_ref
  186.5 36.8 %shard_map.88 = (f32[128,256]{1,0:T(8,128)}, f32[128,128]{1,0:T(8,128)}) custom-call(bf16[128,256]{1,0:T(8,128)(2,1)} %convert_element_type.49.x_ref, bf16[256,2048]{1,0:T(8,128)(2,1)} %inv_ref.5, f32[16,256]{1,0:T(8,128)} %dynamic-slice_bitcast_fusion.pick_ref, f32[7,128,128]{2,1,0:T(8,128)} %shard_map.84.u_ref), custom_call_target="tpu_custom_call" | custom-call | tf_op jit(solution)/shard_map/pallas_call | solution.py:548
  226.3 19.9 %shard_map.89 = (bf16[128,2048]{1,0:T(8,128)(2,1)}, f32[128,128]{1,0:T(8,128)}, f32[16,128]{1,0:T(8,128)}) custom-call(bf16[128,256]{1,0:T(8,128)(2,1)} %copy-done.10, f32[128,128]{1,0:T(8,128)} %convolution_bitcast_fusion.1.up_ref, f32[128,128]{1,0:T(8,128)} %fusion.10.be_ref), custom_call_target="tpu_custom_call" | custom-call | tf_op jit(solution)/shard_map/pallas_call | solution.py:453
  247.6 2.2 fusion.3.image_ref
  250.5 30.3 %shard_map.90 = (f32[8,128]{1,0:T(8,128)}, f32[128,256]{1,0:T(8,128)}) custom-call(f32[2,128,256]{2,1,0:T(8,128)} %pad_maximum_fusion.1.basis_ref, f32[128,256]{1,0:T(8,128)} %fusion.3.image_ref), custom_call_target="tpu_custom_call" | custom-call | tf_op jit(solution)/shard_map/pallas_call | solution.py:679
  280.9 1.5 convert_element_type.52.x_ref
  282.4 38.1 %shard_map.91 = (f32[128,256]{1,0:T(8,128)}, f32[128,128]{1,0:T(8,128)}) custom-call(bf16[128,256]{1,0:T(8,128)(2,1)} %convert_element_type.52.x_ref, bf16[256,2048]{1,0:T(8,128)(2,1)} %inv_ref.5, f32[16,256]{1,0:T(8,128)} %dynamic-slice_bitcast_fusion.pick_ref, f32[7,128,128]{2,1,0:T(8,128)} %shard_map.84.u_ref), custom_call_target="tpu_custom_call" | custom-call | tf_op jit(solution)/shard_map/pallas_call | solution.py:548
  320.5 1.3 fusion.46
  323.5 18.1 %shard_map.92 = (bf16[128,2048]{1,0:T(8,128)(2,1)}, f32[128,128]{1,0:T(8,128)}, f32[16,128]{1,0:T(8,128)}) custom-call(bf16[128,256]{1,0:T(8,128)(2,1)} %copy-done.8, f32[128,128]{1,0:T(8,128)} %convolution_bitcast_fusion.up_ref, f32[128,128]{1,0:T(8,128)} %fusion.9.be_ref), custom_call_target="tpu_custom_call" | custom-call | tf_op jit(solution)/shard_map/pallas_call | solution.py:453
  342.9 2.2 fusion.1.image_ref
  345.9 31.8 %shard_map.93 = (f32[8,128]{1,0:T(8,128)}, f32[128,256]{1,0:T(8,128)}) custom-call(f32[3,128,256]{2,1,0:T(8,128)} %pad_maximum_fusion.basis_ref, f32[128,256]{1,0:T(8,128)} %fusion.1.image_ref), custom_call_target="tpu_custom_call" | custom-call | tf_op jit(solution)/shard_map/pallas_call | solution.py:679
  379.1 1.4 scatter.24
  383.4 3.2 broadcast_select_fusion
  386.7 1.9 fusion.23
  (101 shorter events, 25.9 us)
Async XLA Ops:
  0.0 26.7 %copy-start = (bf16[256,2048]{1,0:T(8,128)(2,1)S(1)}, bf16[256,2048]{1,0:T(8,128)(2,1)}, u32[]{:S(2)}) copy-start(bf16[256,2048]{1,0:T(8,128)(2,1)} %param.51) | copy-start | bytes 3145732
  0.0 1.0 copy-start.15
  1.0 0.9 copy-start.7
  1.0 0.9 copy-start.6
  24.9 0.7 copy-start.16
  25.6 0.8 copy-start.4
  25.6 0.9 copy-start.13
  26.5 0.9 copy-start.2
  26.5 1.0 copy-start.12
  26.7 0.8 copy-start.14
  27.5 34.9 %copy-start.1 = (bf16[256,2048]{1,0:T(8,128)(2,1)S(1)}, bf16[256,2048]{1,0:T(8,128)(2,1)}, u32[]{:S(2)}) copy-start(bf16[256,2048]{1,0:T(8,128)(2,1)} %inv_ref.5) | copy-start | bytes 3145732
  129.6 0.8 copy-start.9
  150.0 1.1 copy-start.18
  224.6 0.8 copy-start.10
  246.2 1.1 copy-start.19
  247.5 2.3 copy-start.3
  247.6 2.2 copy-start.5
  321.8 0.8 copy-start.8
  341.6 1.1 copy-start.17
  342.9 2.2 copy-start.11
  345.9 31.9 %copy-start.20 = (f32[8,128]{1,0:T(8,128)S(1)}, f32[8,128]{1,0:T(8,128)}, u32[]{:S(2)}) copy-start(f32[8,128]{1,0:T(8,128)} %get-tuple-element.283) | copy-start | bytes 12292
  379.1 1.4 copy-start.21

commit v9 on v8

--- a/solution.py
+++ b/solution.py
@@ -352,22 +352,11 @@
     )(x)
 
 
-def _operator_kernel(n_sec, n_blk, x_ref, up_ref, be_ref, g_ref, b_ref, a_ref, *scratch):
+def _operator_phase(n_sec, n_blk, x_ref, up_ref, piece_ref, g_ref, b_ref, a_ref, scratch):
     gslots, bslots, aslots, gsend, grecv, bsend, brecv, asend, arecv = scratch
     sec, blk = lax.axis_index("sec"), lax.axis_index("blk")
     nxt, prv = lax.rem(sec + 1, n_sec), lax.rem(sec + n_sec - 1, n_sec)
     piece = bslots.shape[1]
-    barrier = pltpu.get_barrier_semaphore()
-    for k in range(1, n_blk):
-        pl.semaphore_signal(
-            barrier, inc=1, device_id={"blk": lax.rem(blk + k, n_blk)}, device_id_type=MESH
-        )
-    for j in range(n_blk):
-        for other in (nxt, prv):
-            pl.semaphore_signal(
-                barrier, inc=1, device_id={"sec": other, "blk": j}, device_id_type=MESH
-            )
-    pl.semaphore_wait(barrier, 3 * n_blk - 1)
     copies = []
     for k in range(1, n_blk):
         copies.append(
@@ -380,11 +369,10 @@
                 device_id_type=MESH,
             )
         )
-    mine = pl.ds(pl.multiple_of(blk * piece, 8), piece)
     for j in range(n_blk):
         copies.append(
             pltpu.make_async_remote_copy(
-                src_ref=be_ref.at[mine],
+                src_ref=piece_ref,
                 dst_ref=bslots.at[blk],
                 send_sem=bsend.at[j],
                 recv_sem=brecv.at[blk],
@@ -417,7 +405,7 @@
         ).wait_recv()
     for j in range(n_blk):
         pltpu.make_async_remote_copy(
-            src_ref=be_ref.at[mine],
+            src_ref=piece_ref,
             dst_ref=bslots.at[j],
             send_sem=bsend.at[j],
             recv_sem=brecv.at[j],
@@ -446,6 +434,33 @@
     a_ref[...] = jnp.where(sec <= n_sec - 2, total, jnp.zeros_like(total))
 
 
+def _operator_scratch(n_blk, rows, width, dtype, piece, cases):
+    return [
+        pltpu.VMEM((n_blk, rows, width), dtype),
+        pltpu.VMEM((n_blk, piece, cases), jnp.float32),
+        pltpu.VMEM((n_blk, piece, cases), jnp.float32),
+    ] + [pltpu.SemaphoreType.DMA((n_blk,))] * 6
+
+
+def _operator_kernel(n_sec, n_blk, x_ref, up_ref, be_ref, g_ref, b_ref, a_ref, *scratch):
+    sec, blk = lax.axis_index("sec"), lax.axis_index("blk")
+    nxt, prv = lax.rem(sec + 1, n_sec), lax.rem(sec + n_sec - 1, n_sec)
+    piece = scratch[1].shape[1]
+    barrier = pltpu.get_barrier_semaphore()
+    for k in range(1, n_blk):
+        pl.semaphore_signal(
+            barrier, inc=1, device_id={"blk": lax.rem(blk + k, n_blk)}, device_id_type=MESH
+        )
+    for j in range(n_blk):
+        for other in (nxt, prv):
+            pl.semaphore_signal(
+                barrier, inc=1, device_id={"sec": other, "blk": j}, device_id_type=MESH
+            )
+    pl.semaphore_wait(barrier, 3 * n_blk - 1)
+    mine = be_ref.at[pl.ds(pl.multiple_of(blk * piece, 8), piece)]
+    _operator_phase(n_sec, n_blk, x_ref, up_ref, mine, g_ref, b_ref, a_ref, scratch)
+
+
 def operator_exchange(x, up_t, be_t, n_sec, n_blk):
     rows, width = x.shape
     panel, cases = up_t.shape
@@ -459,18 +474,18 @@
         ),
         in_specs=[pl.BlockSpec(memory_space=pltpu.VMEM)] * 3,
         out_specs=[pl.BlockSpec(memory_space=pltpu.VMEM)] * 3,
-        scratch_shapes=[
-            pltpu.VMEM((n_blk, rows, width), x.dtype),
-            pltpu.VMEM((n_blk, piece, cases), jnp.float32),
-            pltpu.VMEM((n_blk, piece, cases), jnp.float32),
-        ]
-        + [pltpu.SemaphoreType.DMA((n_blk,))] * 6,
+        scratch_shapes=_operator_scratch(n_blk, rows, width, x.dtype, piece, cases),
         compiler_params=pltpu.CompilerParams(collective_id=5, has_side_effects=True),
     )(x, up_t, be_t)
 
 
-def _precondition_kernel(n_sec, n_blk, rounds, x_ref, inv_ref, pick_ref, u_ref, w_ref, o_ref, *scratch):
-    gslots, fpiece, fslots, fmat, carry, slots, gsend, grecv, fsend, frecv, ssend, srecv = scratch
+def _precondition_kernel(
+    n_sec, n_blk, rounds, x_ref, inv_ref, pick_ref, u_ref, gain_ref, ahead_ref,
+    d_ref, g_ref, b_ref, a_ref, *scratch
+):
+    gslots, fpiece, fslots, fmat, carry, slots, gsend, grecv, fsend, frecv, ssend, srecv = scratch[:12]
+    rounded, upward, own_piece = scratch[12:15]
+    phase_scratch = scratch[15:]
     sec, blk = lax.axis_index("sec"), lax.axis_index("blk")
     first = rounds[0][1]
     offsets = len(first) + 1
@@ -507,7 +522,6 @@
             contract,
             preferred_element_type=jnp.float32,
         )
-    w_ref[...] = folded
     fpiece[...] = lax.dot_general(
         pick_ref[...], folded, contract, precision=lax.Precision.HIGHEST,
         preferred_element_type=jnp.float32,
@@ -534,10 +548,24 @@
             joined = joined + jnp.where(sec >= j * d, term, jnp.zeros_like(term))
         carry[k + 1] = joined
         flat += len(js)
-    o_ref[...] = carry[len(rounds)]
-
-
-def precondition_sweep(x, inverse, picks, chain, n_sec, n_blk):
+    before = carry[len(rounds)].T
+    direction = folded - lax.dot_general(
+        before, gain_ref[...], contract, precision=lax.Precision.HIGHEST,
+        preferred_element_type=jnp.float32,
+    )
+    d_ref[...] = direction
+    rounded[...] = direction.astype(rounded.dtype)
+    upward[...] = jnp.dot(
+        rounded[...], ahead_ref[...], preferred_element_type=jnp.float32
+    ).T
+    own_piece[...] = lax.dot_general(
+        pick_ref[...], rounded[...].astype(jnp.float32), contract,
+        precision=lax.Precision.HIGHEST, preferred_element_type=jnp.float32,
+    )
+    _operator_phase(n_sec, n_blk, rounded, upward, own_piece, g_ref, b_ref, a_ref, phase_scratch)
+
+
+def precondition_sweep(x, inverse, picks, chain, gain, ahead, n_sec, n_blk):
     cases, width = x.shape
     piece, _ = picks.shape
     panel = piece * n_blk
@@ -549,10 +577,12 @@
         functools.partial(_precondition_kernel, n_sec, n_blk, plan),
         out_shape=(
             jax.ShapeDtypeStruct((cases, width), jnp.float32),
+            jax.ShapeDtypeStruct((cases, n_blk * width), x.dtype),
             jax.ShapeDtypeStruct((panel, cases), jnp.float32),
+            jax.ShapeDtypeStruct((piece, cases), jnp.float32),
         ),
-        in_specs=[pl.BlockSpec(memory_space=pltpu.VMEM)] * 4,
-        out_specs=[pl.BlockSpec(memory_space=pltpu.VMEM)] * 2,
+        in_specs=[pl.BlockSpec(memory_space=pltpu.VMEM)] * 6,
+        out_specs=[pl.BlockSpec(memory_space=pltpu.VMEM)] * 4,
         scratch_shapes=[
             pltpu.VMEM((n_blk, cases, width), x.dtype),
             pltpu.VMEM((piece, cases), jnp.float32),
@@ -566,9 +596,13 @@
             pltpu.SemaphoreType.DMA((offsets * n_blk,)),
             pltpu.SemaphoreType.DMA((total,)),
             pltpu.SemaphoreType.DMA((total,)),
-        ],
+            pltpu.VMEM((cases, width), x.dtype),
+            pltpu.VMEM((panel, cases), jnp.float32),
+            pltpu.VMEM((piece, cases), jnp.float32),
+        ]
+        + _operator_scratch(n_blk, cases, width, x.dtype, piece, cases),
         compiler_params=pltpu.CompilerParams(collective_id=6, has_side_effects=True),
-    )(x, inverse, picks, chain)
+    )(x, inverse, picks, chain, gain, ahead)
 
 
 def _exchange_sum(stages, source, slots, partial, sends, recvs, out):
@@ -755,10 +789,27 @@
     def fold_section(carry, piece):
         return section_terms(carry[0], carry[1], piece)
 
+    n_sec, n_blk = mesh_shape["sec"], mesh_shape["blk"]
+    piece = panel_width // n_blk
+    local_picks = lax.dynamic_slice_in_dim(selector, lax.axis_index("blk") * piece, piece, 1)
+
+    def finish(gathered, behind_t, ahead_piece):
+        dense_part = lax.dot_general(
+            gathered, section_block, contract, preferred_element_type=jnp.float32
+        )
+        lower_term = lax.dot_general(
+            behind_t.astype(jnp.bfloat16),
+            back_panel,
+            (((0,), (1,)), ((), ())),
+            preferred_element_type=jnp.float32,
+        )
+        upper_term = lax.dot_general(
+            ahead_piece, local_picks, (((0,), (1,)), ((), ())), precision=highest
+        )
+        return dense_part + lower_term + upper_term
+
     def operator(vector):
         rounded = vector.astype(jnp.bfloat16)
-        n_sec, n_blk = mesh_shape["sec"], mesh_shape["blk"]
-        piece = panel_width // n_blk
         up_t = lax.dot_general(
             ahead_panel, rounded, (((0,), (1,)), ((), ())), preferred_element_type=jnp.float32
         )
@@ -768,21 +819,7 @@
             (((0,), (1,)), ((), ())),
             preferred_element_type=jnp.float32,
         )
-        gathered, behind_t, ahead_piece = operator_exchange(rounded, up_t, be_t, n_sec, n_blk)
-        dense_part = lax.dot_general(
-            gathered, section_block, contract, preferred_element_type=jnp.float32
-        )
-        lower_term = lax.dot_general(
-            behind_t.astype(jnp.bfloat16),
-            back_panel,
-            (((0,), (1,)), ((), ())),
-            preferred_element_type=jnp.float32,
-        )
-        local_picks = lax.dynamic_slice_in_dim(selector, lax.axis_index("blk") * piece, piece, 1)
-        upper_term = lax.dot_general(
-            ahead_piece, local_picks, (((0,), (1,)), ((), ())), precision=highest
-        )
-        return dense_part + lower_term + upper_term
+        return finish(*operator_exchange(rounded, up_t, be_t, n_sec, n_blk))
 
     def compose(earlier, later):
         first_map, first_value = earlier
@@ -803,13 +840,11 @@
     hessen = jnp.zeros((cases, KRYLOV + 1, KRYLOV), jnp.float32)
     for column in range(KRYLOV):
         precondition_rounded = basis[column].astype(jnp.bfloat16)
-        precondition_folded, before_t = precondition_sweep(
-            precondition_rounded, block_inverse, own_picks, chain, mesh_shape["sec"], mesh_shape["blk"]
-        )
-        direction = precondition_folded - lax.dot_general(
-            before_t, gain_panel, (((0,), (1,)), ((), ())), precision=highest
-        )
-        product = operator(direction) + jac_diag * direction
+        direction, gathered, behind_t, ahead_piece = precondition_sweep(
+            precondition_rounded, block_inverse, own_picks, chain, gain_panel, ahead_panel,
+            n_sec, n_blk,
+        )
+        product = finish(gathered, behind_t, ahead_piece) + jac_diag * direction
         stacked = jnp.stack(basis)
         sums, following = project(stacked, product, mesh_shape)
         hessen = hessen.at[:, : column + 2, column].set(sums[: column + 2].T)

time: 391 us -> 369 us (0.944)
  Pallas kernels: 329 us -> 313 us
  matrix products: 24.3 us -> 15.4 us
    pallas_call x4 -> x1, Pallas kernels: 78.8 us -> 22.1 us  [operator_exchange(): pl.pallas_call(functools.partial(_operator_kernel, n_sec, n_blk), out_sha...]
    pallas_call x3, Pallas kernels: 118 us -> 161 us  [precondition_sweep(): pl.pallas_call(functools.partial(_precondition_kernel, n_sec, n_blk, plan...]
    dot_general x15 -> x12, matrix products: 16.5 us -> 12.6 us  [the longest x4 8.33 us: finish(): lax.dot_general(gathered, section_block, contract, preferred_element_type...]
where the time goes in v9:
time: 369 us; the launch traced here: 367 us
  Pallas kernels  313 us (85%)
  other arithmetic  16.1 us (4%)
  matrix products  15.4 us (4%)
  blocking collectives  14 us (4%)
  local copies, waits for them, and re-layouts  8.65 us (2%)
    pallas_call x3, Pallas kernels, precondition_sweep(): pl.pallas_call(functools.partial(_precondition_kernel, n_sec, n_blk, plan...  161 us
    pallas_call x3, Pallas kernels, project(): pl.pallas_call(functools.partial(_project_kernel, stages, depth), out_sha...  92.3 us
    pallas_call x1, Pallas kernels, operator_exchange(): pl.pallas_call(functools.partial(_operator_kernel, n_sec, n_blk), out_sha...  22.1 us
    pallas_call x1, Pallas kernels, scan_maps(): pl.pallas_call(functools.partial(_maps_kernel, n, n_blk, rounds), out_sha...  20.6 us
    pallas_call x1, Pallas kernels, all_sum(): pl.pallas_call(functools.partial(_reduce_kernel, stages), out_shape=jax.S...  17.2 us
    all_gather x1, blocking collectives, local(): lax.all_gather(back_panel, 'blk', axis=0, tiled=True)  14 us
    dot_general x4, matrix products, finish(): lax.dot_general(gathered, section_block, contract, preferred_element_type...  8.33 us

profile of v9, /device:TPU:1, one launch (start us, length us, event | category | flops | bytes accessed | tf_op | source)
XLA Modules:
  0.0 367.4 jit_solution(14159797952031978689)
XLA Ops:
  0.0 1.0 convert_element_type.30.x_ref
  2.5 0.8 fusion.43.up_ref
  3.4 22.1 %shard_map.82 = (bf16[128,2048]{1,0:T(8,128)(2,1)}, f32[128,128]{1,0:T(8,128)}, f32[16,128]{1,0:T(8,128)}) custom-call(bf16[128,256]{1,0:T(8,128)(2,1)} %copy-done.8, f32[128,128]{1,0:T(8,128)} %fusion.43.up_ref, f32[128,128]{1,0:T(8,128)} %fusion.9.be_ref), custom_call_target="tpu_custom_call" | custom-call | tf_op jit(solution)/shard_map/pallas_call | solution.py:468
  28.0 1.7 multiply_reduce_fusion
  30.3 17.2 %shard_map.83 = f32[8,128]{1,0:T(8,128)} custom-call(f32[8,128]{1,0:T(8,128)} %scatter.20.x_ref), custom_call_target="tpu_custom_call" | custom-call | tf_op jit(solution)/shard_map/pallas_call | solution.py:106
  48.9 14.0 %all_gather.3 = bf16[2048,128]{1,0:T(8,128)(2,1)S(1)} all-gather(bf16[256,128]{1,0:T(8,128)(2,1)S(1)} %copy-done.5), channel_id=1, replica_groups=mesh['sec'=32,'blk'=8] {'blk'}, dimensions={0}, use_global_device_ids=true | all-gather | bytes 589824 | tf_op jit(solution)/shard_map/all_gather | solution.py:771
  64.2 20.6 %shard_map.84.u_ref = f32[7,128,128]{2,1,0:T(8,128)} custom-call(f32[16,128]{1,0:T(8,128)} %convolution_negate_fusion.e_ref), custom_call_target="tpu_custom_call" | custom-call | tf_op jit(solution)/shard_map/pallas_call | solution.py:282
  85.4 57.3 %shard_map.85 = (f32[128,256]{1,0:T(8,128)}, bf16[128,2048]{1,0:T(8,128)(2,1)}, f32[128,128]{1,0:T(8,128)}, f32[16,128]{1,0:T(8,128)}) custom-call(bf16[128,256]{1,0:T(8,128)(2,1)} %get-tuple-element.295.x_ref, bf16[256,2048]{1,0:T(8,128)(2,1)} %inv_ref.5, f32[16,256]{1,0:T(8,128)} %dynamic-slice_bitcast_fusion.pick_ref, f32[7,128,128]{2,1,0:T(8,128)} %shard_map.84.u_ref, ...), custom_call_target="tpu_custom_call" | custom-call | tf_op jit(solution)/shard_map/pallas_call | solution.py:576
  142.7 1.0 fusion.16
  144.7 2.2 fusion.5.image_ref
  146.9 30.3 %shard_map.86 = (f32[8,128]{1,0:T(8,128)}, f32[128,256]{1,0:T(8,128)}) custom-call(f32[1,128,256]{2,1,0:T(8,128)} %get-tuple-element.296.basis_ref, f32[128,256]{1,0:T(8,128)} %fusion.5.image_ref), custom_call_target="tpu_custom_call" | custom-call | tf_op jit(solution)/shard_map/pallas_call | solution.py:713
  177.2 1.5 convert_element_type.36.x_ref
  178.7 51.4 %shard_map.87 = (f32[128,256]{1,0:T(8,128)}, bf16[128,2048]{1,0:T(8,128)(2,1)}, f32[128,128]{1,0:T(8,128)}, f32[16,128]{1,0:T(8,128)}) custom-call(bf16[128,256]{1,0:T(8,128)(2,1)} %convert_element_type.36.x_ref, bf16[256,2048]{1,0:T(8,128)(2,1)} %inv_ref.5, f32[16,256]{1,0:T(8,128)} %dynamic-slice_bitcast_fusion.pick_ref, f32[7,128,128]{2,1,0:T(8,128)} %shard_map.84.u_ref, ...), custom_call_target="tpu_custom_call" | custom-call | tf_op jit(solution)/shard_map/pallas_call | solution.py:576
  230.1 1.0 fusion.14
  232.0 2.2 fusion.3.image_ref
  235.0 31.6 %shard_map.88 = (f32[8,128]{1,0:T(8,128)}, f32[128,256]{1,0:T(8,128)}) custom-call(f32[2,128,256]{2,1,0:T(8,128)} %pad_maximum_fusion.1.basis_ref, f32[128,256]{1,0:T(8,128)} %fusion.3.image_ref), custom_call_target="tpu_custom_call" | custom-call | tf_op jit(solution)/shard_map/pallas_call | solution.py:713
  266.5 1.5 convert_element_type.38.x_ref
  268.1 52.0 %shard_map.89 = (f32[128,256]{1,0:T(8,128)}, bf16[128,2048]{1,0:T(8,128)(2,1)}, f32[128,128]{1,0:T(8,128)}, f32[16,128]{1,0:T(8,128)}) custom-call(bf16[128,256]{1,0:T(8,128)(2,1)} %convert_element_type.38.x_ref, bf16[256,2048]{1,0:T(8,128)(2,1)} %inv_ref.5, f32[16,256]{1,0:T(8,128)} %dynamic-slice_bitcast_fusion.pick_ref, f32[7,128,128]{2,1,0:T(8,128)} %shard_map.84.u_ref, ...), custom_call_target="tpu_custom_call" | custom-call | tf_op jit(solution)/shard_map/pallas_call | solution.py:576
  320.1 1.0 fusion.35
  322.0 2.2 fusion.1.image_ref
  325.0 30.5 %shard_map.90 = (f32[8,128]{1,0:T(8,128)}, f32[128,256]{1,0:T(8,128)}) custom-call(f32[3,128,256]{2,1,0:T(8,128)} %pad_maximum_fusion.basis_ref, f32[128,256]{1,0:T(8,128)} %fusion.1.image_ref), custom_call_target="tpu_custom_call" | custom-call | tf_op jit(solution)/shard_map/pallas_call | solution.py:713
  356.8 1.5 scatter.24
  361.2 3.3 broadcast_select_fusion
  364.6 2.0 fusion.22
  (91 shorter events, 17.1 us)
Async XLA Ops:
  0.0 27.2 %copy-start = (bf16[256,2048]{1,0:T(8,128)(2,1)S(1)}, bf16[256,2048]{1,0:T(8,128)(2,1)}, u32[]{:S(2)}) copy-start(bf16[256,2048]{1,0:T(8,128)(2,1)} %param.51) | copy-start | bytes 3145732
  1.0 1.5 copy-start.8
  1.0 0.7 copy-start.20
  1.7 0.8 copy-start.7
  25.5 0.7 copy-start.17
  26.2 0.8 copy-start.5
  26.2 0.9 copy-start.14
  27.0 0.9 copy-start.2
  27.0 1.0 copy-start.13
  27.2 0.8 copy-start.16
  28.0 34.9 %copy-start.1 = (bf16[256,2048]{1,0:T(8,128)(2,1)S(1)}, bf16[256,2048]{1,0:T(8,128)(2,1)}, u32[]{:S(2)}) copy-start(bf16[256,2048]{1,0:T(8,128)(2,1)} %inv_ref.5) | copy-start | bytes 3145732
  63.4 21.4 %copy-start.3 = (f32[256,128]{1,0:T(8,128)}, f32[256,128]{1,0:T(8,128)S(1)}, u32[]{:S(2)}) copy-start(f32[256,128]{1,0:T(8,128)S(1)} %fusion.44.gain_ref) | copy-start | bytes 393220
  142.7 1.1 copy-start.18
  143.8 0.9 copy-start.9
  230.1 1.1 copy-start.19
  231.1 0.9 copy-start.10
  232.0 2.2 copy-start.4
  232.0 2.2 copy-start.6
  320.1 1.0 copy-start.15
  321.1 0.9 copy-start.11
  322.0 2.2 copy-start.12
  325.0 30.5 %copy-start.21 = (f32[8,128]{1,0:T(8,128)S(1)}, f32[8,128]{1,0:T(8,128)}, u32[]{:S(2)}) copy-start(f32[8,128]{1,0:T(8,128)} %get-tuple-element.278) | copy-start | bytes 12292
  356.8 1.5 copy-start.22

commit v10 on v9

--- a/solution.py
+++ b/solution.py
@@ -217,10 +217,10 @@
             mats[o, j * piece : (j + 1) * piece, :] = slots[o * n_blk + j]
 
 
-def _greet_all(n_sec, n_blk, offsets, rounds, blk_peers):
+def _greet_all(n_sec, n_blk, offsets, rounds, blk_peers, stages=()):
     barrier = pltpu.get_barrier_semaphore()
     sec, blk = lax.axis_index("sec"), lax.axis_index("blk")
-    count = 0
+    count = _signal_stages(barrier, stages)
     if blk_peers:
         for k in range(1, n_blk):
             pl.semaphore_signal(
@@ -480,16 +480,19 @@
 
 
 def _precondition_kernel(
-    n_sec, n_blk, rounds, x_ref, inv_ref, pick_ref, u_ref, gain_ref, ahead_ref,
-    d_ref, g_ref, b_ref, a_ref, *scratch
+    n_sec, n_blk, rounds, stages, depth, basis_ref, image_ref, inv_ref, pick_ref, u_ref,
+    gain_ref, ahead_ref, h_ref, next_ref, d_ref, g_ref, b_ref, a_ref, *scratch
 ):
     gslots, fpiece, fslots, fmat, carry, slots, gsend, grecv, fsend, frecv, ssend, srecv = scratch[:12]
-    rounded, upward, own_piece = scratch[12:15]
-    phase_scratch = scratch[15:]
+    rounded, upward, own_piece, x_ref = scratch[12:16]
+    phase_scratch = scratch[16:25]
+    project_scratch = scratch[25:]
     sec, blk = lax.axis_index("sec"), lax.axis_index("blk")
     first = rounds[0][1]
     offsets = len(first) + 1
-    _greet_all(n_sec, n_blk, offsets, rounds, True)
+    _greet_all(n_sec, n_blk, offsets, rounds, True, stages)
+    _project_body(stages, depth, basis_ref, image_ref, h_ref, next_ref, project_scratch)
+    x_ref[...] = next_ref[...].astype(x_ref.dtype)
 
     def blk_copy(k, target, slot):
         return pltpu.make_async_remote_copy(
@@ -565,26 +568,31 @@
     _operator_phase(n_sec, n_blk, rounded, upward, own_piece, g_ref, b_ref, a_ref, phase_scratch)
 
 
-def precondition_sweep(x, inverse, picks, chain, gain, ahead, n_sec, n_blk):
-    cases, width = x.shape
+def precondition_sweep(basis, image, inverse, picks, chain, gain, ahead, mesh_shape, depth):
+    n_sec, n_blk = mesh_shape["sec"], mesh_shape["blk"]
+    stages = _global_stages(mesh_shape)
+    cases, width = image.shape
     piece, _ = picks.shape
     panel = piece * n_blk
     plan = _plan(n_sec)
     rounds = len(plan)
     total = sum(len(js) for _, js in plan)
     offsets = len(plan[0][1]) + 1
+    dtype = jnp.bfloat16
     return pl.pallas_call(
-        functools.partial(_precondition_kernel, n_sec, n_blk, plan),
+        functools.partial(_precondition_kernel, n_sec, n_blk, plan, stages, depth),
         out_shape=(
+            jax.ShapeDtypeStruct((8, cases), jnp.float32),
             jax.ShapeDtypeStruct((cases, width), jnp.float32),
-            jax.ShapeDtypeStruct((cases, n_blk * width), x.dtype),
+            jax.ShapeDtypeStruct((cases, width), jnp.float32),
+            jax.ShapeDtypeStruct((cases, n_blk * width), dtype),
             jax.ShapeDtypeStruct((panel, cases), jnp.float32),
             jax.ShapeDtypeStruct((piece, cases), jnp.float32),
         ),
-        in_specs=[pl.BlockSpec(memory_space=pltpu.VMEM)] * 6,
-        out_specs=[pl.BlockSpec(memory_space=pltpu.VMEM)] * 4,
+        in_specs=[pl.BlockSpec(memory_space=pltpu.VMEM)] * 7,
+        out_specs=[pl.BlockSpec(memory_space=pltpu.VMEM)] * 6,
         scratch_shapes=[
-            pltpu.VMEM((n_blk, cases, width), x.dtype),
+            pltpu.VMEM((n_blk, cases, width), dtype),
             pltpu.VMEM((piece, cases), jnp.float32),
             pltpu.VMEM((offsets * n_blk, piece, cases), jnp.float32),
             pltpu.VMEM((offsets, panel, cases), jnp.float32),
@@ -596,13 +604,15 @@
             pltpu.SemaphoreType.DMA((offsets * n_blk,)),
             pltpu.SemaphoreType.DMA((total,)),
             pltpu.SemaphoreType.DMA((total,)),
-            pltpu.VMEM((cases, width), x.dtype),
+            pltpu.VMEM((cases, width), dtype),
             pltpu.VMEM((panel, cases), jnp.float32),
             pltpu.VMEM((piece, cases), jnp.float32),
+            pltpu.VMEM((cases, width), dtype),
         ]
-        + _operator_scratch(n_blk, cases, width, x.dtype, piece, cases),
-        compiler_params=pltpu.CompilerParams(collective_id=6, has_side_effects=True),
-    )(x, inverse, picks, chain, gain, ahead)
+        + _operator_scratch(n_blk, cases, width, dtype, piece, cases)
+        + _project_scratch(stages, cases),
+        compiler_params=pltpu.CompilerParams(collective_id=10 + depth, has_side_effects=True),
+    )(basis, image, inverse, picks, chain, gain, ahead)
 
 
 def _exchange_sum(stages, source, slots, partial, sends, recvs, out):
@@ -644,20 +654,21 @@
             source = partial
 
 
-def _project_kernel(stages, depth, basis_ref, image_ref, h_ref, next_ref, *scratch):
+def _project_scratch(stages, cases):
+    def buffers():
+        out = [pltpu.VMEM((n, 8, cases), jnp.float32) for _, n in stages]
+        out.append(pltpu.VMEM((8, cases), jnp.float32))
+        out += [pltpu.SemaphoreType.DMA((n,)) for _, n in stages]
+        out += [pltpu.SemaphoreType.DMA((n,)) for _, n in stages]
+        return out
+
+    return buffers() + buffers() + [pltpu.VMEM((8, cases), jnp.float32)] * 2
+
+
+def _project_body(stages, depth, basis_ref, image_ref, h_ref, next_ref, scratch):
     count = len(stages)
     first, second = scratch[: 3 * count + 1], scratch[3 * count + 1 : 6 * count + 2]
-    rows, work = scratch[6 * count + 2 :]
-    barrier = pltpu.get_barrier_semaphore()
-    peers = 0
-    for axis, n in stages:
-        mine = lax.axis_index(axis)
-        for k in range(1, n):
-            pl.semaphore_signal(
-                barrier, inc=1, device_id={axis: lax.rem(mine + k, n)}, device_id_type=MESH
-            )
-            peers += 1
-    pl.semaphore_wait(barrier, peers)
+    rows, work = scratch[6 * count + 2 : 6 * count + 4]
     highest = lax.Precision.HIGHEST
     contract = (((1,), (1,)), ((), ()))
     image = image_ref[...]
@@ -666,13 +677,6 @@
         lax.broadcasted_iota(jnp.int32, (image.shape[0],) * 2, 0)
         == lax.broadcasted_iota(jnp.int32, (image.shape[0],) * 2, 1)
     ).astype(jnp.float32)
-    rows[...] = jnp.zeros_like(rows)
-    for i in range(depth):
-        summed = lax.dot_general(
-            ones, image * basis_ref[i], contract, precision=highest,
-            preferred_element_type=jnp.float32,
-        )
-        rows[i : i + 1, :] = summed[0:1, :]
 
     def run(buffers, source, out):
         slots = buffers[:count]
@@ -681,12 +685,22 @@
         recvs = buffers[2 * count + 1 :]
         _exchange_sum(stages, source, slots, partial, sends, recvs, out)
 
-    run(first, rows, h_ref)
-    columns = lax.dot_general(
-        eye, h_ref[...], contract, precision=highest, preferred_element_type=jnp.float32
-    )
-    for i in range(depth):
-        image = image - columns[:, i : i + 1] * basis_ref[i]
+    if depth > 0:
+        rows[...] = jnp.zeros_like(rows)
+        for i in range(depth):
+            summed = lax.dot_general(
+                ones, image * basis_ref[i], contract, precision=highest,
+                preferred_element_type=jnp.float32,
+            )
+            rows[i : i + 1, :] = summed[0:1, :]
+        run(first, rows, h_ref)
+        columns = lax.dot_general(
+            eye, h_ref[...], contract, precision=highest, preferred_element_type=jnp.float32
+        )
+        for i in range(depth):
+            image = image - columns[:, i : i + 1] * basis_ref[i]
+    else:
+        h_ref[...] = jnp.zeros_like(h_ref)
     work[...] = lax.dot_general(
         ones, image * image, contract, precision=highest, preferred_element_type=jnp.float32
     )
@@ -699,17 +713,31 @@
     next_ref[...] = image / scale[:, 0:1]
 
 
+def _signal_stages(barrier, stages):
+    peers = 0
+    for axis, n in stages:
+        mine = lax.axis_index(axis)
+        for k in range(1, n):
+            pl.semaphore_signal(
+                barrier, inc=1, device_id={axis: lax.rem(mine + k, n)}, device_id_type=MESH
+            )
+            peers += 1
+    return peers
+
+
+def _project_kernel(stages, depth, basis_ref, image_ref, h_ref, next_ref, *scratch):
+    barrier = pltpu.get_barrier_semaphore()
+    pl.semaphore_wait(barrier, _signal_stages(barrier, stages))
+    _project_body(stages, depth, basis_ref, image_ref, h_ref, next_ref, scratch)
+
+
+def _global_stages(mesh_shape):
+    return tuple((axis, mesh_shape[axis]) for axis in ("blk", "sec") if mesh_shape[axis] > 1)
+
+
 def project(stacked, image, mesh_shape):
     depth, cases, width = stacked.shape
-    stages = tuple((axis, mesh_shape[axis]) for axis in ("blk", "sec") if mesh_shape[axis] > 1)
-
-    def buffers():
-        out = [pltpu.VMEM((n, 8, cases), jnp.float32) for _, n in stages]
-        out.append(pltpu.VMEM((8, cases), jnp.float32))
-        out += [pltpu.SemaphoreType.DMA((n,)) for _, n in stages]
-        out += [pltpu.SemaphoreType.DMA((n,)) for _, n in stages]
-        return out
-
+    stages = _global_stages(mesh_shape)
     return pl.pallas_call(
         functools.partial(_project_kernel, stages, depth),
         out_shape=(
@@ -718,9 +746,7 @@
         ),
         in_specs=[pl.BlockSpec(memory_space=pltpu.VMEM)] * 2,
         out_specs=[pl.BlockSpec(memory_space=pltpu.VMEM)] * 2,
-        scratch_shapes=buffers()
-        + buffers()
-        + [pltpu.VMEM((8, cases), jnp.float32), pltpu.VMEM((8, cases), jnp.float32)],
+        scratch_shapes=_project_scratch(stages, cases),
         compiler_params=pltpu.CompilerParams(collective_id=6 + depth, has_side_effects=True),
     )(stacked, image)
 
@@ -834,22 +860,26 @@
     bent = jnp.tanh(state_now)
     residual = source - operator(state_now) - fan_gain[None, :] * bent
     jac_diag = fan_gain[None, :] * (1.0 - bent * bent)
-    beta = lengths(residual)
-    basis = [residual / beta[:, None]]
+    hessen = jnp.zeros((cases, KRYLOV + 1, KRYLOV), jnp.float32)
+    basis = []
     directions = []
-    hessen = jnp.zeros((cases, KRYLOV + 1, KRYLOV), jnp.float32)
+    product = residual
+    beta = None
     for column in range(KRYLOV):
-        precondition_rounded = basis[column].astype(jnp.bfloat16)
-        direction, gathered, behind_t, ahead_piece = precondition_sweep(
-            precondition_rounded, block_inverse, own_picks, chain, gain_panel, ahead_panel,
-            n_sec, n_blk,
-        )
-        product = finish(gathered, behind_t, ahead_piece) + jac_diag * direction
-        stacked = jnp.stack(basis)
-        sums, following = project(stacked, product, mesh_shape)
-        hessen = hessen.at[:, : column + 2, column].set(sums[: column + 2].T)
+        stacked = jnp.stack(basis) if basis else residual[None]
+        sums, following, direction, gathered, behind_t, ahead_piece = precondition_sweep(
+            stacked, product, block_inverse, own_picks, chain, gain_panel, ahead_panel,
+            mesh_shape, len(basis),
+        )
+        if column == 0:
+            beta = sums[0]
+        else:
+            hessen = hessen.at[:, : column + 1, column - 1].set(sums[: column + 1].T)
         basis.append(following)
         directions.append(direction)
+        product = finish(gathered, behind_t, ahead_piece) + jac_diag * direction
+    sums, _ = project(jnp.stack(basis), product, mesh_shape)
+    hessen = hessen.at[:, : KRYLOV + 1, KRYLOV - 1].set(sums[: KRYLOV + 1].T)
     weights = least_squares(hessen, beta)
     update = jnp.zeros_like(state_now)
     for column in range(KRYLOV):

time: 369 us -> 353 us (0.957)
  Pallas kernels: 313 us -> 303 us
  other arithmetic: 16.1 us -> 11.5 us
    pallas_call x3, Pallas kernels: 161 us -> 229 us  [precondition_sweep(): pl.pallas_call(functools.partial(_precondition_kernel, n_sec, n_blk, plan...]
    pallas_call x3 -> x1, Pallas kernels: 92.3 us -> 29.9 us  [project(): pl.pallas_call(functools.partial(_project_kernel, stages, depth), out_sha...]
    pallas_call x1 -> x0, Pallas kernels: 17.2 us -> none  [all_sum(): pl.pallas_call(functools.partial(_reduce_kernel, stages), out_shape=jax.S...]
    convert_element_type x3 -> x0, other arithmetic: 3.84 us -> none  [local(): precondition_rounded = basis[column].astype(jnp.bfloat16)]
where the time goes in v10:
time: 353 us; the launch traced here: 352 us
  Pallas kernels  303 us (86%)
  matrix products  15.9 us (5%)
  blocking collectives  12.7 us (4%)
  other arithmetic  11.5 us (3%)
  local copies, waits for them, and re-layouts  8.05 us (2%)
    pallas_call x3, Pallas kernels, precondition_sweep(): pl.pallas_call(functools.partial(_precondition_kernel, n_sec, n_blk, plan...  229 us
    pallas_call x1, Pallas kernels, project(): pl.pallas_call(functools.partial(_project_kernel, stages, depth), out_sha...  29.9 us
    pallas_call x1, Pallas kernels, scan_maps(): pl.pallas_call(functools.partial(_maps_kernel, n, n_blk, rounds), out_sha...  22.6 us
    pallas_call x1, Pallas kernels, operator_exchange(): pl.pallas_call(functools.partial(_operator_kernel, n_sec, n_blk), out_sha...  22.1 us
    all_gather x1, blocking collectives, local(): lax.all_gather(back_panel, 'blk', axis=0, tiled=True)  12.7 us
    dot_general x4, matrix products, finish(): lax.dot_general(gathered, section_block, contract, preferred_element_type...  8.92 us

profile of v10, /device:TPU:1, one launch (start us, length us, event | category | flops | bytes accessed | tf_op | source)
XLA Modules:
  0.0 351.8 jit_solution(16204607321636236731)
XLA Ops:
  0.0 1.0 convert_element_type.21.x_ref
  1.7 0.8 fusion.9.be_ref
  2.6 0.8 fusion.40.up_ref
  3.4 22.1 %shard_map.82 = (bf16[128,2048]{1,0:T(8,128)(2,1)}, f32[128,128]{1,0:T(8,128)}, f32[16,128]{1,0:T(8,128)}) custom-call(bf16[128,256]{1,0:T(8,128)(2,1)} %copy-done.7, f32[128,128]{1,0:T(8,128)} %fusion.40.up_ref, f32[128,128]{1,0:T(8,128)} %fusion.9.be_ref), custom_call_target="tpu_custom_call" | custom-call | tf_op jit(solution)/shard_map/pallas_call | solution.py:468
  28.0 2.3 fusion.8.image_ref
  30.3 12.7 %all_gather.3 = bf16[2048,128]{1,0:T(8,128)(2,1)S(1)} all-gather(bf16[256,128]{1,0:T(8,128)(2,1)S(1)} %copy-done.4), channel_id=1, replica_groups=mesh['sec'=32,'blk'=8] {'blk'}, dimensions={0}, use_global_device_ids=true | all-gather | bytes 589824 | tf_op jit(solution)/shard_map/all_gather | solution.py:797
  43.4 0.8 convolution_negate_fusion.e_ref
  44.1 22.6 %shard_map.83.u_ref = f32[7,128,128]{2,1,0:T(8,128)} custom-call(f32[16,128]{1,0:T(8,128)} %convolution_negate_fusion.e_ref), custom_call_target="tpu_custom_call" | custom-call | tf_op jit(solution)/shard_map/pallas_call | solution.py:282
  67.4 72.8 %shard_map.84 = (f32[8,128]{1,0:T(8,128)}, f32[128,256]{1,0:T(8,128)}, f32[128,256]{1,0:T(8,128)}, bf16[128,2048]{1,0:T(8,128)(2,1)}, f32[128,128]{1,0:T(8,128)}, /*index=5*/f32[16,128]{1,0:T(8,128)}) custom-call(f32[1,128,256]{2,1,0:T(8,128)} %bitcast.122, f32[128,256]{1,0:T(8,128)} %fusion.8.image_ref, bf16[256,2048]{1,0:T(8,128)(2,1)} %inv_ref.5, ...), custom_call_target="tpu_custom_call" | custom-call | tf_op jit(solution)/shard_map/pallas_call | solution.py:582
  140.2 1.0 fusion.16
  142.1 2.2 fusion.5.image_ref
  144.3 75.1 %shard_map.85 = (f32[8,128]{1,0:T(8,128)}, f32[128,256]{1,0:T(8,128)}, f32[128,256]{1,0:T(8,128)}, bf16[128,2048]{1,0:T(8,128)(2,1)}, f32[128,128]{1,0:T(8,128)}, /*index=5*/f32[16,128]{1,0:T(8,128)}) custom-call(f32[1,128,256]{2,1,0:T(8,128)} %bitcast.119, f32[128,256]{1,0:T(8,128)} %fusion.5.image_ref, bf16[256,2048]{1,0:T(8,128)(2,1)} %inv_ref.5, ...), custom_call_target="tpu_custom_call" | custom-call | tf_op jit(solution)/shard_map/pallas_call | solution.py:582
  219.5 1.0 fusion.33
  221.4 2.2 fusion.3.image_ref
  223.6 0.7 pad_maximum_fusion.1.basis_ref
  224.4 80.8 %shard_map.86 = (f32[8,128]{1,0:T(8,128)}, f32[128,256]{1,0:T(8,128)}, f32[128,256]{1,0:T(8,128)}, bf16[128,2048]{1,0:T(8,128)(2,1)}, f32[128,128]{1,0:T(8,128)}, /*index=5*/f32[16,128]{1,0:T(8,128)}) custom-call(f32[2,128,256]{2,1,0:T(8,128)} %pad_maximum_fusion.1.basis_ref, f32[128,256]{1,0:T(8,128)} %fusion.3.image_ref, bf16[256,2048]{1,0:T(8,128)(2,1)} %inv_ref.5, ...), custom_call_target="tpu_custom_call" | custom-call | tf_op jit(solution)/shard_map/pallas_call | solution.py:582
  305.2 1.0 fusion.32
  307.1 2.2 fusion.1.image_ref
  309.4 0.8 pad_maximum_fusion.basis_ref
  310.1 29.9 %shard_map.87 = (f32[8,128]{1,0:T(8,128)}, f32[128,256]{1,0:T(8,128)}) custom-call(f32[3,128,256]{2,1,0:T(8,128)} %pad_maximum_fusion.basis_ref, f32[128,256]{1,0:T(8,128)} %fusion.1.image_ref), custom_call_target="tpu_custom_call" | custom-call | tf_op jit(solution)/shard_map/pallas_call | solution.py:741
  341.3 1.4 scatter.19
  345.7 3.3 broadcast_select_fusion
  349.0 2.0 fusion.20
  351.0 0.8 add_add_fusion
  (83 shorter events, 11.1 us)
Async XLA Ops:
  0.0 27.2 %copy-start = (bf16[256,2048]{1,0:T(8,128)(2,1)S(1)}, bf16[256,2048]{1,0:T(8,128)(2,1)}, u32[]{:S(2)}) copy-start(bf16[256,2048]{1,0:T(8,128)(2,1)} %param.49) | copy-start | bytes 3145732
  1.0 1.5 copy-start.7
  1.0 0.7 copy-start.20
  1.7 0.9 copy-start.6
  25.5 0.7 copy-start.18
  26.2 0.8 copy-start.4
  26.2 0.9 copy-start.15
  27.0 0.9 copy-start.2
  27.0 1.0 copy-start.12
  27.2 0.8 copy-start.17
  28.0 14.9 %copy-start.1 = (bf16[256,2048]{1,0:T(8,128)(2,1)S(1)}, bf16[256,2048]{1,0:T(8,128)(2,1)}, u32[]{:S(2)}) copy-start(bf16[256,2048]{1,0:T(8,128)(2,1)} %inv_ref.5) | copy-start | bytes 3145732
  43.4 23.4 %copy-start.3 = (f32[256,128]{1,0:T(8,128)}, f32[256,128]{1,0:T(8,128)S(1)}, u32[]{:S(2)}) copy-start(f32[256,128]{1,0:T(8,128)S(1)} %fusion.41.gain_ref) | copy-start | bytes 393220
  140.2 1.1 copy-start.19
  141.2 0.9 copy-start.8
  219.5 1.0 copy-start.16
  220.5 0.9 copy-start.9
  221.4 2.2 copy-start.5
  221.4 2.2 copy-start.11
  305.2 1.0 copy-start.14
  306.2 0.9 copy-start.10
  307.1 2.2 copy-start.13
  310.1 29.9 %copy-start.21 = (f32[8,128]{1,0:T(8,128)S(1)}, f32[8,128]{1,0:T(8,128)}, u32[]{:S(2)}) copy-start(f32[8,128]{1,0:T(8,128)} %get-tuple-element.269) | copy-start | bytes 12292
  341.3 1.4 copy-start.22

commit v11 on v10

--- a/solution.py
+++ b/solution.py
@@ -241,11 +241,10 @@
     pl.semaphore_wait(barrier, count)
 
 
-def _maps_kernel(n, n_blk, rounds, e_ref, a_ref, eslots, emat, current, slots, esend, erecv, sends, recvs):
+def _maps_body(n, n_blk, rounds, e_ref, a_ref, eslots, emat, current, slots, esend, erecv, sends, recvs):
     sec = lax.axis_index("sec")
     first = rounds[0][1]
     offsets = len(first) + 1
-    _greet_all(n, n_blk, offsets, rounds, False)
     _spread(n, n_blk, offsets, e_ref, eslots, esend, erecv)
     _assemble(n_blk, offsets, eslots, emat)
     joined = emat[0]
@@ -274,28 +273,88 @@
         flat += len(js)
 
 
-def scan_maps(e_piece, n, n_blk):
-    rounds = _plan(n)
+def _setup_kernel(
+    n_sec, n_blk, rounds, x_ref, up_ref, be_ref, back_ref, inv_ref, pick_ref,
+    g_ref, b_ref, a_ref, gain_ref, chain_ref, *scratch
+):
+    phase_scratch = scratch[:9]
+    pslots, psend, precv, epiece = scratch[9:13]
+    maps_scratch = scratch[13:]
+    sec, blk = lax.axis_index("sec"), lax.axis_index("blk")
+    offsets = len(rounds[0][1]) + 1
+    _greet_all(n_sec, n_blk, offsets, rounds, True)
+    piece = epiece.shape[0]
+    mine = be_ref.at[pl.ds(pl.multiple_of(blk * piece, 8), piece)]
+    _operator_phase(n_sec, n_blk, x_ref, up_ref, mine, g_ref, b_ref, a_ref, phase_scratch)
+
+    def blk_copy(k, target, slot):
+        return pltpu.make_async_remote_copy(
+            src_ref=back_ref,
+            dst_ref=pslots.at[slot],
+            send_sem=psend.at[k],
+            recv_sem=precv.at[slot],
+            device_id={"blk": target},
+            device_id_type=MESH,
+        )
+
+    outgoing = [blk_copy(k, lax.rem(blk + k, n_blk), blk) for k in range(1, n_blk)]
+    for copy in outgoing:
+        copy.start()
+    pslots[blk] = back_ref[...]
+    for k in range(1, n_blk):
+        sender = lax.rem(blk + k, n_blk)
+        blk_copy(k, sender, sender).wait_recv()
+    for copy in outgoing:
+        copy.wait_send()
+    rows = back_ref.shape[0]
+    gain = jnp.dot(inv_ref[:, 0:rows], pslots[0], preferred_element_type=jnp.float32)
+    for j in range(1, n_blk):
+        gain = gain + jnp.dot(
+            inv_ref[:, j * rows : (j + 1) * rows], pslots[j], preferred_element_type=jnp.float32
+        )
+    gain_ref[...] = gain
+    epiece[...] = -jnp.dot(
+        pick_ref[...], gain, precision=lax.Precision.HIGHEST, preferred_element_type=jnp.float32
+    )
+    _maps_body(n_sec, n_blk, rounds, epiece, chain_ref, *maps_scratch)
+
+
+def setup_exchange(x, up_t, be_t, back, inverse, picks, n_sec, n_blk):
+    cases, width = x.shape
+    panel, _ = up_t.shape
+    piece = panel // n_blk
+    rows, panel_width = back.shape
+    rounds = _plan(n_sec)
     total = sum(len(js) for _, js in rounds)
     offsets = len(rounds[0][1]) + 1
-    piece, width = e_piece.shape
     return pl.pallas_call(
-        functools.partial(_maps_kernel, n, n_blk, rounds),
-        out_shape=jax.ShapeDtypeStruct((total, width, width), jnp.float32),
-        in_specs=[pl.BlockSpec(memory_space=pltpu.VMEM)],
-        out_specs=pl.BlockSpec(memory_space=pltpu.VMEM),
-        scratch_shapes=[
-            pltpu.VMEM((offsets * n_blk, piece, width), jnp.float32),
-            pltpu.VMEM((offsets, width, width), jnp.float32),
-            pltpu.VMEM((width, width), jnp.float32),
-            pltpu.VMEM((total, width, width), jnp.float32),
+        functools.partial(_setup_kernel, n_sec, n_blk, rounds),
+        out_shape=(
+            jax.ShapeDtypeStruct((cases, n_blk * width), x.dtype),
+            jax.ShapeDtypeStruct((panel, cases), jnp.float32),
+            jax.ShapeDtypeStruct((piece, cases), jnp.float32),
+            jax.ShapeDtypeStruct((rows, panel_width), jnp.float32),
+            jax.ShapeDtypeStruct((total, panel_width, panel_width), jnp.float32),
+        ),
+        in_specs=[pl.BlockSpec(memory_space=pltpu.VMEM)] * 6,
+        out_specs=[pl.BlockSpec(memory_space=pltpu.VMEM)] * 5,
+        scratch_shapes=_operator_scratch(n_blk, cases, width, x.dtype, piece, cases)
+        + [
+            pltpu.VMEM((n_blk, rows, panel_width), back.dtype),
+            pltpu.SemaphoreType.DMA((n_blk,)),
+            pltpu.SemaphoreType.DMA((n_blk,)),
+            pltpu.VMEM((piece, panel_width), jnp.float32),
+            pltpu.VMEM((offsets * n_blk, piece, panel_width), jnp.float32),
+            pltpu.VMEM((offsets, panel_width, panel_width), jnp.float32),
+            pltpu.VMEM((panel_width, panel_width), jnp.float32),
+            pltpu.VMEM((total, panel_width, panel_width), jnp.float32),
             pltpu.SemaphoreType.DMA((offsets * n_blk,)),
             pltpu.SemaphoreType.DMA((offsets * n_blk,)),
             pltpu.SemaphoreType.DMA((total,)),
             pltpu.SemaphoreType.DMA((total,)),
         ],
-        compiler_params=pltpu.CompilerParams(collective_id=2, has_side_effects=True),
-    )(e_piece)
+        compiler_params=pltpu.CompilerParams(collective_id=3, has_side_effects=True),
+    )(x, up_t, be_t, back, inverse, picks)
 
 
 def _gather_kernel(n, x_ref, o_ref, slots, sends, recvs):
@@ -792,16 +851,9 @@
     first_row = lax.axis_index("blk") * node_rows
     selector = (indices[None, :] == first_row + jnp.arange(node_rows)[:, None]).astype(jnp.float32)
     contract = (((1,), (1,)), ((), ()))
-    gain_panel = jnp.dot(
-        block_inverse,
-        lax.all_gather(back_panel, "blk", axis=0, tiled=True),
-        preferred_element_type=jnp.float32,
-    )
 
     own_piece = panel_width // mesh_shape["blk"]
     own_picks = lax.dynamic_slice_in_dim(selector, lax.axis_index("blk") * own_piece, own_piece, 1).T
-    own_maps = -jnp.dot(own_picks, gain_panel, precision=highest)
-    chain = scan_maps(own_maps, mesh_shape["sec"], mesh_shape["blk"])
 
     def section_terms(dense_part, behind_vals, piece):
         width = piece.shape[1]
@@ -858,7 +910,25 @@
         return jnp.sqrt(global_sum(jnp.sum(vector * vector, axis=1)[None], mesh_shape)[0] + epsilon)
 
     bent = jnp.tanh(state_now)
-    residual = source - operator(state_now) - fan_gain[None, :] * bent
+    state_rounded = state_now.astype(jnp.bfloat16)
+    gathered, behind_t, ahead_piece, gain_panel, chain = setup_exchange(
+        state_rounded,
+        lax.dot_general(
+            ahead_panel, state_rounded, (((0,), (1,)), ((), ())), preferred_element_type=jnp.float32
+        ),
+        lax.dot_general(
+            selector.astype(jnp.bfloat16),
+            state_rounded,
+            (((0,), (1,)), ((), ())),
+            preferred_element_type=jnp.float32,
+        ),
+        back_panel,
+        block_inverse,
+        own_picks,
+        n_sec,
+        n_blk,
+    )
+    residual = source - finish(gathered, behind_t, ahead_piece) - fan_gain[None, :] * bent
     jac_diag = fan_gain[None, :] * (1.0 - bent * bent)
     hessen = jnp.zeros((cases, KRYLOV + 1, KRYLOV), jnp.float32)
     basis = []

time: 353 us -> 342 us (0.969)
  blocking collectives: 12.7 us -> 0 us
  Pallas kernels: 303 us -> 307 us
    all_gather x1 -> x0, blocking collectives: 12.7 us -> none  [local(): lax.all_gather(back_panel, 'blk', axis=0, tiled=True)]
    pallas_call x2 -> x1, Pallas kernels: 44.7 us -> 47.8 us  [setup_exchange(): pl.pallas_call(functools.partial(_setup_kernel, n_sec, n_blk, rounds), ou...]
where the time goes in v11:
time: 342 us; the launch traced here: 341 us
  Pallas kernels  307 us (90%)
  matrix products  15.3 us (4%)
  other arithmetic  11.2 us (3%)
  local copies, waits for them, and re-layouts  6.79 us (2%)
    pallas_call x3, Pallas kernels, precondition_sweep(): pl.pallas_call(functools.partial(_precondition_kernel, n_sec, n_blk, plan...  226 us
    pallas_call x1, Pallas kernels, setup_exchange(): pl.pallas_call(functools.partial(_setup_kernel, n_sec, n_blk, rounds), ou...  47.8 us
    pallas_call x1, Pallas kernels, project(): pl.pallas_call(functools.partial(_project_kernel, stages, depth), out_sha...  33 us
    dot_general x4, matrix products, finish(): lax.dot_general(gathered, section_block, contract, preferred_element_type...  8.83 us

profile of v11, /device:TPU:1, one launch (start us, length us, event | category | flops | bytes accessed | tf_op | source)
XLA Modules:
  0.0 340.9 jit_solution(2178167596443288549)
XLA Ops:
  0.0 0.9 broadcast_compare_fusion
  2.1 0.8 fusion.9.be_ref
  3.0 0.8 fusion.48.up_ref
  3.8 47.8 %shard_map.82 = (bf16[128,2048]{1,0:T(8,128)(2,1)}, f32[128,128]{1,0:T(8,128)}, f32[16,128]{1,0:T(8,128)}, f32[256,128]{1,0:T(8,128)}, f32[7,128,128]{2,1,0:T(8,128)}) custom-call(bf16[128,256]{1,0:T(8,128)(2,1)} %copy-done.5, f32[128,128]{1,0:T(8,128)} %fusion.48.up_ref, f32[128,128]{1,0:T(8,128)} %fusion.9.be_ref, bf16[256,128]{1,0:T(8,128)(2,1)} %back_ref.1, ...), custom_call_target="tpu_custom_call" | custom-call | tf_op jit(solution)/shard_map/pallas_call | solution.py:330
  51.7 1.0 fusion.26
  53.6 2.2 fusion.8.image_ref
  55.8 68.5 %shard_map.83 = (f32[8,128]{1,0:T(8,128)}, f32[128,256]{1,0:T(8,128)}, f32[128,256]{1,0:T(8,128)}, bf16[128,2048]{1,0:T(8,128)(2,1)}, f32[128,128]{1,0:T(8,128)}, /*index=5*/f32[16,128]{1,0:T(8,128)}) custom-call(f32[1,128,256]{2,1,0:T(8,128)} %bitcast.119, f32[128,256]{1,0:T(8,128)} %fusion.8.image_ref, bf16[256,2048]{1,0:T(8,128)(2,1)} %inv_ref.7, ...), custom_call_target="tpu_custom_call" | custom-call | tf_op jit(solution)/shard_map/pallas_call | solution.py:641
  124.4 1.0 fusion.16
  126.3 2.2 fusion.5.image_ref
  128.5 76.9 %shard_map.84 = (f32[8,128]{1,0:T(8,128)}, f32[128,256]{1,0:T(8,128)}, f32[128,256]{1,0:T(8,128)}, bf16[128,2048]{1,0:T(8,128)(2,1)}, f32[128,128]{1,0:T(8,128)}, /*index=5*/f32[16,128]{1,0:T(8,128)}) custom-call(f32[1,128,256]{2,1,0:T(8,128)} %bitcast.116, f32[128,256]{1,0:T(8,128)} %fusion.5.image_ref, bf16[256,2048]{1,0:T(8,128)(2,1)} %inv_ref.7, ...), custom_call_target="tpu_custom_call" | custom-call | tf_op jit(solution)/shard_map/pallas_call | solution.py:641
  205.5 1.0 fusion.22
  206.7 0.7 copy-done.7
  207.4 2.2 fusion.3.image_ref
  209.6 0.7 pad_maximum_fusion.1.basis_ref
  210.4 80.9 %shard_map.85 = (f32[8,128]{1,0:T(8,128)}, f32[128,256]{1,0:T(8,128)}, f32[128,256]{1,0:T(8,128)}, bf16[128,2048]{1,0:T(8,128)(2,1)}, f32[128,128]{1,0:T(8,128)}, /*index=5*/f32[16,128]{1,0:T(8,128)}) custom-call(f32[2,128,256]{2,1,0:T(8,128)} %pad_maximum_fusion.1.basis_ref, f32[128,256]{1,0:T(8,128)} %fusion.3.image_ref, bf16[256,2048]{1,0:T(8,128)(2,1)} %inv_ref.7, ...), custom_call_target="tpu_custom_call" | custom-call | tf_op jit(solution)/shard_map/pallas_call | solution.py:641
  291.3 1.0 fusion.20
  293.2 2.2 fusion.1.image_ref
  295.4 0.8 pad_maximum_fusion.basis_ref
  296.2 33.0 %shard_map.86 = (f32[8,128]{1,0:T(8,128)}, f32[128,256]{1,0:T(8,128)}) custom-call(f32[3,128,256]{2,1,0:T(8,128)} %pad_maximum_fusion.basis_ref, f32[128,256]{1,0:T(8,128)} %fusion.1.image_ref), custom_call_target="tpu_custom_call" | custom-call | tf_op jit(solution)/shard_map/pallas_call | solution.py:800
  330.5 1.4 scatter.19
  333.4 0.7 compare_reduce_fusion.1
  334.8 3.2 broadcast_select_fusion
  338.1 2.0 fusion.32
  340.1 0.8 add_add_fusion
  (73 shorter events, 7.6 us)
Async XLA Ops:
  0.0 52.9 %copy-start = (bf16[256,2048]{1,0:T(8,128)(2,1)S(1)}, bf16[256,2048]{1,0:T(8,128)(2,1)}, u32[]{:S(2)}) copy-start(bf16[256,2048]{1,0:T(8,128)(2,1)} %param.49) | copy-start | bytes 3145732
  0.0 1.5 copy-start.1
  1.5 0.7 copy-start.17
  2.1 0.8 copy-start.5
  2.1 0.9 copy-start.4
  51.7 1.0 copy-start.2
  51.7 1.0 copy-start.13
  52.7 0.9 copy-start.10
  52.9 0.7 copy-start.15
  124.3 1.1 copy-start.16
  125.4 0.9 copy-start.6
  205.4 1.0 copy-start.14
  206.5 0.9 copy-start.7
  207.4 2.2 copy-start.3
  207.4 2.2 copy-start.9
  291.3 1.0 copy-start.12
  292.3 0.9 copy-start.8
  293.2 2.2 copy-start.11
  296.2 33.0 %copy-start.18 = (f32[8,128]{1,0:T(8,128)S(1)}, f32[8,128]{1,0:T(8,128)}, u32[]{:S(2)}) copy-start(f32[8,128]{1,0:T(8,128)} %get-tuple-element.273) | copy-start | bytes 12292
  330.5 1.4 copy-start.19

commit v12 on v11

--- a/solution.py
+++ b/solution.py
@@ -810,35 +810,32 @@
     )(stacked, image)
 
 
-def least_squares(hessen, beta):
-    cases = hessen.shape[0]
-    depth = hessen.shape[2]
-    rhs = jnp.zeros((cases, depth + 1), jnp.float32).at[:, 0].set(beta)
-    upper = hessen
+def least_squares(columns, beta, depth):
+    zero = jnp.zeros_like(beta)
+    upper = [
+        [columns[j][i] if i <= j + 1 else zero for j in range(depth)] for i in range(depth + 1)
+    ]
+    rhs = [beta] + [zero] * depth
     for column in range(depth):
-        upper_row = upper[:, column, :]
-        lower_row = upper[:, column + 1, :]
-        radius = jnp.sqrt(upper_row[:, column] ** 2 + lower_row[:, column] ** 2)
-        cosine = upper_row[:, column] / radius
-        sine_term = lower_row[:, column] / radius
-        upper = upper.at[:, column, :].set(
-            cosine[:, None] * upper_row + sine_term[:, None] * lower_row
-        )
-        upper = upper.at[:, column + 1, :].set(
-            -sine_term[:, None] * upper_row + cosine[:, None] * lower_row
-        )
-        first_rhs = rhs[:, column]
-        second_rhs = rhs[:, column + 1]
-        rhs = rhs.at[:, column].set(cosine * first_rhs + sine_term * second_rhs)
-        rhs = rhs.at[:, column + 1].set(-sine_term * first_rhs + cosine * second_rhs)
-    weights = jnp.zeros((cases, depth), jnp.float32)
+        upper_row, lower_row = upper[column], upper[column + 1]
+        radius = jnp.sqrt(upper_row[column] ** 2 + lower_row[column] ** 2)
+        cosine = upper_row[column] / radius
+        sine_term = lower_row[column] / radius
+        upper[column] = [cosine * a + sine_term * b for a, b in zip(upper_row, lower_row)]
+        upper[column + 1] = [-sine_term * a + cosine * b for a, b in zip(upper_row, lower_row)]
+        first_rhs, second_rhs = rhs[column], rhs[column + 1]
+        rhs[column] = cosine * first_rhs + sine_term * second_rhs
+        rhs[column + 1] = -sine_term * first_rhs + cosine * second_rhs
+    weights = [zero] * depth
     for column in reversed(range(depth)):
-        remain = rhs[:, column] - jnp.sum(
-            upper[:, column, column + 1 :] * weights[:, column + 1 :], axis=1
-        )
-        weights = weights.at[:, column].set(remain / upper[:, column, column])
+        remain = rhs[column]
+        if column + 1 < depth:
+            tail = upper[column][column + 1] * weights[column + 1]
+            for k in range(column + 2, depth):
+                tail = tail + upper[column][k] * weights[k]
+            remain = remain - tail
+        weights[column] = remain / upper[column][column]
     return weights
-
 
 def local(
     mesh_shape,
@@ -930,7 +927,7 @@
     )
     residual = source - finish(gathered, behind_t, ahead_piece) - fan_gain[None, :] * bent
     jac_diag = fan_gain[None, :] * (1.0 - bent * bent)
-    hessen = jnp.zeros((cases, KRYLOV + 1, KRYLOV), jnp.float32)
+    columns = []
     basis = []
     directions = []
     product = residual
@@ -944,16 +941,16 @@
         if column == 0:
             beta = sums[0]
         else:
-            hessen = hessen.at[:, : column + 1, column - 1].set(sums[: column + 1].T)
+            columns.append(sums[: column + 1])
         basis.append(following)
         directions.append(direction)
         product = finish(gathered, behind_t, ahead_piece) + jac_diag * direction
     sums, _ = project(jnp.stack(basis), product, mesh_shape)
-    hessen = hessen.at[:, : KRYLOV + 1, KRYLOV - 1].set(sums[: KRYLOV + 1].T)
-    weights = least_squares(hessen, beta)
+    columns.append(sums[: KRYLOV + 1])
+    weights = least_squares(columns, beta, KRYLOV)
     update = jnp.zeros_like(state_now)
     for column in range(KRYLOV):
-        update = update + weights[:, column : column + 1] * directions[column]
+        update = update + weights[column][:, None] * directions[column]
     return state_now + update
 
 

time: 342 us -> 331 us (0.968)
  other arithmetic: 11.2 us -> 5.3 us
where the time goes in v12:
time: 331 us; the launch traced here: 330 us
  Pallas kernels  307 us (93%)
  matrix products  13.8 us (4%)
  other arithmetic  5.3 us (2%)
  local copies, waits for them, and re-layouts  3.81 us (1%)
    pallas_call x3, Pallas kernels, precondition_sweep(): pl.pallas_call(functools.partial(_precondition_kernel, n_sec, n_blk, plan...  227 us
    pallas_call x1, Pallas kernels, setup_exchange(): pl.pallas_call(functools.partial(_setup_kernel, n_sec, n_blk, rounds), ou...  47.8 us
    pallas_call x1, Pallas kernels, project(): pl.pallas_call(functools.partial(_project_kernel, stages, depth), out_sha...  32.7 us
    dot_general x4, matrix products, finish(): lax.dot_general(gathered, section_block, contract, preferred_element_type...  7.76 us

profile of v12, /device:TPU:1, one launch (start us, length us, event | category | flops | bytes accessed | tf_op | source)
XLA Modules:
  0.0 330.3 jit_solution(14828507262014713665)
XLA Ops:
  0.0 1.0 convert_element_type.21.x_ref
  1.1 0.8 fusion.9.be_ref
  1.9 0.8 fusion.62.up_ref
  2.8 0.6 dynamic-slice_bitcast_fusion.pick_ref
  3.4 47.8 %shard_map.82 = (bf16[128,2048]{1,0:T(8,128)(2,1)}, f32[128,128]{1,0:T(8,128)}, f32[16,128]{1,0:T(8,128)}, f32[256,128]{1,0:T(8,128)}, f32[7,128,128]{2,1,0:T(8,128)}) custom-call(bf16[128,256]{1,0:T(8,128)(2,1)} %copy-done.5, f32[128,128]{1,0:T(8,128)} %fusion.62.up_ref, f32[128,128]{1,0:T(8,128)} %fusion.9.be_ref, bf16[256,128]{1,0:T(8,128)(2,1)} %back_ref.1, ...), custom_call_target="tpu_custom_call" | custom-call | tf_op jit(solution)/shard_map/pallas_call | solution.py:330
  51.3 1.1 fusion.18
  52.7 0.6 copy-done.1
  53.3 2.2 fusion.8.image_ref
  55.5 68.5 %shard_map.83 = (f32[8,128]{1,0:T(8,128)}, f32[128,256]{1,0:T(8,128)}, f32[128,256]{1,0:T(8,128)}, bf16[128,2048]{1,0:T(8,128)(2,1)}, f32[128,128]{1,0:T(8,128)}, /*index=5*/f32[16,128]{1,0:T(8,128)}) custom-call(f32[1,128,256]{2,1,0:T(8,128)} %bitcast.222, f32[128,256]{1,0:T(8,128)} %fusion.8.image_ref, bf16[256,2048]{1,0:T(8,128)(2,1)} %inv_ref.7, ...), custom_call_target="tpu_custom_call" | custom-call | tf_op jit(solution)/shard_map/pallas_call | solution.py:641
  124.0 1.0 fusion.16
  125.4 0.6 copy-done.6
  126.0 2.2 fusion.5.image_ref
  128.2 76.9 %shard_map.84 = (f32[8,128]{1,0:T(8,128)}, f32[128,256]{1,0:T(8,128)}, f32[128,256]{1,0:T(8,128)}, bf16[128,2048]{1,0:T(8,128)(2,1)}, f32[128,128]{1,0:T(8,128)}, /*index=5*/f32[16,128]{1,0:T(8,128)}) custom-call(f32[1,128,256]{2,1,0:T(8,128)} %bitcast.219, f32[128,256]{1,0:T(8,128)} %fusion.5.image_ref, bf16[256,2048]{1,0:T(8,128)(2,1)} %inv_ref.7, ...), custom_call_target="tpu_custom_call" | custom-call | tf_op jit(solution)/shard_map/pallas_call | solution.py:641
  205.1 1.0 fusion.14
  206.4 0.6 copy-done.7
  207.1 2.2 fusion.3.image_ref
  209.3 0.7 pad_maximum_fusion.1.basis_ref
  210.0 81.1 %shard_map.85 = (f32[8,128]{1,0:T(8,128)}, f32[128,256]{1,0:T(8,128)}, f32[128,256]{1,0:T(8,128)}, bf16[128,2048]{1,0:T(8,128)(2,1)}, f32[128,128]{1,0:T(8,128)}, /*index=5*/f32[16,128]{1,0:T(8,128)}) custom-call(f32[2,128,256]{2,1,0:T(8,128)} %pad_maximum_fusion.1.basis_ref, f32[128,256]{1,0:T(8,128)} %fusion.3.image_ref, bf16[256,2048]{1,0:T(8,128)(2,1)} %inv_ref.7, ...), custom_call_target="tpu_custom_call" | custom-call | tf_op jit(solution)/shard_map/pallas_call | solution.py:641
  291.2 1.8 pad_maximum_fusion.basis_ref
  294.0 0.7 copy-done.8
  294.7 1.1 fusion.1.image_ref
  295.8 32.7 %shard_map.86 = (f32[8,128]{1,0:T(8,128)}, f32[128,256]{1,0:T(8,128)}) custom-call(f32[3,128,256]{2,1,0:T(8,128)} %pad_maximum_fusion.basis_ref, f32[128,256]{1,0:T(8,128)} %fusion.1.image_ref), custom_call_target="tpu_custom_call" | custom-call | tf_op jit(solution)/shard_map/pallas_call | solution.py:800
  328.6 1.0 fusion.49
  329.5 0.8 add_add_fusion
  (41 shorter events, 2.0 us)
Async XLA Ops:
  0.0 52.7 %copy-start = (bf16[256,2048]{1,0:T(8,128)(2,1)S(1)}, bf16[256,2048]{1,0:T(8,128)(2,1)}, u32[]{:S(2)}) copy-start(bf16[256,2048]{1,0:T(8,128)(2,1)} %param.11) | copy-start | bytes 3145732
  0.0 1.0 copy-start.18
  1.0 0.9 copy-start.5
  1.0 0.9 copy-start.4
  3.4 47.8 %copy-start.2 = (bf16[256,128]{1,0:T(8,128)(2,1)S(1)}, bf16[256,128]{1,0:T(8,128)(2,1)}, u32[]{:S(2)}) copy-start(bf16[256,128]{1,0:T(8,128)(2,1)} %back_ref.1) | copy-start | bytes 196612
  51.3 1.1 copy-start.15
  51.3 1.4 copy-start.11
  52.4 0.9 copy-start.1
  52.4 0.9 copy-start.13
  124.0 1.0 copy-start.16
  125.1 0.9 copy-start.6
  205.1 1.0 copy-start.17
  206.1 0.9 copy-start.7
  207.1 2.2 copy-start.3
  207.1 2.2 copy-start.10
  291.2 1.8 copy-start.14
  291.2 2.8 copy-start.9
  292.9 0.8 copy-start.12
  293.8 0.9 copy-start.8

commit v13 on v12

--- a/solution.py
+++ b/solution.py
@@ -540,12 +540,14 @@
 
 def _precondition_kernel(
     n_sec, n_blk, rounds, stages, depth, basis_ref, image_ref, inv_ref, pick_ref, u_ref,
-    gain_ref, ahead_ref, h_ref, next_ref, d_ref, g_ref, b_ref, a_ref, *scratch
+    gain_ref, ahead_ref, block_ref, back_ref, spread_ref, jac_ref,
+    h_ref, next_ref, d_ref, p_ref, *scratch
 ):
     gslots, fpiece, fslots, fmat, carry, slots, gsend, grecv, fsend, frecv, ssend, srecv = scratch[:12]
     rounded, upward, own_piece, x_ref = scratch[12:16]
-    phase_scratch = scratch[16:25]
-    project_scratch = scratch[25:]
+    g_ref, b_ref, a_ref = scratch[16:19]
+    phase_scratch = scratch[19:28]
+    project_scratch = scratch[28:]
     sec, blk = lax.axis_index("sec"), lax.axis_index("blk")
     first = rounds[0][1]
     offsets = len(first) + 1
@@ -625,9 +627,28 @@
         precision=lax.Precision.HIGHEST, preferred_element_type=jnp.float32,
     )
     _operator_phase(n_sec, n_blk, rounded, upward, own_piece, g_ref, b_ref, a_ref, phase_scratch)
-
-
-def precondition_sweep(basis, image, inverse, picks, chain, gain, ahead, mesh_shape, depth):
+    product = jac_ref[...] * direction
+    for j in range(n_blk):
+        product = product + lax.dot_general(
+            g_ref[:, j * width : (j + 1) * width],
+            block_ref[:, j * width : (j + 1) * width],
+            contract,
+            preferred_element_type=jnp.float32,
+        )
+    product = product + lax.dot_general(
+        b_ref[...].T.astype(back_ref.dtype), back_ref[...], contract,
+        preferred_element_type=jnp.float32,
+    )
+    product = product + jnp.dot(
+        spread_ref[...], a_ref[...], precision=lax.Precision.HIGHEST,
+        preferred_element_type=jnp.float32,
+    ).T
+    p_ref[...] = product
+
+
+def precondition_sweep(
+    basis, image, inverse, picks, chain, gain, ahead, block, back, spread, jac, mesh_shape, depth
+):
     n_sec, n_blk = mesh_shape["sec"], mesh_shape["blk"]
     stages = _global_stages(mesh_shape)
     cases, width = image.shape
@@ -644,12 +665,10 @@
             jax.ShapeDtypeStruct((8, cases), jnp.float32),
             jax.ShapeDtypeStruct((cases, width), jnp.float32),
             jax.ShapeDtypeStruct((cases, width), jnp.float32),
-            jax.ShapeDtypeStruct((cases, n_blk * width), dtype),
-            jax.ShapeDtypeStruct((panel, cases), jnp.float32),
-            jax.ShapeDtypeStruct((piece, cases), jnp.float32),
+            jax.ShapeDtypeStruct((cases, width), jnp.float32),
         ),
-        in_specs=[pl.BlockSpec(memory_space=pltpu.VMEM)] * 7,
-        out_specs=[pl.BlockSpec(memory_space=pltpu.VMEM)] * 6,
+        in_specs=[pl.BlockSpec(memory_space=pltpu.VMEM)] * 11,
+        out_specs=[pl.BlockSpec(memory_space=pltpu.VMEM)] * 4,
         scratch_shapes=[
             pltpu.VMEM((n_blk, cases, width), dtype),
             pltpu.VMEM((piece, cases), jnp.float32),
@@ -667,11 +686,14 @@
             pltpu.VMEM((panel, cases), jnp.float32),
             pltpu.VMEM((piece, cases), jnp.float32),
             pltpu.VMEM((cases, width), dtype),
+            pltpu.VMEM((cases, n_blk * width), dtype),
+            pltpu.VMEM((panel, cases), jnp.float32),
+            pltpu.VMEM((piece, cases), jnp.float32),
         ]
         + _operator_scratch(n_blk, cases, width, dtype, piece, cases)
         + _project_scratch(stages, cases),
         compiler_params=pltpu.CompilerParams(collective_id=10 + depth, has_side_effects=True),
-    )(basis, image, inverse, picks, chain, gain, ahead)
+    )(basis, image, inverse, picks, chain, gain, ahead, block, back, spread, jac)
 
 
 def _exchange_sum(stages, source, slots, partial, sends, recvs, out):
@@ -934,9 +956,9 @@
     beta = None
     for column in range(KRYLOV):
         stacked = jnp.stack(basis) if basis else residual[None]
-        sums, following, direction, gathered, behind_t, ahead_piece = precondition_sweep(
+        sums, following, direction, product = precondition_sweep(
             stacked, product, block_inverse, own_picks, chain, gain_panel, ahead_panel,
-            mesh_shape, len(basis),
+            section_block, back_panel, local_picks, jac_diag, mesh_shape, len(basis),
         )
         if column == 0:
             beta = sums[0]
@@ -944,7 +966,6 @@
             columns.append(sums[: column + 1])
         basis.append(following)
         directions.append(direction)
-        product = finish(gathered, behind_t, ahead_piece) + jac_diag * direction
     sums, _ = project(jnp.stack(basis), product, mesh_shape)
     columns.append(sums[: KRYLOV + 1])
     weights = least_squares(columns, beta, KRYLOV)

time: 331 us -> 325 us (0.982)
  matrix products: 13.8 us -> 4.41 us
    dot_general x4 -> x1, matrix products: 7.76 us -> 2.19 us  [finish(): lax.dot_general(gathered, section_block, contract, preferred_element_type...]
where the time goes in v13:
time: 325 us; the launch traced here: 324 us
  Pallas kernels  310 us (95%)
  other arithmetic  5.76 us (2%)
  matrix products  4.41 us (1%)
  local copies, waits for them, and re-layouts  4.39 us (1%)
    pallas_call x3, Pallas kernels, precondition_sweep(): pl.pallas_call(functools.partial(_precondition_kernel, n_sec, n_blk, plan...  229 us
    pallas_call x1, Pallas kernels, setup_exchange(): pl.pallas_call(functools.partial(_setup_kernel, n_sec, n_blk, rounds), ou...  47.8 us
    pallas_call x1, Pallas kernels, project(): pl.pallas_call(functools.partial(_project_kernel, stages, depth), out_sha...  33.1 us

profile of v13, /device:TPU:1, one launch (start us, length us, event | category | flops | bytes accessed | tf_op | source)
XLA Modules:
  0.0 324.3 jit_solution(10798625050364412248)
XLA Ops:
  0.0 0.6 copy-done.14
  0.7 0.1 broadcast_compare_fusion
  0.8 0.8 constant_dynamic-slice_fusion.spread_ref
  1.5 0.1 fusion.49
  1.7 0.7 copy.9.pick_ref
  2.3 0.2 copy-done.2
  2.6 0.7 subtract_multiply_fusion
  3.2 0.9 fusion.5.be_ref
  4.2 0.8 fusion.41.up_ref
  5.0 47.8 %shard_map.82 = (bf16[128,2048]{1,0:T(8,128)(2,1)}, f32[128,128]{1,0:T(8,128)}, f32[16,128]{1,0:T(8,128)}, f32[256,128]{1,0:T(8,128)}, f32[7,128,128]{2,1,0:T(8,128)}) custom-call(bf16[128,256]{1,0:T(8,128)(2,1)} %copy-done.5, f32[128,128]{1,0:T(8,128)} %fusion.41.up_ref, f32[128,128]{1,0:T(8,128)} %fusion.5.be_ref, bf16[256,128]{1,0:T(8,128)(2,1)} %back_ref.7, ...), custom_call_target="tpu_custom_call" | custom-call | tf_op jit(solution)/shard_map/pallas_call | solution.py:330
  52.8 0.7 copy-done.12
  53.5 0.3 fusion.3
  53.8 0.5 copy-done.1
  54.4 0.2 fusion.8
  54.6 0.7 copy-done.7
  55.3 2.2 fusion.2.image_ref
  57.5 69.3 %shard_map.83 = (f32[8,128]{1,0:T(8,128)}, f32[128,256]{1,0:T(8,128)}, f32[128,256]{1,0:T(8,128)}, f32[128,256]{1,0:T(8,128)}) custom-call(f32[1,128,256]{2,1,0:T(8,128)} %bitcast.207, f32[128,256]{1,0:T(8,128)} %fusion.2.image_ref, bf16[256,2048]{1,0:T(8,128)(2,1)} %inv_ref.7, f32[16,256]{1,0:T(8,128)} %copy.9.pick_ref, ...), custom_call_target="tpu_custom_call" | custom-call | tf_op jit(solution)/shard_map/pallas_call | solution.py:662
  126.8 77.6 %shard_map.84 = (f32[8,128]{1,0:T(8,128)}, f32[128,256]{1,0:T(8,128)}, f32[128,256]{1,0:T(8,128)}, f32[128,256]{1,0:T(8,128)}) custom-call(f32[1,128,256]{2,1,0:T(8,128)} %bitcast.208, f32[128,256]{1,0:T(8,128)} %get-tuple-element.29.image_ref, bf16[256,2048]{1,0:T(8,128)(2,1)} %inv_ref.7, f32[16,256]{1,0:T(8,128)} %copy.9.pick_ref, ...), custom_call_target="tpu_custom_call" | custom-call | tf_op jit(solution)/shard_map/pallas_call | solution.py:662
  204.4 1.6 pad_maximum_fusion.1.basis_ref
  206.0 81.7 %shard_map.85 = (f32[8,128]{1,0:T(8,128)}, f32[128,256]{1,0:T(8,128)}, f32[128,256]{1,0:T(8,128)}, f32[128,256]{1,0:T(8,128)}) custom-call(f32[2,128,256]{2,1,0:T(8,128)} %pad_maximum_fusion.1.basis_ref, f32[128,256]{1,0:T(8,128)} %get-tuple-element.33.image_ref, bf16[256,2048]{1,0:T(8,128)(2,1)} %inv_ref.7, f32[16,256]{1,0:T(8,128)} %copy.9.pick_ref, ...), custom_call_target="tpu_custom_call" | custom-call | tf_op jit(solution)/shard_map/pallas_call | solution.py:662
  287.8 1.7 pad_maximum_fusion.basis_ref
  289.5 33.1 %shard_map.86 = (f32[8,128]{1,0:T(8,128)}, f32[128,256]{1,0:T(8,128)}) custom-call(f32[3,128,256]{2,1,0:T(8,128)} %pad_maximum_fusion.basis_ref, f32[128,256]{1,0:T(8,128)} %get-tuple-element.36.image_ref), custom_call_target="tpu_custom_call" | custom-call | tf_op jit(solution)/shard_map/pallas_call | solution.py:822
  322.6 0.9 fusion.31
  323.5 0.8 add_add_fusion
  (26 shorter events, 0.1 us)
Async XLA Ops:
  0.0 0.7 copy-start.14
  1.6 0.9 copy-start.2
  1.6 0.9 copy-start.13
  2.6 1.6 copy-start.4
  3.2 0.9 copy-start.5
  3.2 51.3 %copy-start = (bf16[256,2048]{1,0:T(8,128)(2,1)S(1)}, bf16[256,2048]{1,0:T(8,128)(2,1)}, u32[]{:S(2)}) copy-start(bf16[256,2048]{1,0:T(8,128)(2,1)} %block_ref.5) | copy-start | bytes 3145732
  52.8 0.7 copy-start.12
  53.5 0.8 copy-start.1
  53.5 0.9 copy-start.11
  54.4 0.9 copy-start.7
  126.8 77.6 %copy-start.3 = (f32[128,256]{1,0:T(8,128)S(1)}, f32[128,256]{1,0:T(8,128)}, u32[]{:S(2)}) copy-start(f32[128,256]{1,0:T(8,128)} %get-tuple-element.28) | copy-start | bytes 393220
  206.0 81.8 %copy-start.6 = (f32[128,256]{1,0:T(8,128)S(1)}, f32[128,256]{1,0:T(8,128)}, u32[]{:S(2)}) copy-start(f32[128,256]{1,0:T(8,128)} %get-tuple-element.32) | copy-start | bytes 393220
  289.4 34.0 %copy-start.8 = (f32[128,256]{1,0:T(8,128)S(1)}, f32[128,256]{1,0:T(8,128)}, u32[]{:S(2)}) copy-start(f32[128,256]{1,0:T(8,128)} %get-tuple-element.38) | copy-start | bytes 393220
  289.5 34.0 %copy-start.9 = (f32[128,256]{1,0:T(8,128)S(1)}, f32[128,256]{1,0:T(8,128)}, u32[]{:S(2)}) copy-start(f32[128,256]{1,0:T(8,128)} %get-tuple-element.39) | copy-start | bytes 393220
  289.5 34.1 %copy-start.10 = (f32[128,256]{1,0:T(8,128)S(1)}, f32[128,256]{1,0:T(8,128)}, u32[]{:S(2)}) copy-start(f32[128,256]{1,0:T(8,128)} %get-tuple-element.40) | copy-start | bytes 393220

commit v14 on v13

--- a/solution.py
+++ b/solution.py
@@ -538,11 +538,11 @@
     )(x, up_t, be_t)
 
 
-def _precondition_kernel(
-    n_sec, n_blk, rounds, stages, depth, basis_ref, image_ref, inv_ref, pick_ref, u_ref,
-    gain_ref, ahead_ref, block_ref, back_ref, spread_ref, jac_ref,
-    h_ref, next_ref, d_ref, p_ref, *scratch
-):
+def _precondition_kernel(n_sec, n_blk, rounds, stages, depth, *refs):
+    basis_refs = refs[:depth]
+    (image_ref, inv_ref, pick_ref, u_ref, gain_ref, ahead_ref, block_ref, back_ref, spread_ref,
+     jac_ref, h_ref, next_ref, d_ref, p_ref) = refs[depth : depth + 14]
+    scratch = refs[depth + 14 :]
     gslots, fpiece, fslots, fmat, carry, slots, gsend, grecv, fsend, frecv, ssend, srecv = scratch[:12]
     rounded, upward, own_piece, x_ref = scratch[12:16]
     g_ref, b_ref, a_ref = scratch[16:19]
@@ -552,7 +552,7 @@
     first = rounds[0][1]
     offsets = len(first) + 1
     _greet_all(n_sec, n_blk, offsets, rounds, True, stages)
-    _project_body(stages, depth, basis_ref, image_ref, h_ref, next_ref, project_scratch)
+    _project_body(stages, depth, basis_refs, image_ref, h_ref, next_ref, project_scratch)
     x_ref[...] = next_ref[...].astype(x_ref.dtype)
 
     def blk_copy(k, target, slot):
@@ -667,7 +667,7 @@
             jax.ShapeDtypeStruct((cases, width), jnp.float32),
             jax.ShapeDtypeStruct((cases, width), jnp.float32),
         ),
-        in_specs=[pl.BlockSpec(memory_space=pltpu.VMEM)] * 11,
+        in_specs=[pl.BlockSpec(memory_space=pltpu.VMEM)] * (depth + 10),
         out_specs=[pl.BlockSpec(memory_space=pltpu.VMEM)] * 4,
         scratch_shapes=[
             pltpu.VMEM((n_blk, cases, width), dtype),
@@ -693,7 +693,7 @@
         + _operator_scratch(n_blk, cases, width, dtype, piece, cases)
         + _project_scratch(stages, cases),
         compiler_params=pltpu.CompilerParams(collective_id=10 + depth, has_side_effects=True),
-    )(basis, image, inverse, picks, chain, gain, ahead, block, back, spread, jac)
+    )(*basis, image, inverse, picks, chain, gain, ahead, block, back, spread, jac)
 
 
 def _exchange_sum(stages, source, slots, partial, sends, recvs, out):
@@ -746,7 +746,7 @@
     return buffers() + buffers() + [pltpu.VMEM((8, cases), jnp.float32)] * 2
 
 
-def _project_body(stages, depth, basis_ref, image_ref, h_ref, next_ref, scratch):
+def _project_body(stages, depth, basis_refs, image_ref, h_ref, next_ref, scratch):
     count = len(stages)
     first, second = scratch[: 3 * count + 1], scratch[3 * count + 1 : 6 * count + 2]
     rows, work = scratch[6 * count + 2 : 6 * count + 4]
@@ -770,7 +770,7 @@
         rows[...] = jnp.zeros_like(rows)
         for i in range(depth):
             summed = lax.dot_general(
-                ones, image * basis_ref[i], contract, precision=highest,
+                ones, image * basis_refs[i][...], contract, precision=highest,
                 preferred_element_type=jnp.float32,
             )
             rows[i : i + 1, :] = summed[0:1, :]
@@ -779,7 +779,7 @@
             eye, h_ref[...], contract, precision=highest, preferred_element_type=jnp.float32
         )
         for i in range(depth):
-            image = image - columns[:, i : i + 1] * basis_ref[i]
+            image = image - columns[:, i : i + 1] * basis_refs[i][...]
     else:
         h_ref[...] = jnp.zeros_like(h_ref)
     work[...] = lax.dot_general(
@@ -806,18 +806,21 @@
     return peers
 
 
-def _project_kernel(stages, depth, basis_ref, image_ref, h_ref, next_ref, *scratch):
+def _project_kernel(stages, depth, *refs):
+    basis_refs = refs[:depth]
+    image_ref, h_ref, next_ref = refs[depth : depth + 3]
     barrier = pltpu.get_barrier_semaphore()
     pl.semaphore_wait(barrier, _signal_stages(barrier, stages))
-    _project_body(stages, depth, basis_ref, image_ref, h_ref, next_ref, scratch)
+    _project_body(stages, depth, basis_refs, image_ref, h_ref, next_ref, refs[depth + 3 :])
 
 
 def _global_stages(mesh_shape):
     return tuple((axis, mesh_shape[axis]) for axis in ("blk", "sec") if mesh_shape[axis] > 1)
 
 
-def project(stacked, image, mesh_shape):
-    depth, cases, width = stacked.shape
+def project(basis, image, mesh_shape):
+    depth = len(basis)
+    cases, width = image.shape
     stages = _global_stages(mesh_shape)
     return pl.pallas_call(
         functools.partial(_project_kernel, stages, depth),
@@ -825,11 +828,11 @@
             jax.ShapeDtypeStruct((8, cases), jnp.float32),
             jax.ShapeDtypeStruct((cases, width), jnp.float32),
         ),
-        in_specs=[pl.BlockSpec(memory_space=pltpu.VMEM)] * 2,
+        in_specs=[pl.BlockSpec(memory_space=pltpu.VMEM)] * (depth + 1),
         out_specs=[pl.BlockSpec(memory_space=pltpu.VMEM)] * 2,
         scratch_shapes=_project_scratch(stages, cases),
         compiler_params=pltpu.CompilerParams(collective_id=6 + depth, has_side_effects=True),
-    )(stacked, image)
+    )(*basis, image)
 
 
 def least_squares(columns, beta, depth):
@@ -955,9 +958,8 @@
     product = residual
     beta = None
     for column in range(KRYLOV):
-        stacked = jnp.stack(basis) if basis else residual[None]
         sums, following, direction, product = precondition_sweep(
-            stacked, product, block_inverse, own_picks, chain, gain_panel, ahead_panel,
+            list(basis), product, block_inverse, own_picks, chain, gain_panel, ahead_panel,
             section_block, back_panel, local_picks, jac_diag, mesh_shape, len(basis),
         )
         if column == 0:
@@ -966,7 +968,7 @@
             columns.append(sums[: column + 1])
         basis.append(following)
         directions.append(direction)
-    sums, _ = project(jnp.stack(basis), product, mesh_shape)
+    sums, _ = project(basis, product, mesh_shape)
     columns.append(sums[: KRYLOV + 1])
     weights = least_squares(columns, beta, KRYLOV)
     update = jnp.zeros_like(state_now)

time: 325 us -> 321 us (0.988)
  other arithmetic: 5.76 us -> 2.49 us
    another operation x2 -> x0, other arithmetic: 3.3 us -> none  [the longest x1 1.68 us: local(): sums, _ = project(jnp.stack(basis), product, mesh_shape)]
where the time goes in v14:
time: 321 us
  Pallas kernels  309 us (96%)
  matrix products  4.4 us (1%)
  local copies, waits for them, and re-layouts  4.37 us (1%)
    pallas_call x3, Pallas kernels, precondition_sweep(): pl.pallas_call(functools.partial(_precondition_kernel, n_sec, n_blk, plan...  228 us
    pallas_call x1, Pallas kernels, setup_exchange(): pl.pallas_call(functools.partial(_setup_kernel, n_sec, n_blk, rounds), ou...  47.8 us
    pallas_call x1, Pallas kernels, project(): pl.pallas_call(functools.partial(_project_kernel, stages, depth), out_sha...  33.2 us

profile of v14, /device:TPU:1, one launch (start us, length us, event | category | flops | bytes accessed | tf_op | source)
XLA Modules:
  0.0 320.7 jit_solution(11713812413723313838)
XLA Ops:
  0.0 0.6 copy-done.12
  0.7 0.1 broadcast_compare_fusion
  0.8 0.8 constant_dynamic-slice_fusion.refs_8_.refs_9_.refs_10_
  1.5 0.1 fusion.49
  1.6 0.0 copy-start.2
  1.7 0.7 copy.9.pick_ref.refs_2_.refs_3_.refs_4_
  2.3 0.2 copy-done.2
  2.5 0.7 subtract_multiply_fusion
  3.2 0.9 fusion.5.be_ref
  4.1 0.8 fusion.41.up_ref
  5.0 47.8 %shard_map.82 = (bf16[128,2048]{1,0:T(8,128)(2,1)}, f32[128,128]{1,0:T(8,128)}, f32[16,128]{1,0:T(8,128)}, f32[256,128]{1,0:T(8,128)}, f32[7,128,128]{2,1,0:T(8,128)}) custom-call(bf16[128,256]{1,0:T(8,128)(2,1)} %copy-done.4, f32[128,128]{1,0:T(8,128)} %fusion.41.up_ref, f32[128,128]{1,0:T(8,128)} %fusion.5.be_ref, bf16[256,128]{1,0:T(8,128)(2,1)} %refs_9_.1, ...), custom_call_target="tpu_custom_call" | custom-call | tf_op jit(solution)/shard_map/pallas_call | solution.py:330
  52.8 0.7 copy-done.10
  53.5 0.3 fusion.3
  53.8 0.5 copy-done.1
  54.3 0.0 copy-done.9
  54.4 0.2 fusion.8
  54.6 0.7 copy-done.5
  55.3 2.2 fusion.2.refs_0_
  57.4 69.1 %shard_map.83 = (f32[8,128]{1,0:T(8,128)}, f32[128,256]{1,0:T(8,128)}, f32[128,256]{1,0:T(8,128)}, f32[128,256]{1,0:T(8,128)}) custom-call(f32[128,256]{1,0:T(8,128)} %fusion.2.refs_0_, bf16[256,2048]{1,0:T(8,128)(2,1)} %refs_3_.1, f32[16,256]{1,0:T(8,128)} %copy.9.pick_ref.refs_2_.refs_3_.refs_4_, f32[7,128,128]{2,1,0:T(8,128)} %get-tuple-element.26.refs_3_.refs_4_.refs_5_, ...), custom_call_target="tpu_custom_call" | custom-call | tf_op jit(solution)/shard_map/pallas_call | solution.py:662
  126.6 77.7 %shard_map.84 = (f32[8,128]{1,0:T(8,128)}, f32[128,256]{1,0:T(8,128)}, f32[128,256]{1,0:T(8,128)}, f32[128,256]{1,0:T(8,128)}) custom-call(f32[128,256]{1,0:T(8,128)} %get-tuple-element.28.refs_0_, f32[128,256]{1,0:T(8,128)} %get-tuple-element.29.refs_1_, bf16[256,2048]{1,0:T(8,128)(2,1)} %refs_3_.1, f32[16,256]{1,0:T(8,128)} %copy.9.pick_ref.refs_2_.refs_3_.refs_4_, ...), custom_call_target="tpu_custom_call" | custom-call | tf_op jit(solution)/shard_map/pallas_call | solution.py:662
  204.3 81.5 %shard_map.85 = (f32[8,128]{1,0:T(8,128)}, f32[128,256]{1,0:T(8,128)}, f32[128,256]{1,0:T(8,128)}, f32[128,256]{1,0:T(8,128)}) custom-call(f32[128,256]{1,0:T(8,128)} %get-tuple-element.28.refs_0_, f32[128,256]{1,0:T(8,128)} %get-tuple-element.32.refs_1_, f32[128,256]{1,0:T(8,128)} %get-tuple-element.33.refs_2_, bf16[256,2048]{1,0:T(8,128)(2,1)} %refs_3_.1, ...), custom_call_target="tpu_custom_call" | custom-call | tf_op jit(solution)/shard_map/pallas_call | solution.py:662
  285.8 33.2 %shard_map.86 = (f32[8,128]{1,0:T(8,128)}, f32[128,256]{1,0:T(8,128)}) custom-call(f32[128,256]{1,0:T(8,128)} %get-tuple-element.28.refs_0_, f32[128,256]{1,0:T(8,128)} %get-tuple-element.32.refs_1_, f32[128,256]{1,0:T(8,128)} %get-tuple-element.35.refs_2_, f32[128,256]{1,0:T(8,128)} %get-tuple-element.36.refs_3_), custom_call_target="tpu_custom_call" | custom-call | tf_op jit(solution)/shard_map/pallas_call | solution.py:825
  319.0 0.9 fusion.31
  320.0 0.8 add_add_fusion
  (20 shorter events, 0.0 us)
Async XLA Ops:
  0.0 0.7 copy-start.12
  1.6 0.9 copy-start.2
  1.6 0.9 copy-start.11
  2.5 1.6 copy-start.3
  3.2 0.9 copy-start.4
  3.2 51.3 %copy-start = (bf16[256,2048]{1,0:T(8,128)(2,1)S(1)}, bf16[256,2048]{1,0:T(8,128)(2,1)}, u32[]{:S(2)}) copy-start(bf16[256,2048]{1,0:T(8,128)(2,1)} %refs_8_.3) | copy-start | bytes 3145732
  52.8 0.7 copy-start.10
  53.5 0.8 copy-start.1
  53.5 0.9 copy-start.9
  54.4 0.9 copy-start.5
  285.8 34.2 %copy-start.6 = (f32[128,256]{1,0:T(8,128)S(1)}, f32[128,256]{1,0:T(8,128)}, u32[]{:S(2)}) copy-start(f32[128,256]{1,0:T(8,128)} %get-tuple-element.38) | copy-start | bytes 393220
  285.8 34.2 %copy-start.7 = (f32[128,256]{1,0:T(8,128)S(1)}, f32[128,256]{1,0:T(8,128)}, u32[]{:S(2)}) copy-start(f32[128,256]{1,0:T(8,128)} %get-tuple-element.39) | copy-start | bytes 393220
  285.8 34.2 %copy-start.8 = (f32[128,256]{1,0:T(8,128)S(1)}, f32[128,256]{1,0:T(8,128)}, u32[]{:S(2)}) copy-start(f32[128,256]{1,0:T(8,128)} %get-tuple-element.40) | copy-start | bytes 393220

commit v15 on v14

--- a/solution.py
+++ b/solution.py
@@ -274,18 +274,43 @@
 
 
 def _setup_kernel(
-    n_sec, n_blk, rounds, x_ref, up_ref, be_ref, back_ref, inv_ref, pick_ref,
-    g_ref, b_ref, a_ref, gain_ref, chain_ref, *scratch
+    n_sec, n_blk, rounds, x_ref, ahead_ref, block_ref, spread_ref, back_ref, inv_ref, pick_ref,
+    k_ref, gain_ref, chain_ref, *scratch
 ):
     phase_scratch = scratch[:9]
     pslots, psend, precv, epiece = scratch[9:13]
-    maps_scratch = scratch[13:]
+    g_ref, b_ref, a_ref, upward, own_piece = scratch[13:18]
+    maps_scratch = scratch[18:]
     sec, blk = lax.axis_index("sec"), lax.axis_index("blk")
     offsets = len(rounds[0][1]) + 1
     _greet_all(n_sec, n_blk, offsets, rounds, True)
-    piece = epiece.shape[0]
-    mine = be_ref.at[pl.ds(pl.multiple_of(blk * piece, 8), piece)]
-    _operator_phase(n_sec, n_blk, x_ref, up_ref, mine, g_ref, b_ref, a_ref, phase_scratch)
+    contract = (((1,), (1,)), ((), ()))
+    upward[...] = jnp.dot(x_ref[...], ahead_ref[...], preferred_element_type=jnp.float32).T
+    own_piece[...] = lax.dot_general(
+        pick_ref[...], x_ref[...].astype(jnp.float32), contract,
+        precision=lax.Precision.HIGHEST, preferred_element_type=jnp.float32,
+    )
+    _operator_phase(n_sec, n_blk, x_ref, upward, own_piece, g_ref, b_ref, a_ref, phase_scratch)
+    width = x_ref.shape[1]
+    product = lax.dot_general(
+        g_ref[:, 0:width], block_ref[:, 0:width], contract, preferred_element_type=jnp.float32
+    )
+    for j in range(1, n_blk):
+        product = product + lax.dot_general(
+            g_ref[:, j * width : (j + 1) * width],
+            block_ref[:, j * width : (j + 1) * width],
+            contract,
+            preferred_element_type=jnp.float32,
+        )
+    product = product + lax.dot_general(
+        b_ref[...].T.astype(back_ref.dtype), back_ref[...], contract,
+        preferred_element_type=jnp.float32,
+    )
+    product = product + jnp.dot(
+        spread_ref[...], a_ref[...], precision=lax.Precision.HIGHEST,
+        preferred_element_type=jnp.float32,
+    ).T
+    k_ref[...] = product
 
     def blk_copy(k, target, slot):
         return pltpu.make_async_remote_copy(
@@ -319,9 +344,9 @@
     _maps_body(n_sec, n_blk, rounds, epiece, chain_ref, *maps_scratch)
 
 
-def setup_exchange(x, up_t, be_t, back, inverse, picks, n_sec, n_blk):
+def setup_exchange(x, ahead, block, spread, back, inverse, picks, n_sec, n_blk):
     cases, width = x.shape
-    panel, _ = up_t.shape
+    panel = ahead.shape[1]
     piece = panel // n_blk
     rows, panel_width = back.shape
     rounds = _plan(n_sec)
@@ -330,20 +355,23 @@
     return pl.pallas_call(
         functools.partial(_setup_kernel, n_sec, n_blk, rounds),
         out_shape=(
-            jax.ShapeDtypeStruct((cases, n_blk * width), x.dtype),
-            jax.ShapeDtypeStruct((panel, cases), jnp.float32),
-            jax.ShapeDtypeStruct((piece, cases), jnp.float32),
+            jax.ShapeDtypeStruct((cases, width), jnp.float32),
             jax.ShapeDtypeStruct((rows, panel_width), jnp.float32),
             jax.ShapeDtypeStruct((total, panel_width, panel_width), jnp.float32),
         ),
-        in_specs=[pl.BlockSpec(memory_space=pltpu.VMEM)] * 6,
-        out_specs=[pl.BlockSpec(memory_space=pltpu.VMEM)] * 5,
+        in_specs=[pl.BlockSpec(memory_space=pltpu.VMEM)] * 7,
+        out_specs=[pl.BlockSpec(memory_space=pltpu.VMEM)] * 3,
         scratch_shapes=_operator_scratch(n_blk, cases, width, x.dtype, piece, cases)
         + [
             pltpu.VMEM((n_blk, rows, panel_width), back.dtype),
             pltpu.SemaphoreType.DMA((n_blk,)),
             pltpu.SemaphoreType.DMA((n_blk,)),
             pltpu.VMEM((piece, panel_width), jnp.float32),
+            pltpu.VMEM((cases, n_blk * width), x.dtype),
+            pltpu.VMEM((panel, cases), jnp.float32),
+            pltpu.VMEM((piece, cases), jnp.float32),
+            pltpu.VMEM((panel, cases), jnp.float32),
+            pltpu.VMEM((piece, cases), jnp.float32),
             pltpu.VMEM((offsets * n_blk, piece, panel_width), jnp.float32),
             pltpu.VMEM((offsets, panel_width, panel_width), jnp.float32),
             pltpu.VMEM((panel_width, panel_width), jnp.float32),
@@ -354,7 +382,7 @@
             pltpu.SemaphoreType.DMA((total,)),
         ],
         compiler_params=pltpu.CompilerParams(collective_id=3, has_side_effects=True),
-    )(x, up_t, be_t, back, inverse, picks)
+    )(x, ahead, block, spread, back, inverse, picks)
 
 
 def _gather_kernel(n, x_ref, o_ref, slots, sends, recvs):
@@ -933,24 +961,11 @@
 
     bent = jnp.tanh(state_now)
     state_rounded = state_now.astype(jnp.bfloat16)
-    gathered, behind_t, ahead_piece, gain_panel, chain = setup_exchange(
-        state_rounded,
-        lax.dot_general(
-            ahead_panel, state_rounded, (((0,), (1,)), ((), ())), preferred_element_type=jnp.float32
-        ),
-        lax.dot_general(
-            selector.astype(jnp.bfloat16),
-            state_rounded,
-            (((0,), (1,)), ((), ())),
-            preferred_element_type=jnp.float32,
-        ),
-        back_panel,
-        block_inverse,
-        own_picks,
-        n_sec,
-        n_blk,
-    )
-    residual = source - finish(gathered, behind_t, ahead_piece) - fan_gain[None, :] * bent
+    applied, gain_panel, chain = setup_exchange(
+        state_rounded, ahead_panel, section_block, local_picks, back_panel, block_inverse,
+        own_picks, n_sec, n_blk,
+    )
+    residual = source - applied - fan_gain[None, :] * bent
     jac_diag = fan_gain[None, :] * (1.0 - bent * bent)
     columns = []
     basis = []

time: 321 us -> 319 us (level)
  matrix products: 4.4 us -> 0 us
    dot_general x5 -> x0, matrix products: 4.4 us -> none  [the longest x1 2.18 us: finish(): lax.dot_general(gathered, section_block, contract, preferred_element_type...]
where the time goes in v15:
time: 319 us; the launch traced here: 318 us
  Pallas kernels  310 us (97%)
  other arithmetic  5.62 us (2%)
    pallas_call x3, Pallas kernels, precondition_sweep(): pl.pallas_call(functools.partial(_precondition_kernel, n_sec, n_blk, plan...  228 us
    pallas_call x1, Pallas kernels, setup_exchange(): pl.pallas_call(functools.partial(_setup_kernel, n_sec, n_blk, rounds), ou...  49.3 us
    pallas_call x1, Pallas kernels, project(): pl.pallas_call(functools.partial(_project_kernel, stages, depth), out_sha...  32.8 us

profile of v15, /device:TPU:1, one launch (start us, length us, event | category | flops | bytes accessed | tf_op | source)
XLA Modules:
  0.0 318.3 jit_solution(591232659945144219)
XLA Ops:
  0.0 0.0 copy-start.6
  0.0 0.7 copy-done.6
  0.7 0.1 dynamic-slice
  0.7 1.5 convert_element_type.6.x_ref
  2.3 0.8 fusion
  3.0 0.7 copy.9.pick_ref.refs_2_.refs_3_.refs_4_
  3.7 49.3 %shard_map.82 = (f32[128,256]{1,0:T(8,128)}, f32[256,128]{1,0:T(8,128)}, f32[7,128,128]{2,1,0:T(8,128)}) custom-call(bf16[128,256]{1,0:T(8,128)(2,1)} %convert_element_type.6.x_ref, bf16[256,128]{1,0:T(8,128)(2,1)} %refs_7_.5, bf16[256,2048]{1,0:T(8,128)(2,1)} %refs_8_.3, f32[256,16]{1,0:T(8,128)} %get-tuple-element.43.spread_ref.refs_8_.refs_9_.refs_10_, ...), custom_call_target="tpu_custom_call" | custom-call | tf_op jit(solution)/shard_map/pallas_call | solution.py:355
  53.0 0.0 copy-start.5
  53.0 0.0 copy-done
  53.0 0.0 copy-done.1
  53.1 0.7 copy-done.5
  53.7 1.6 subtract_multiply_fusion
  55.3 69.2 %shard_map.83 = (f32[8,128]{1,0:T(8,128)}, f32[128,256]{1,0:T(8,128)}, f32[128,256]{1,0:T(8,128)}, f32[128,256]{1,0:T(8,128)}) custom-call(f32[128,256]{1,0:T(8,128)} %get-tuple-element.41.refs_0_, bf16[256,2048]{1,0:T(8,128)(2,1)} %refs_3_.1, f32[16,256]{1,0:T(8,128)} %copy.9.pick_ref.refs_2_.refs_3_.refs_4_, ...), custom_call_target="tpu_custom_call" | custom-call | tf_op jit(solution)/shard_map/pallas_call | solution.py:690
  124.6 77.6 %shard_map.84 = (f32[8,128]{1,0:T(8,128)}, f32[128,256]{1,0:T(8,128)}, f32[128,256]{1,0:T(8,128)}, f32[128,256]{1,0:T(8,128)}) custom-call(f32[128,256]{1,0:T(8,128)} %get-tuple-element.24.refs_0_, f32[128,256]{1,0:T(8,128)} %get-tuple-element.25.refs_1_, bf16[256,2048]{1,0:T(8,128)(2,1)} %refs_3_.1, f32[16,256]{1,0:T(8,128)} %copy.9.pick_ref.refs_2_.refs_3_.refs_4_, ...), custom_call_target="tpu_custom_call" | custom-call | tf_op jit(solution)/shard_map/pallas_call | solution.py:690
  202.1 81.6 %shard_map.85 = (f32[8,128]{1,0:T(8,128)}, f32[128,256]{1,0:T(8,128)}, f32[128,256]{1,0:T(8,128)}, f32[128,256]{1,0:T(8,128)}) custom-call(f32[128,256]{1,0:T(8,128)} %get-tuple-element.24.refs_0_, f32[128,256]{1,0:T(8,128)} %get-tuple-element.28.refs_1_, f32[128,256]{1,0:T(8,128)} %get-tuple-element.29.refs_2_, bf16[256,2048]{1,0:T(8,128)(2,1)} %refs_3_.1, ...), custom_call_target="tpu_custom_call" | custom-call | tf_op jit(solution)/shard_map/pallas_call | solution.py:690
  283.7 0.0 copy-start.2
  283.7 0.0 copy-start.3
  283.7 0.0 copy-start.4
  283.8 32.8 %shard_map.86 = (f32[8,128]{1,0:T(8,128)}, f32[128,256]{1,0:T(8,128)}) custom-call(f32[128,256]{1,0:T(8,128)} %get-tuple-element.24.refs_0_, f32[128,256]{1,0:T(8,128)} %get-tuple-element.28.refs_1_, f32[128,256]{1,0:T(8,128)} %get-tuple-element.31.refs_2_, f32[128,256]{1,0:T(8,128)} %get-tuple-element.32.refs_3_), custom_call_target="tpu_custom_call" | custom-call | tf_op jit(solution)/shard_map/pallas_call | solution.py:853
  316.6 0.9 fusion.22
  317.5 0.0 copy-done.2
  317.5 0.0 copy-done.3
  317.5 0.0 copy-done.4
  317.5 0.8 add_add_fusion
  (3 shorter events, 0.0 us)
Async XLA Ops:
  0.0 0.7 copy-start.6
  3.7 49.3 %copy-start = (f32[128,256]{1,0:T(8,128)S(1)}, f32[128,256]{1,0:T(8,128)}, u32[]{:S(2)}) copy-start(f32[128,256]{1,0:T(8,128)} %param.8) | copy-start | bytes 393220
  3.7 49.3 %copy-start.1 = (f32[128,256]{1,0:T(8,128)S(1)}, f32[128,256]{1,0:T(8,128)}, u32[]{:S(2)}) copy-start(f32[128,256]{1,0:T(8,128)} %param.9) | copy-start | bytes 393220
  53.0 0.7 copy-start.5
  283.7 33.8 %copy-start.2 = (f32[128,256]{1,0:T(8,128)S(1)}, f32[128,256]{1,0:T(8,128)}, u32[]{:S(2)}) copy-start(f32[128,256]{1,0:T(8,128)} %get-tuple-element.34) | copy-start | bytes 393220
  283.7 33.8 %copy-start.3 = (f32[128,256]{1,0:T(8,128)S(1)}, f32[128,256]{1,0:T(8,128)}, u32[]{:S(2)}) copy-start(f32[128,256]{1,0:T(8,128)} %get-tuple-element.35) | copy-start | bytes 393220
  283.7 33.8 %copy-start.4 = (f32[128,256]{1,0:T(8,128)S(1)}, f32[128,256]{1,0:T(8,128)}, u32[]{:S(2)}) copy-start(f32[128,256]{1,0:T(8,128)} %get-tuple-element.36) | copy-start | bytes 393220

commit v16 on v15

--- a/solution.py
+++ b/solution.py
@@ -151,7 +151,7 @@
     copy.wait_send()
 
 
-RADIX = 4
+RADIX = 8
 
 
 def _plan(n):

time: 319 us -> 343 us (1.075)
  Pallas kernels: 310 us -> 335 us
    pallas_call x3, Pallas kernels: 228 us -> 244 us  [precondition_sweep(): pl.pallas_call(functools.partial(_precondition_kernel, n_sec, n_blk, plan...]
    pallas_call x1, Pallas kernels: 49.3 us -> 57.7 us  [setup_exchange(): pl.pallas_call(functools.partial(_setup_kernel, n_sec, n_blk, rounds), ou...]
where the time goes in v16:
time: 343 us
  Pallas kernels  335 us (98%)
  other arithmetic  5.62 us (2%)
    pallas_call x3, Pallas kernels, precondition_sweep(): pl.pallas_call(functools.partial(_precondition_kernel, n_sec, n_blk, plan...  244 us
    pallas_call x1, Pallas kernels, setup_exchange(): pl.pallas_call(functools.partial(_setup_kernel, n_sec, n_blk, rounds), ou...  57.7 us
    pallas_call x1, Pallas kernels, project(): pl.pallas_call(functools.partial(_project_kernel, stages, depth), out_sha...  34.1 us

profile of v16, /device:TPU:1, one launch (start us, length us, event | category | flops | bytes accessed | tf_op | source)
XLA Modules:
  0.0 343.2 jit_solution(9523817186707735833)
XLA Ops:
  0.0 0.0 copy-start.6
  0.0 0.7 copy-done.6
  0.7 0.1 dynamic-slice
  0.7 1.5 convert_element_type.6.x_ref
  2.3 0.8 fusion
  3.0 0.7 copy.9.pick_ref.refs_2_.refs_3_.refs_4_
  3.7 57.7 %shard_map.82 = (f32[128,256]{1,0:T(8,128)}, f32[256,128]{1,0:T(8,128)}, f32[10,128,128]{2,1,0:T(8,128)}) custom-call(bf16[128,256]{1,0:T(8,128)(2,1)} %convert_element_type.6.x_ref, bf16[256,128]{1,0:T(8,128)(2,1)} %refs_7_.5, bf16[256,2048]{1,0:T(8,128)(2,1)} %refs_8_.3, f32[256,16]{1,0:T(8,128)} %get-tuple-element.43.spread_ref.refs_8_.refs_9_.refs_10_, ...), custom_call_target="tpu_custom_call" | custom-call | tf_op jit(solution)/shard_map/pallas_call | solution.py:355
  61.4 0.0 copy-start.5
  61.4 0.0 copy-done
  61.4 0.0 copy-done.1
  61.4 0.7 copy-done.5
  62.1 1.7 subtract_multiply_fusion
  63.7 76.3 %shard_map.83 = (f32[8,128]{1,0:T(8,128)}, f32[128,256]{1,0:T(8,128)}, f32[128,256]{1,0:T(8,128)}, f32[128,256]{1,0:T(8,128)}) custom-call(f32[128,256]{1,0:T(8,128)} %get-tuple-element.41.refs_0_, bf16[256,2048]{1,0:T(8,128)(2,1)} %refs_3_.1, f32[16,256]{1,0:T(8,128)} %copy.9.pick_ref.refs_2_.refs_3_.refs_4_, ...), custom_call_target="tpu_custom_call" | custom-call | tf_op jit(solution)/shard_map/pallas_call | solution.py:690
  140.1 83.2 %shard_map.84 = (f32[8,128]{1,0:T(8,128)}, f32[128,256]{1,0:T(8,128)}, f32[128,256]{1,0:T(8,128)}, f32[128,256]{1,0:T(8,128)}) custom-call(f32[128,256]{1,0:T(8,128)} %get-tuple-element.24.refs_0_, f32[128,256]{1,0:T(8,128)} %get-tuple-element.25.refs_1_, bf16[256,2048]{1,0:T(8,128)(2,1)} %refs_3_.1, f32[16,256]{1,0:T(8,128)} %copy.9.pick_ref.refs_2_.refs_3_.refs_4_, ...), custom_call_target="tpu_custom_call" | custom-call | tf_op jit(solution)/shard_map/pallas_call | solution.py:690
  223.3 84.1 %shard_map.85 = (f32[8,128]{1,0:T(8,128)}, f32[128,256]{1,0:T(8,128)}, f32[128,256]{1,0:T(8,128)}, f32[128,256]{1,0:T(8,128)}) custom-call(f32[128,256]{1,0:T(8,128)} %get-tuple-element.24.refs_0_, f32[128,256]{1,0:T(8,128)} %get-tuple-element.28.refs_1_, f32[128,256]{1,0:T(8,128)} %get-tuple-element.29.refs_2_, bf16[256,2048]{1,0:T(8,128)(2,1)} %refs_3_.1, ...), custom_call_target="tpu_custom_call" | custom-call | tf_op jit(solution)/shard_map/pallas_call | solution.py:690
  307.4 0.0 copy-start.2
  307.4 0.0 copy-start.3
  307.4 0.0 copy-start.4
  307.4 34.1 %shard_map.86 = (f32[8,128]{1,0:T(8,128)}, f32[128,256]{1,0:T(8,128)}) custom-call(f32[128,256]{1,0:T(8,128)} %get-tuple-element.24.refs_0_, f32[128,256]{1,0:T(8,128)} %get-tuple-element.28.refs_1_, f32[128,256]{1,0:T(8,128)} %get-tuple-element.31.refs_2_, f32[128,256]{1,0:T(8,128)} %get-tuple-element.32.refs_3_), custom_call_target="tpu_custom_call" | custom-call | tf_op jit(solution)/shard_map/pallas_call | solution.py:853
  341.4 0.9 fusion.22
  342.3 0.0 copy-done.2
  342.4 0.0 copy-done.3
  342.4 0.0 copy-done.4
  342.4 0.8 add_add_fusion
  (3 shorter events, 0.0 us)
Async XLA Ops:
  0.0 0.7 copy-start.6
  3.7 57.7 %copy-start = (f32[128,256]{1,0:T(8,128)S(1)}, f32[128,256]{1,0:T(8,128)}, u32[]{:S(2)}) copy-start(f32[128,256]{1,0:T(8,128)} %param.8) | copy-start | bytes 393220
  3.7 57.7 %copy-start.1 = (f32[128,256]{1,0:T(8,128)S(1)}, f32[128,256]{1,0:T(8,128)}, u32[]{:S(2)}) copy-start(f32[128,256]{1,0:T(8,128)} %param.9) | copy-start | bytes 393220
  61.4 0.7 copy-start.5
  307.4 35.0 %copy-start.2 = (f32[128,256]{1,0:T(8,128)S(1)}, f32[128,256]{1,0:T(8,128)}, u32[]{:S(2)}) copy-start(f32[128,256]{1,0:T(8,128)} %get-tuple-element.34) | copy-start | bytes 393220
  307.4 35.0 %copy-start.3 = (f32[128,256]{1,0:T(8,128)S(1)}, f32[128,256]{1,0:T(8,128)}, u32[]{:S(2)}) copy-start(f32[128,256]{1,0:T(8,128)} %get-tuple-element.35) | copy-start | bytes 393220
  307.4 35.0 %copy-start.4 = (f32[128,256]{1,0:T(8,128)S(1)}, f32[128,256]{1,0:T(8,128)}, u32[]{:S(2)}) copy-start(f32[128,256]{1,0:T(8,128)} %get-tuple-element.36) | copy-start | bytes 393220

commit v17 on v15

--- a/solution.py
+++ b/solution.py
@@ -227,13 +227,20 @@
                 barrier, inc=1, device_id={"blk": lax.rem(blk + k, n_blk)}, device_id_type=MESH
             )
             count += 1
+    covered = bool(stages)
     for o in range(1, offsets + 1):
-        for j in range(n_blk):
+        for k in range(1 if covered else 0, n_blk):
             for peer in (lax.rem(sec + o, n_sec), lax.rem(sec + n_sec - o, n_sec)):
                 pl.semaphore_signal(
-                    barrier, inc=1, device_id={"sec": peer, "blk": j}, device_id_type=MESH
+                    barrier,
+                    inc=1,
+                    device_id={"sec": peer, "blk": lax.rem(blk + k, n_blk)},
+                    device_id_type=MESH,
                 )
                 count += 1
+    if covered:
+        pl.semaphore_wait(barrier, count)
+        return
     for d in sorted({j * d for d, js in rounds[1:] for j in js}):
         for peer in (lax.rem(sec + d, n_sec), lax.rem(sec + n_sec - d, n_sec)):
             pl.semaphore_signal(barrier, inc=1, device_id={"sec": peer}, device_id_type=MESH)
@@ -579,7 +586,7 @@
     sec, blk = lax.axis_index("sec"), lax.axis_index("blk")
     first = rounds[0][1]
     offsets = len(first) + 1
-    _greet_all(n_sec, n_blk, offsets, rounds, True, stages)
+    _greet_all(n_sec, n_blk, offsets, rounds, False, stages)
     _project_body(stages, depth, basis_refs, image_ref, h_ref, next_ref, project_scratch)
     x_ref[...] = next_ref[...].astype(x_ref.dtype)
 

time: 319 us -> 319 us (level)
  no operation moved by 1% of the time
where the time goes in v17:
time: 319 us; the launch traced here: 318 us
  Pallas kernels  311 us (97%)
  other arithmetic  5.62 us (2%)
    pallas_call x3, Pallas kernels, precondition_sweep(): pl.pallas_call(functools.partial(_precondition_kernel, n_sec, n_blk, plan...  229 us
    pallas_call x1, Pallas kernels, setup_exchange(): pl.pallas_call(functools.partial(_setup_kernel, n_sec, n_blk, rounds), ou...  49.3 us
    pallas_call x1, Pallas kernels, project(): pl.pallas_call(functools.partial(_project_kernel, stages, depth), out_sha...  31.8 us

profile of v17, /device:TPU:1, one launch (start us, length us, event | category | flops | bytes accessed | tf_op | source)
XLA Modules:
  0.0 318.4 jit_solution(7830485142356345259)
XLA Ops:
  0.0 0.0 copy-start.6
  0.0 0.7 copy-done.6
  0.7 0.1 dynamic-slice
  0.7 1.5 convert_element_type.6.x_ref
  2.3 0.8 fusion
  3.0 0.7 copy.9.pick_ref.refs_2_.refs_3_.refs_4_
  3.7 49.3 %shard_map.82 = (f32[128,256]{1,0:T(8,128)}, f32[256,128]{1,0:T(8,128)}, f32[7,128,128]{2,1,0:T(8,128)}) custom-call(bf16[128,256]{1,0:T(8,128)(2,1)} %convert_element_type.6.x_ref, bf16[256,128]{1,0:T(8,128)(2,1)} %refs_7_.5, bf16[256,2048]{1,0:T(8,128)(2,1)} %refs_8_.3, f32[256,16]{1,0:T(8,128)} %get-tuple-element.43.spread_ref.refs_8_.refs_9_.refs_10_, ...), custom_call_target="tpu_custom_call" | custom-call | tf_op jit(solution)/shard_map/pallas_call | solution.py:362
  53.0 0.0 copy-start.5
  53.0 0.0 copy-done
  53.0 0.0 copy-done.1
  53.0 0.7 copy-done.5
  53.7 1.6 subtract_multiply_fusion
  55.3 69.2 %shard_map.83 = (f32[8,128]{1,0:T(8,128)}, f32[128,256]{1,0:T(8,128)}, f32[128,256]{1,0:T(8,128)}, f32[128,256]{1,0:T(8,128)}) custom-call(f32[128,256]{1,0:T(8,128)} %get-tuple-element.41.refs_0_, bf16[256,2048]{1,0:T(8,128)(2,1)} %refs_3_.1, f32[16,256]{1,0:T(8,128)} %copy.9.pick_ref.refs_2_.refs_3_.refs_4_, ...), custom_call_target="tpu_custom_call" | custom-call | tf_op jit(solution)/shard_map/pallas_call | solution.py:697
  124.5 77.6 %shard_map.84 = (f32[8,128]{1,0:T(8,128)}, f32[128,256]{1,0:T(8,128)}, f32[128,256]{1,0:T(8,128)}, f32[128,256]{1,0:T(8,128)}) custom-call(f32[128,256]{1,0:T(8,128)} %get-tuple-element.24.refs_0_, f32[128,256]{1,0:T(8,128)} %get-tuple-element.25.refs_1_, bf16[256,2048]{1,0:T(8,128)(2,1)} %refs_3_.1, f32[16,256]{1,0:T(8,128)} %copy.9.pick_ref.refs_2_.refs_3_.refs_4_, ...), custom_call_target="tpu_custom_call" | custom-call | tf_op jit(solution)/shard_map/pallas_call | solution.py:697
  202.1 82.6 %shard_map.85 = (f32[8,128]{1,0:T(8,128)}, f32[128,256]{1,0:T(8,128)}, f32[128,256]{1,0:T(8,128)}, f32[128,256]{1,0:T(8,128)}) custom-call(f32[128,256]{1,0:T(8,128)} %get-tuple-element.24.refs_0_, f32[128,256]{1,0:T(8,128)} %get-tuple-element.28.refs_1_, f32[128,256]{1,0:T(8,128)} %get-tuple-element.29.refs_2_, bf16[256,2048]{1,0:T(8,128)(2,1)} %refs_3_.1, ...), custom_call_target="tpu_custom_call" | custom-call | tf_op jit(solution)/shard_map/pallas_call | solution.py:697
  284.8 0.0 copy-start.2
  284.8 0.0 copy-start.3
  284.8 0.0 copy-start.4
  284.8 31.8 %shard_map.86 = (f32[8,128]{1,0:T(8,128)}, f32[128,256]{1,0:T(8,128)}) custom-call(f32[128,256]{1,0:T(8,128)} %get-tuple-element.24.refs_0_, f32[128,256]{1,0:T(8,128)} %get-tuple-element.28.refs_1_, f32[128,256]{1,0:T(8,128)} %get-tuple-element.31.refs_2_, f32[128,256]{1,0:T(8,128)} %get-tuple-element.32.refs_3_), custom_call_target="tpu_custom_call" | custom-call | tf_op jit(solution)/shard_map/pallas_call | solution.py:860
  316.6 0.9 fusion.22
  317.6 0.0 copy-done.2
  317.6 0.0 copy-done.3
  317.6 0.0 copy-done.4
  317.6 0.8 add_add_fusion
  (3 shorter events, 0.0 us)
Async XLA Ops:
  0.0 0.7 copy-start.6
  3.7 49.3 %copy-start = (f32[128,256]{1,0:T(8,128)S(1)}, f32[128,256]{1,0:T(8,128)}, u32[]{:S(2)}) copy-start(f32[128,256]{1,0:T(8,128)} %param.8) | copy-start | bytes 393220
  3.7 49.3 %copy-start.1 = (f32[128,256]{1,0:T(8,128)S(1)}, f32[128,256]{1,0:T(8,128)}, u32[]{:S(2)}) copy-start(f32[128,256]{1,0:T(8,128)} %param.9) | copy-start | bytes 393220
  53.0 0.7 copy-start.5
  284.8 32.8 %copy-start.2 = (f32[128,256]{1,0:T(8,128)S(1)}, f32[128,256]{1,0:T(8,128)}, u32[]{:S(2)}) copy-start(f32[128,256]{1,0:T(8,128)} %get-tuple-element.34) | copy-start | bytes 393220
  284.8 32.8 %copy-start.3 = (f32[128,256]{1,0:T(8,128)S(1)}, f32[128,256]{1,0:T(8,128)}, u32[]{:S(2)}) copy-start(f32[128,256]{1,0:T(8,128)} %get-tuple-element.35) | copy-start | bytes 393220
  284.8 32.8 %copy-start.4 = (f32[128,256]{1,0:T(8,128)S(1)}, f32[128,256]{1,0:T(8,128)}, u32[]{:S(2)}) copy-start(f32[128,256]{1,0:T(8,128)} %get-tuple-element.36) | copy-start | bytes 393220

commit v18 on v17

--- a/solution.py
+++ b/solution.py
@@ -297,27 +297,6 @@
         pick_ref[...], x_ref[...].astype(jnp.float32), contract,
         precision=lax.Precision.HIGHEST, preferred_element_type=jnp.float32,
     )
-    _operator_phase(n_sec, n_blk, x_ref, upward, own_piece, g_ref, b_ref, a_ref, phase_scratch)
-    width = x_ref.shape[1]
-    product = lax.dot_general(
-        g_ref[:, 0:width], block_ref[:, 0:width], contract, preferred_element_type=jnp.float32
-    )
-    for j in range(1, n_blk):
-        product = product + lax.dot_general(
-            g_ref[:, j * width : (j + 1) * width],
-            block_ref[:, j * width : (j + 1) * width],
-            contract,
-            preferred_element_type=jnp.float32,
-        )
-    product = product + lax.dot_general(
-        b_ref[...].T.astype(back_ref.dtype), back_ref[...], contract,
-        preferred_element_type=jnp.float32,
-    )
-    product = product + jnp.dot(
-        spread_ref[...], a_ref[...], precision=lax.Precision.HIGHEST,
-        preferred_element_type=jnp.float32,
-    ).T
-    k_ref[...] = product
 
     def blk_copy(k, target, slot):
         return pltpu.make_async_remote_copy(
@@ -332,6 +311,27 @@
     outgoing = [blk_copy(k, lax.rem(blk + k, n_blk), blk) for k in range(1, n_blk)]
     for copy in outgoing:
         copy.start()
+    _operator_phase(n_sec, n_blk, x_ref, upward, own_piece, g_ref, b_ref, a_ref, phase_scratch)
+    width = x_ref.shape[1]
+    product = lax.dot_general(
+        g_ref[:, 0:width], block_ref[:, 0:width], contract, preferred_element_type=jnp.float32
+    )
+    for j in range(1, n_blk):
+        product = product + lax.dot_general(
+            g_ref[:, j * width : (j + 1) * width],
+            block_ref[:, j * width : (j + 1) * width],
+            contract,
+            preferred_element_type=jnp.float32,
+        )
+    product = product + lax.dot_general(
+        b_ref[...].T.astype(back_ref.dtype), back_ref[...], contract,
+        preferred_element_type=jnp.float32,
+    )
+    product = product + jnp.dot(
+        spread_ref[...], a_ref[...], precision=lax.Precision.HIGHEST,
+        preferred_element_type=jnp.float32,
+    ).T
+    k_ref[...] = product
     pslots[blk] = back_ref[...]
     for k in range(1, n_blk):
         sender = lax.rem(blk + k, n_blk)

time: 319 us -> 316 us (level)
  no operation moved by 1% of the time
where the time goes in v18:
time: 316 us
  Pallas kernels  308 us (97%)
  other arithmetic  5.62 us (2%)
    pallas_call x3, Pallas kernels, precondition_sweep(): pl.pallas_call(functools.partial(_precondition_kernel, n_sec, n_blk, plan...  229 us
    pallas_call x1, Pallas kernels, setup_exchange(): pl.pallas_call(functools.partial(_setup_kernel, n_sec, n_blk, rounds), ou...  47.3 us
    pallas_call x1, Pallas kernels, project(): pl.pallas_call(functools.partial(_project_kernel, stages, depth), out_sha...  31.9 us

profile of v18, /device:TPU:1, one launch (start us, length us, event | category | flops | bytes accessed | tf_op | source)
XLA Modules:
  0.0 316.1 jit_solution(18190764217090061819)
XLA Ops:
  0.0 0.0 copy-start.6
  0.0 0.7 copy-done.6
  0.7 0.1 dynamic-slice
  0.7 1.5 convert_element_type.6.x_ref
  2.3 0.8 fusion
  3.0 0.7 copy.9.pick_ref.refs_2_.refs_3_.refs_4_
  3.7 47.3 %shard_map.82 = (f32[128,256]{1,0:T(8,128)}, f32[256,128]{1,0:T(8,128)}, f32[7,128,128]{2,1,0:T(8,128)}) custom-call(bf16[128,256]{1,0:T(8,128)(2,1)} %convert_element_type.6.x_ref, bf16[256,128]{1,0:T(8,128)(2,1)} %refs_7_.5, bf16[256,2048]{1,0:T(8,128)(2,1)} %refs_8_.3, f32[256,16]{1,0:T(8,128)} %get-tuple-element.43.spread_ref.refs_8_.refs_9_.refs_10_, ...), custom_call_target="tpu_custom_call" | custom-call | tf_op jit(solution)/shard_map/pallas_call | solution.py:362
  51.0 0.0 copy-start.5
  51.0 0.0 copy-done
  51.1 0.0 copy-done.1
  51.1 0.7 copy-done.5
  51.7 1.6 subtract_multiply_fusion
  53.4 70.4 %shard_map.83 = (f32[8,128]{1,0:T(8,128)}, f32[128,256]{1,0:T(8,128)}, f32[128,256]{1,0:T(8,128)}, f32[128,256]{1,0:T(8,128)}) custom-call(f32[128,256]{1,0:T(8,128)} %get-tuple-element.41.refs_0_, bf16[256,2048]{1,0:T(8,128)(2,1)} %refs_3_.1, f32[16,256]{1,0:T(8,128)} %copy.9.pick_ref.refs_2_.refs_3_.refs_4_, ...), custom_call_target="tpu_custom_call" | custom-call | tf_op jit(solution)/shard_map/pallas_call | solution.py:697
  123.8 76.7 %shard_map.84 = (f32[8,128]{1,0:T(8,128)}, f32[128,256]{1,0:T(8,128)}, f32[128,256]{1,0:T(8,128)}, f32[128,256]{1,0:T(8,128)}) custom-call(f32[128,256]{1,0:T(8,128)} %get-tuple-element.24.refs_0_, f32[128,256]{1,0:T(8,128)} %get-tuple-element.25.refs_1_, bf16[256,2048]{1,0:T(8,128)(2,1)} %refs_3_.1, f32[16,256]{1,0:T(8,128)} %copy.9.pick_ref.refs_2_.refs_3_.refs_4_, ...), custom_call_target="tpu_custom_call" | custom-call | tf_op jit(solution)/shard_map/pallas_call | solution.py:697
  200.5 82.0 %shard_map.85 = (f32[8,128]{1,0:T(8,128)}, f32[128,256]{1,0:T(8,128)}, f32[128,256]{1,0:T(8,128)}, f32[128,256]{1,0:T(8,128)}) custom-call(f32[128,256]{1,0:T(8,128)} %get-tuple-element.24.refs_0_, f32[128,256]{1,0:T(8,128)} %get-tuple-element.28.refs_1_, f32[128,256]{1,0:T(8,128)} %get-tuple-element.29.refs_2_, bf16[256,2048]{1,0:T(8,128)(2,1)} %refs_3_.1, ...), custom_call_target="tpu_custom_call" | custom-call | tf_op jit(solution)/shard_map/pallas_call | solution.py:697
  282.4 0.0 copy-start.2
  282.5 0.0 copy-start.3
  282.5 0.0 copy-start.4
  282.5 31.9 %shard_map.86 = (f32[8,128]{1,0:T(8,128)}, f32[128,256]{1,0:T(8,128)}) custom-call(f32[128,256]{1,0:T(8,128)} %get-tuple-element.24.refs_0_, f32[128,256]{1,0:T(8,128)} %get-tuple-element.28.refs_1_, f32[128,256]{1,0:T(8,128)} %get-tuple-element.31.refs_2_, f32[128,256]{1,0:T(8,128)} %get-tuple-element.32.refs_3_), custom_call_target="tpu_custom_call" | custom-call | tf_op jit(solution)/shard_map/pallas_call | solution.py:860
  314.4 0.9 fusion.22
  315.3 0.0 copy-done.2
  315.3 0.0 copy-done.3
  315.3 0.0 copy-done.4
  315.3 0.8 add_add_fusion
  (3 shorter events, 0.0 us)
Async XLA Ops:
  0.0 0.7 copy-start.6
  3.7 47.3 %copy-start = (f32[128,256]{1,0:T(8,128)S(1)}, f32[128,256]{1,0:T(8,128)}, u32[]{:S(2)}) copy-start(f32[128,256]{1,0:T(8,128)} %param.8) | copy-start | bytes 393220
  3.7 47.4 %copy-start.1 = (f32[128,256]{1,0:T(8,128)S(1)}, f32[128,256]{1,0:T(8,128)}, u32[]{:S(2)}) copy-start(f32[128,256]{1,0:T(8,128)} %param.9) | copy-start | bytes 393220
  51.0 0.7 copy-start.5
  282.4 32.9 %copy-start.2 = (f32[128,256]{1,0:T(8,128)S(1)}, f32[128,256]{1,0:T(8,128)}, u32[]{:S(2)}) copy-start(f32[128,256]{1,0:T(8,128)} %get-tuple-element.34) | copy-start | bytes 393220
  282.5 32.9 %copy-start.3 = (f32[128,256]{1,0:T(8,128)S(1)}, f32[128,256]{1,0:T(8,128)}, u32[]{:S(2)}) copy-start(f32[128,256]{1,0:T(8,128)} %get-tuple-element.35) | copy-start | bytes 393220
  282.5 32.9 %copy-start.4 = (f32[128,256]{1,0:T(8,128)S(1)}, f32[128,256]{1,0:T(8,128)}, u32[]{:S(2)}) copy-start(f32[128,256]{1,0:T(8,128)} %get-tuple-element.36) | copy-start | bytes 393220

commit v19 on v18

--- a/solution.py
+++ b/solution.py
@@ -603,24 +603,25 @@
     outgoing = [blk_copy(k, lax.rem(blk + k, n_blk), blk) for k in range(1, n_blk)]
     for copy in outgoing:
         copy.start()
-    gslots[blk] = x_ref[...]
+    width = x_ref.shape[1]
+    contract = (((1,), (1,)), ((), ()))
+    folded = lax.dot_general(
+        x_ref[...],
+        inv_ref[:, pl.ds(pl.multiple_of(blk * width, width), width)],
+        contract,
+        preferred_element_type=jnp.float32,
+    )
     for k in range(1, n_blk):
         sender = lax.rem(blk + k, n_blk)
         blk_copy(k, sender, sender).wait_recv()
+        folded = folded + lax.dot_general(
+            gslots[sender],
+            inv_ref[:, pl.ds(pl.multiple_of(sender * width, width), width)],
+            contract,
+            preferred_element_type=jnp.float32,
+        )
     for copy in outgoing:
         copy.wait_send()
-    width = x_ref.shape[1]
-    contract = (((1,), (1,)), ((), ()))
-    folded = lax.dot_general(
-        gslots[0], inv_ref[:, 0:width], contract, preferred_element_type=jnp.float32
-    )
-    for j in range(1, n_blk):
-        folded = folded + lax.dot_general(
-            gslots[j],
-            inv_ref[:, j * width : (j + 1) * width],
-            contract,
-            preferred_element_type=jnp.float32,
-        )
     fpiece[...] = lax.dot_general(
         pick_ref[...], folded, contract, precision=lax.Precision.HIGHEST,
         preferred_element_type=jnp.float32,

time: 316 us -> 316 us (level)
  no operation moved by 1% of the time
where the time goes in v19:
time: 316 us
  Pallas kernels  308 us (97%)
  other arithmetic  5.62 us (2%)
    pallas_call x3, Pallas kernels, precondition_sweep(): pl.pallas_call(functools.partial(_precondition_kernel, n_sec, n_blk, plan...  228 us
    pallas_call x1, Pallas kernels, setup_exchange(): pl.pallas_call(functools.partial(_setup_kernel, n_sec, n_blk, rounds), ou...  47.3 us
    pallas_call x1, Pallas kernels, project(): pl.pallas_call(functools.partial(_project_kernel, stages, depth), out_sha...  32.3 us

profile of v19, /device:TPU:1, one launch (start us, length us, event | category | flops | bytes accessed | tf_op | source)
XLA Modules:
  0.0 315.6 jit_solution(15163967161260358255)
XLA Ops:
  0.0 0.0 copy-start.6
  0.0 0.7 copy-done.6
  0.7 0.1 dynamic-slice
  0.7 1.5 convert_element_type.6.x_ref
  2.3 0.8 fusion
  3.0 0.7 copy.9.pick_ref.refs_2_.refs_3_.refs_4_
  3.7 47.3 %shard_map.82 = (f32[128,256]{1,0:T(8,128)}, f32[256,128]{1,0:T(8,128)}, f32[7,128,128]{2,1,0:T(8,128)}) custom-call(bf16[128,256]{1,0:T(8,128)(2,1)} %convert_element_type.6.x_ref, bf16[256,128]{1,0:T(8,128)(2,1)} %refs_7_.5, bf16[256,2048]{1,0:T(8,128)(2,1)} %refs_8_.3, f32[256,16]{1,0:T(8,128)} %get-tuple-element.43.spread_ref.refs_8_.refs_9_.refs_10_, ...), custom_call_target="tpu_custom_call" | custom-call | tf_op jit(solution)/shard_map/pallas_call | solution.py:362
  51.0 0.0 copy-start.5
  51.0 0.0 copy-done
  51.1 0.0 copy-done.1
  51.1 0.7 copy-done.5
  51.7 1.6 subtract_multiply_fusion
  53.4 70.5 %shard_map.83 = (f32[8,128]{1,0:T(8,128)}, f32[128,256]{1,0:T(8,128)}, f32[128,256]{1,0:T(8,128)}, f32[128,256]{1,0:T(8,128)}) custom-call(f32[128,256]{1,0:T(8,128)} %get-tuple-element.41.refs_0_, bf16[256,2048]{1,0:T(8,128)(2,1)} %refs_3_.1, f32[16,256]{1,0:T(8,128)} %copy.9.pick_ref.refs_2_.refs_3_.refs_4_, ...), custom_call_target="tpu_custom_call" | custom-call | tf_op jit(solution)/shard_map/pallas_call | solution.py:698
  123.8 76.8 %shard_map.84 = (f32[8,128]{1,0:T(8,128)}, f32[128,256]{1,0:T(8,128)}, f32[128,256]{1,0:T(8,128)}, f32[128,256]{1,0:T(8,128)}) custom-call(f32[128,256]{1,0:T(8,128)} %get-tuple-element.24.refs_0_, f32[128,256]{1,0:T(8,128)} %get-tuple-element.25.refs_1_, bf16[256,2048]{1,0:T(8,128)(2,1)} %refs_3_.1, f32[16,256]{1,0:T(8,128)} %copy.9.pick_ref.refs_2_.refs_3_.refs_4_, ...), custom_call_target="tpu_custom_call" | custom-call | tf_op jit(solution)/shard_map/pallas_call | solution.py:698
  200.7 80.8 %shard_map.85 = (f32[8,128]{1,0:T(8,128)}, f32[128,256]{1,0:T(8,128)}, f32[128,256]{1,0:T(8,128)}, f32[128,256]{1,0:T(8,128)}) custom-call(f32[128,256]{1,0:T(8,128)} %get-tuple-element.24.refs_0_, f32[128,256]{1,0:T(8,128)} %get-tuple-element.28.refs_1_, f32[128,256]{1,0:T(8,128)} %get-tuple-element.29.refs_2_, bf16[256,2048]{1,0:T(8,128)(2,1)} %refs_3_.1, ...), custom_call_target="tpu_custom_call" | custom-call | tf_op jit(solution)/shard_map/pallas_call | solution.py:698
  281.5 0.0 copy-start.2
  281.5 0.0 copy-start.3
  281.5 0.0 copy-start.4
  281.5 32.3 %shard_map.86 = (f32[8,128]{1,0:T(8,128)}, f32[128,256]{1,0:T(8,128)}) custom-call(f32[128,256]{1,0:T(8,128)} %get-tuple-element.24.refs_0_, f32[128,256]{1,0:T(8,128)} %get-tuple-element.28.refs_1_, f32[128,256]{1,0:T(8,128)} %get-tuple-element.31.refs_2_, f32[128,256]{1,0:T(8,128)} %get-tuple-element.32.refs_3_), custom_call_target="tpu_custom_call" | custom-call | tf_op jit(solution)/shard_map/pallas_call | solution.py:861
  313.9 0.9 fusion.22
  314.8 0.0 copy-done.2
  314.8 0.0 copy-done.3
  314.8 0.0 copy-done.4
  314.8 0.8 add_add_fusion
  (3 shorter events, 0.0 us)
Async XLA Ops:
  0.0 0.7 copy-start.6
  3.7 47.3 %copy-start = (f32[128,256]{1,0:T(8,128)S(1)}, f32[128,256]{1,0:T(8,128)}, u32[]{:S(2)}) copy-start(f32[128,256]{1,0:T(8,128)} %param.8) | copy-start | bytes 393220
  3.7 47.4 %copy-start.1 = (f32[128,256]{1,0:T(8,128)S(1)}, f32[128,256]{1,0:T(8,128)}, u32[]{:S(2)}) copy-start(f32[128,256]{1,0:T(8,128)} %param.9) | copy-start | bytes 393220
  51.0 0.7 copy-start.5
  281.5 33.3 %copy-start.2 = (f32[128,256]{1,0:T(8,128)S(1)}, f32[128,256]{1,0:T(8,128)}, u32[]{:S(2)}) copy-start(f32[128,256]{1,0:T(8,128)} %get-tuple-element.34) | copy-start | bytes 393220
  281.5 33.3 %copy-start.3 = (f32[128,256]{1,0:T(8,128)S(1)}, f32[128,256]{1,0:T(8,128)}, u32[]{:S(2)}) copy-start(f32[128,256]{1,0:T(8,128)} %get-tuple-element.35) | copy-start | bytes 393220
  281.5 33.3 %copy-start.4 = (f32[128,256]{1,0:T(8,128)S(1)}, f32[128,256]{1,0:T(8,128)}, u32[]{:S(2)}) copy-start(f32[128,256]{1,0:T(8,128)} %get-tuple-element.36) | copy-start | bytes 393220
